TPU v7x, 32 devices: a whole 2x2x4 slice. The times are simulated.
32 devices in a mesh: strip: 8 (over z, x), sect: 4 (over y, core).
Axes of the slice: x: 2, y: 2, z: 4, core: 2. Of those that a mesh axis runs over, the one named last changes fastest.
Arguments:
- currents: float32 [32768], P(('strip', 'sect')), may hold values from -6 to 6
- plane_weights: float32 [8, 32768], P(None, ('strip', 'sect')), may hold values from 0 to 1
- cell_weights: float32 [32768, 128], P(('strip', 'sect')), may hold values from 0 to 1
- brick_dest: int32 [8192, 1], P(('strip', 'sect')), may hold values from 0 to 3; in each aligned block of 256 rows (0 to 255, 256 to 511, ...) at most 96 rows name the same one
- brick_tile: int32 [8192], P(('strip', 'sect')), may hold values from 0 to 383
- brick_count: int32 [32], P(('strip', 'sect')), may hold values from 64 to 256, as said below
- kern_across: float32 [5, 2, 17], replicated, may hold values from -1.5 to 1.5
- kern_along: float32 [5, 2, 17], replicated, may hold values from -1.5 to 1.5
- plane_mix: float32 [5, 2, 8, 8], replicated, may hold values from -1.5 to 1.5
Outputs:
- grid_potential: float32 [8, 384, 4096], P(None, None, ('strip', 'sect'))
- segment_potential: float32 [32768], P(('strip', 'sect'))
Inputs may be any that keep to these rules, and one draw needn't show every extreme that they name: `brick_dest`: among the 256 bricks of one section at most 96 name the same owner section. `brick_tile`: tile t covers cells across track (t // 8) * 8 onward and along track (t % 8) * 16 onward within the owner's block; several bricks may share a tile. A section's live bricks are its first brick_count ones; the others carry no current and see zero potential.
All inputs are finite; a program needn't handle non-finite values.
Results may differ from a plain program's by a relative error of at most 0.00015.
Values sent between devices are 32-bit elements; how exact they have to be, the bound alone decides.
No kernel may reach another device: no remote copies, remote signals or barrier semaphores. Data moves between devices by JAX's collectives and lax.ppermute only.
A program may use at most 192 MiB of HBM per device.

v0:
```python
import jax
import jax.numpy as jnp
from jax import lax
from jax.sharding import PartitionSpec as P

NY = 384
CX = 128
LEVELS = 4
BX = 16
BY = 8
TILES = 384


precise = lax.Precision.HIGHEST


def padded_2(value, sides, width):
    for axis, dim in sides:
        peers, length = (lax.axis_size(axis), value.shape[dim])
        up = [(i, (i + 1) % peers) for i in range(peers - 1)]
        down = [(j, i) for i, j in up]
        last = lax.slice_in_dim(value, length - width, length, axis=dim)
        initial = lax.slice_in_dim(value, 0, width, axis=dim)
        before = lax.ppermute(last, axis, up)
        after = lax.ppermute(initial, axis, down)
        value = jnp.concatenate([before, value, after], axis=dim)
    return value


def across_ranks(charge_field, kernel):
    reach = kernel.shape[-1] // 2
    extent = charge_field.shape[1]
    padded = jnp.pad(charge_field, ((0, 0), (reach, reach), (0, 0)))
    summed = jnp.zeros((kernel.shape[0],) + charge_field.shape, jnp.float32)
    for offset in range(kernel.shape[-1]):
        summed = (
            summed
            + kernel[:, offset][:, None, None, None] * padded[None, :, offset : offset + extent, :]
        )
    return summed


def along_from_padded(padded, kernel, extent):
    summed = jnp.zeros(padded.shape[:3] + (extent,), jnp.float32)
    for offset in range(kernel.shape[-1]):
        summed = (
            summed
            + kernel[:, offset][:, None, None, None] * padded[:, :, :, offset : offset + extent]
        )
    return summed


def level_term(charge_field, kern_y, kern_x, mixing):
    reach = kern_x.shape[-1] // 2
    extent = charge_field.shape[2]
    field = across_ranks(charge_field, kern_y)
    padded = padded_2(field, ((("strip", "sect"), 3),), reach)
    ranked = along_from_padded(padded, kern_x, extent)
    return jnp.einsum("rzw,rwyx->zyx", mixing, ranked, precision=precise)


def restrict(charge_field):
    planes, rows, columns = charge_field.shape
    return 0.5 * charge_field.reshape(planes, rows // 2, 2, columns // 2, 2).sum(axis=(2, 4))


def prolong(coarse):
    return 0.5 * jnp.repeat(jnp.repeat(coarse, 2, axis=1), 2, axis=2)


def body(
    currents,
    plane_weights,
    cell_weights,
    brick_dest,
    brick_tile,
    brick_count,
    kern_across,
    kern_along,
    plane_mix,
):
    sections = lax.axis_size("sect")
    bricks = brick_tile.shape[0]
    slot_count = currents.shape[0] // bricks
    planes = plane_weights.shape[0]
    cell_count = cell_weights.shape[1]
    capacity = 3 * bricks // (2 * sections)
    buffer_rows = sections * capacity
    alive_mask = (jnp.arange(bricks, dtype=jnp.int32) < brick_count[0]).astype(jnp.float32)
    target = brick_dest[:, 0]
    onehot = (target[:, None] == jnp.arange(sections, dtype=jnp.int32)[None, :]).astype(jnp.int32)
    queue_rank = jnp.sum((jnp.cumsum(onehot, axis=0) - onehot) * onehot, axis=1)
    slot_index = target * capacity + queue_rank
    charge = (
        plane_weights.reshape(planes, bricks, slot_count).transpose(1, 2, 0)
        * (currents.reshape(bricks, slot_count) * alive_mask[:, None])[:, :, None]
    )
    cell_out = (
        jnp.zeros((buffer_rows, slot_count * cell_count), jnp.float32)
        .at[slot_index]
        .set(cell_weights.reshape(bricks, slot_count * cell_count))
    )
    charge_out = (
        jnp.zeros((buffer_rows, slot_count * planes), jnp.float32)
        .at[slot_index]
        .set(charge.reshape(bricks, slot_count * planes))
    )
    tile_out = (
        jnp.zeros((buffer_rows, 1), jnp.float32)
        .at[slot_index]
        .set(brick_tile.astype(jnp.float32)[:, None])
    )
    cell_in, charge_in, tile_in = (
        lax.all_to_all(cell_out, "sect", split_axis=0, concat_axis=0, tiled=True),
        lax.all_to_all(charge_out, "sect", split_axis=0, concat_axis=0, tiled=True),
        lax.all_to_all(tile_out, "sect", split_axis=0, concat_axis=0, tiled=True),
    )
    cell_in = cell_in.reshape(buffer_rows, slot_count, cell_count)
    charge_in = charge_in.reshape(buffer_rows, slot_count, planes)
    tile_ids = tile_in[:, 0].astype(jnp.int32)
    bricks_in = jnp.einsum("ksz,ksc->kzc", charge_in, cell_in, precision=precise)
    tile_grid = jnp.zeros((TILES, planes, cell_count), jnp.float32).at[tile_ids].add(bricks_in)
    charge_grid = (
        tile_grid.reshape(NY // BY, CX // BX, planes, BY, BX)
        .transpose(2, 0, 3, 1, 4)
        .reshape(planes, NY, CX)
    )
    charges = [charge_grid]
    for level_index in range(LEVELS):
        charges.append(restrict(charges[-1]))
    potential = level_term(
        charges[LEVELS], kern_across[LEVELS], kern_along[LEVELS], plane_mix[LEVELS]
    )
    for level_index in range(LEVELS - 1, -1, -1):
        potential = level_term(
            charges[level_index],
            kern_across[level_index],
            kern_along[level_index],
            plane_mix[level_index],
        ) + prolong(potential)
    pot_tiles = (
        potential.reshape(planes, NY // BY, BY, CX // BX, BX)
        .transpose(1, 3, 0, 2, 4)
        .reshape(TILES, planes, cell_count)
    )
    sampled = jnp.einsum("kzc,ksc->ksz", pot_tiles[tile_ids], cell_in, precision=precise).reshape(
        buffer_rows, slot_count * planes
    )
    returned = lax.all_to_all(sampled, "sect", split_axis=0, concat_axis=0, tiled=True)
    own_rows = returned[slot_index].reshape(bricks, slot_count, planes)
    weights_back = plane_weights.reshape(planes, bricks, slot_count)
    segment_potential = (
        jnp.einsum("bsz,zbs->bs", own_rows, weights_back, precision=precise) * alive_mask[:, None]
    )
    return (potential, segment_potential.reshape(bricks * slot_count))


def solution(mesh):
    placed = (
        P(("strip", "sect")),
        P(None, ("strip", "sect")),
        P(("strip", "sect"), None),
        P(("strip", "sect"), None),
        P(("strip", "sect")),
        P(("strip", "sect")),
        P(),
        P(),
        P(),
    )
    return jax.shard_map(
        body,
        mesh=mesh,
        in_specs=placed,
        out_specs=(P(None, None, ("strip", "sect")), P(("strip", "sect"))),
        check_vma=False,
    )
```

profile of v0, /device:TPU:24, one launch (start us, length us, event | category | flops | bytes accessed | tf_op | source)
XLA Modules:
  0.0 396.6 jit_solution(15897147594704825424)
XLA Ops:
  7.1 3.2 all-to-all-start
  23.0 3.3 all-to-all-start.1
  30.3 3.5 all-to-all-start.2
  38.4 7.1 %all-to-all-done.2 = f32[4,96,512]{2,1,0:T(8,128)S(1)} async-done(((f32[4,96,512]{2,1,0:T(8,128)}), f32[4,96,512]{2,1,0:T(8,128)S(1)}, u32[]{:S(2)}, u32[]{:S(2)}) %all-to-all-start.2) | async-done | bytes 786464 | tf_op jit(solution)/shard_map/all_to_all | solution.py:114
  46.6 4.4 %fusion.406 = f32[384,8,128]{2,1,0:T(8,128)S(1)} fusion(f32[384,4,8]{2,1,0:T(4,128)} %reshape.491, f32[384,4,128]{2,1,0:T(4,128)S(1)} %reshape.419), kind=kOutput, calls=%fused_computation.780 | convolution fusion | flops 18874368 | bytes 2408448 | tf_op jit(solution)/shard_map/ksz,ksc->kzc/dot_general | solution.py:121
  51.1 14.9 %scatter_fusion = f32[384,8,128]{2,1,0:T(8,128)S(1)} fusion(f32[384,8,128]{2,1,0:T(8,128)S(1)} %broadcast_in_dim.26, s32[384]{0:T(512)S(1)} %fusion.395, f32[384,8,128]{2,1,0:T(8,128)S(1)} %fusion.406), kind=kCustom, calls=%fused_computation.5 | custom fusion | flops 393216 | bytes 4720128 | tf_op jit(solution)/shard_map/scatter-add | solution.py:122
  66.0 6.6 %reshape.420 = f32[48,8,8,8,16]{4,3,2,1,0:T(8,128)} reshape(f32[384,8,128]{2,1,0:T(8,128)S(1)} %scatter_fusion) | data formatting | bytes 3145728 | tf_op jit(solution)/shard_map/reshape | solution.py:124
  72.6 16.4 %copy.108 = f32[8,48,8,8,16]{4,3,2,1,0:T(8,128)} copy(f32[8,48,8,8,16]{4,2,0,3,1:T(8,128)} %bitcast.145) | data formatting | bytes 3145728 | tf_op jit(solution)/shard_map/transpose | solution.py:125
  89.1 17.8 %copy.127 = f32[8,48,8,8,16]{0,4,3,2,1:T(8,128)} copy(f32[8,48,8,8,16]{4,2,0,3,1:T(8,128)} %bitcast.146) | data formatting | bytes 3145728 | tf_op jit(solution)/shard_map/transpose | solution.py:125
  106.8 25.8 %reduce_sum.49 = f32[8,192,64]{0,2,1:T(8,128)} reduce(f32[8,192,2,64,2]{0,4,3,2,1:T(2,128)} %bitcast.147, f32[]{:T(128)} %constant.5.clone.1), dimensions={2,4}, to_apply=%region_7.8 | reduce | flops 294912 | bytes 1966084 | tf_op jit(solution)/shard_map/reduce_sum | solution.py:64
  132.7 4.9 %copy.128 = f32[8,192,64]{1,0,2:T(8,128)S(1)} copy(f32[8,192,64]{0,2,1:T(8,128)} %reduce_sum.49) | data formatting | bytes 786432 | tf_op jit(solution)/shard_map/reduce_sum | solution.py:64
  137.6 15.6 %copy.129 = f32[8,192,64]{0,2,1:T(8,128)} copy(f32[8,192,64]{1,0,2:T(8,128)S(1)} %broadcast_multiply_fusion) | data formatting | bytes 786432 | tf_op jit(solution)/shard_map/mul | solution.py:64
  153.2 8.3 %reduce_sum.50 = f32[8,96,32]{0,2,1:T(8,128)S(1)} reduce(f32[8,96,2,32,2]{0,4,3,2,1:T(2,128)} %bitcast.149, f32[]{:T(128)} %constant.5.clone.1), dimensions={2,4}, to_apply=%region_8.9 | reduce | flops 73728 | bytes 491524 | tf_op jit(solution)/shard_map/reduce_sum | solution.py:64
  170.2 2.4 collective-permute-start.9
  176.4 5.4 %pad_slice_fusion.233 = (f32[8,192,64]{1,0,2:T(8,128)}, f32[8,192,64]{1,0,2:T(8,128)}, f32[8,192,64]{1,0,2:T(8,128)}, f32[8,192,64]{1,0,2:T(8,128)}, f32[8,192,6...) fusion(f32[8,192,64]{1,0,2:T(8,128)S(1)} %broadcast_multiply_fusion), kind=kLoop, calls=%fused_computation.514 | loop fusion | bytes 6684672 | tf_op jit(solution)/shard_map/slice | solution.py:38
  181.8 7.9 %reshape.421 = f32[8,384,128]{2,1,0:T(8,128)S(1)} reshape(f32[8,48,8,8,16]{4,3,2,1,0:T(8,128)} %copy.108) | data formatting | bytes 3145728 | tf_op jit(solution)/shard_map/reshape | solution.py:126
  191.7 8.0 %pad_slice_fusion.95 = (f32[8,384,128]{2,1,0:T(8,128)}, f32[8,384,128]{2,1,0:T(8,128)}, f32[8,384,128]{2,1,0:T(8,128)}, f32[8,384,128]{2,1,0:T(8,128)}, f32[8,38...) fusion(f32[8,384,128]{2,1,0:T(8,128)S(1)} %reshape.421), kind=kLoop, calls=%fused_computation.201 | loop fusion | bytes 26738688 | tf_op jit(solution)/shard_map/slice | solution.py:38
  203.7 5.3 %collective-permute-start.7 = (f32[2,8,48,8]{2,1,0,3:T(8,128)}, f32[2,8,48,8]{2,1,0,3:T(8,128)}, u32[]{:S(2)}, u32[]{:S(2)}) collective-permute-start(f32[2,8,48,8]{2,1,0,3:T(8,128)} %get-tuple-element.235), channel_id=1, source_target_pairs={{1,0},{2,1},{3,2},{4,3},{5,4},{6,5},{7,6},{8,7},{9,8},{10,9},{11,1... | collective-permute-start | bytes 73736 | tf_op jit(solution)/shard_map/ppermute | solution.py:25
  213.3 3.2 copy.109
  216.6 3.0 copy.110
  221.3 3.2 copy.112
  224.5 3.0 copy.113
  229.2 3.1 copy.115
  232.3 3.0 copy.116
  237.0 3.1 copy.119
  240.1 3.0 copy.120
  244.9 3.1 copy.122
  248.0 3.1 copy.123
  254.8 12.2 %multiply_add_fusion = f32[2,8,384,128]{2,3,1,0:T(8,128)S(1)} fusion(f32[8,384,128]{1,2,0:T(8,128)} %copy.125, f32[2]{0:T(128)S(1)} %copy-done.63, f32[8,384,128]{1,2,0:T(8,128)} %copy.124, f32[2]{0:T(128)S(1)} %copy-done.64, f32[8,384,128]{1,2,0:T(8,128)} %copy.123, f32[2]{0:T(128)S(1)} %copy-done.65, f32[8,384,128]{1,2,0:T(8,128)} %copy.122, ...), kind=kLoop, calls=%fused_computation.92 | loop fusion | flops 25952256 | bytes 29884552 | tf_op jit(solution)/shard_map/add | solution.py:37
  271.9 5.4 %collective-permute-start.5 = (f32[2,8,96,8]{2,1,0,3:T(8,128)}, f32[2,8,96,8]{2,1,0,3:T(8,128)}, u32[]{:S(2)}, u32[]{:S(2)}) collective-permute-start(f32[2,8,96,8]{2,1,0,3:T(8,128)} %get-tuple-element.217), channel_id=1, source_target_pairs={{1,0},{2,1},{3,2},{4,3},{5,4},{6,5},{7,6},{8,7},{9,8},{10,9},{11,1... | collective-permute-start | bytes 147464 | tf_op jit(solution)/shard_map/ppermute | solution.py:25
  283.1 5.4 %collective-permute-start.3 = (f32[2,8,192,8]{2,1,0,3:T(8,128)}, f32[2,8,192,8]{2,1,0,3:T(8,128)}, u32[]{:S(2)}, u32[]{:S(2)}) collective-permute-start(f32[2,8,192,8]{2,1,0,3:T(8,128)} %get-tuple-element.199), channel_id=1, source_target_pairs={{1,0},{2,1},{3,2},{4,3},{5,4},{6,5},{7,6},{8,7},{9,8},{10,9},{11,1... | collective-permute-start | bytes 294920 | tf_op jit(solution)/shard_map/ppermute | solution.py:25
  294.9 5.4 %collective-permute-start.1 = (f32[2,8,384,8]{2,3,1,0:T(8,128)}, f32[2,8,384,8]{2,3,1,0:T(8,128)}, u32[]{:S(2)}, u32[]{:S(2)}) collective-permute-start(f32[2,8,384,8]{2,3,1,0:T(8,128)} %get-tuple-element.181), channel_id=1, source_target_pairs={{1,0},{2,1},{3,2},{4,3},{5,4},{6,5},{7,6},{8,7},{9,8},{10,9},{11,1... | collective-permute-start | bytes 589832 | tf_op jit(solution)/shard_map/ppermute | solution.py:25
  301.2 5.6 %fusion.49 = f32[8,96,32]{1,0,2:T(8,128)} fusion(f32[8,96,32]{1,0,2:T(8,128)S(1)} %bitcast.164, f32[2,8,96,32]{2,1,0,3:T(8,128)} %copy-done.29, f32[2,8,96,8]{2,1,0,3:T(8,128)} %collective-permute-done.5, f32[2,8,96,8]{2,1,0,3:T(8,128)} %collective-permute-done.4, f32[2]{0:T(128)} %get-tuple-element.79, f32[2]{0:T(128)} %get-tuple-element.80, ...), kind=kOutput, calls=%fused_computation.113 | convolution fusion | flops 7176192 | bytes 606720 | tf_op jit(solution)/shard_map/rzw,rwyx->zyx/dot_general | solution.py:59
  310.4 11.3 %fusion.47 = f32[8,192,64]{1,0,2:T(8,128)} fusion(f32[8,192,64]{1,0,2:T(8,128)S(1)} %bitcast.161, f32[2,8,192,64]{2,1,0,3:T(8,128)} %copy-done.28, f32[2,8,192,8]{2,1,0,3:T(8,128)} %collective-permute-done.3, f32[2,8,192,8]{2,1,0,3:T(8,128)} %collective-permute-done.2, f32[2]{0:T(128)} %get-tuple-element.45, f32[2]{0:T(128)} %get-tuple-element.46, ...), kind=kOutput, calls=%fused_computation.96 | convolution fusion | flops 28704768 | bytes 2113544 | tf_op jit(solution)/shard_map/rzw,rwyx->zyx/dot_general | solution.py:59
  323.9 2.4 broadcast_in_dim.37
  326.3 2.7 copy.158
  329.2 2.4 broadcast_in_dim.38
  331.6 3.0 copy.159
  334.8 11.7 %fusion.3 = f32[2,8,384,128]{2,3,1,0:T(8,128)} fusion(f32[2,8,384,8]{2,3,1,0:T(8,128)} %collective-permute-done.1, f32[2,8,384,8]{2,3,1,0:T(8,128)} %collective-permute-done, f32[2,8,384,128]{2,3,1,0:T(8,128)S(1)} %multiply_add_fusion, f32[2]{0:T(128)S(1)} %copy-done.113, f32[2]{0:T(128)S(1)} %copy-done.114, f32[2]{0:T(128)S(1)} %copy-done.115, ...), kind=kLoop, calls=%fused_computation.37 | loop fusion | flops 38535168 | bytes 6684808 | tf_op jit(solution)/shard_map/add | solution.py:47
  346.5 2.7 copy.126
  349.1 3.2 bitcast_add_fusion
  352.7 6.4 %reshape.422 = f32[8,48,8,8,16]{4,3,2,1,0:T(8,128)} reshape(f32[8,384,128]{2,1,0:T(8,128)S(1)} %copy.166) | data formatting | bytes 3145728 | tf_op jit(solution)/shard_map/reshape | solution.py:142
  359.1 11.8 %copy.161 = f32[48,8,8,8,16]{4,3,2,1,0:T(8,128)} copy(f32[48,8,8,8,16]{4,1,3,0,2:T(8,128)} %bitcast.148) | data formatting | bytes 3145728 | tf_op jit(solution)/shard_map/transpose | solution.py:143
  370.9 7.9 %reshape.423 = f32[384,8,128]{2,1,0:T(8,128)S(1)} reshape(f32[48,8,8,8,16]{4,3,2,1,0:T(8,128)} %copy.161) | data formatting | bytes 3145728 | tf_op jit(solution)/shard_map/reshape | solution.py:144
  378.8 2.7 gather_fusion
  381.6 4.1 %fusion.407 = f32[384,4,8]{2,1,0:T(4,128)S(1)} fusion(f32[384,4,128]{2,1,0:T(4,128)S(1)} %copy-done.3, f32[384,8,128]{2,1,0:T(8,128)} %gather_fusion), kind=kOutput, calls=%fused_computation.781 | convolution fusion | flops 18874368 | bytes 2408448 | tf_op jit(solution)/shard_map/kzc,ksc->ksz/dot_general | solution.py:146
  386.6 3.3 all-to-all-start.3
  389.9 4.1 %all-to-all-done.3 = f32[4,96,32]{1,2,0:T(8,128)S(1)} async-done(((f32[4,96,32]{1,2,0:T(8,128)}), f32[4,96,32]{1,2,0:T(8,128)S(1)}, u32[]{:S(2)}, u32[]{:S(2)}) %all-to-all-start.3) | async-done | bytes 49184 | tf_op jit(solution)/shard_map/all_to_all | solution.py:149
  (425 shorter events, 86.9 us)
Async XLA Ops:
  0.6 26.7 %copy-start.47 = (f32[1024,128]{1,0:T(8,128)S(1)}, f32[1024,128]{1,0:T(8,128)}, u32[]{:S(2)}) copy-start(f32[1024,128]{1,0:T(8,128)} %param.11) | copy-start | bytes 1572868
  7.1 15.8 %all-to-all-start = ((f32[4,96,1]{1,2,0:T(1,128)}), f32[4,96,1]{1,2,0:T(1,128)S(1)}, u32[]{:S(2)}, u32[]{:S(2)}) async-start(f32[4,96,1]{1,2,0:T(1,128)} %bitcast.9), calls=%async_computation | async-start | bytes 4096 | tf_op jit(solution)/shard_map/all_to_all | solution.py:116
  19.3 17.7 %copy-start.10 = (f32[8,1024]{0,1:T(8,128)}, f32[8,1024]{0,1:T(8,128)S(1)}, u32[]{:S(2)}) copy-start(f32[8,1024]{0,1:T(8,128)S(1)} %copy.102) | copy-start | bytes 98308
  23.0 7.4 %all-to-all-start.1 = ((f32[4,96,32]{1,2,0:T(8,128)}), f32[4,96,32]{1,2,0:T(8,128)S(1)}, u32[]{:S(2)}, u32[]{:S(2)}) async-start(f32[4,96,32]{1,2,0:T(8,128)} %copy.105), calls=%async_computation.1 | async-start | bytes 131072 | tf_op jit(solution)/shard_map/all_to_all | solution.py:115
  30.3 15.1 %all-to-all-start.2 = ((f32[4,96,512]{2,1,0:T(8,128)}), f32[4,96,512]{2,1,0:T(8,128)S(1)}, u32[]{:S(2)}, u32[]{:S(2)}) async-start(f32[4,96,512]{2,1,0:T(8,128)} %bitcast.15), calls=%async_computation.2 | async-start | bytes 1572864 | tf_op jit(solution)/shard_map/all_to_all | solution.py:114
  137.6 38.8 %copy-start = (f32[8,192,64]{1,0,2:T(8,128)}, f32[8,192,64]{1,0,2:T(8,128)S(1)}, u32[]{:S(2)}) copy-start(f32[8,192,64]{1,0,2:T(8,128)S(1)} %broadcast_multiply_fusion) | copy-start | bytes 1179652
  170.2 101.8 %collective-permute-start.9 = (f32[2,8,24,8]{2,1,0,3:T(8,128)}, f32[2,8,24,8]{2,1,0,3:T(8,128)}, u32[]{:S(2)}, u32[]{:S(2)}) collective-permute-start(f32[2,8,24,8]{2,1,0,3:T(8,128)} %multiply_add_fusion.4), channel_id=1, source_target_pairs={{1,0},{2,1},{3,2},{4,3},{5,4},{6,5},{7,6},{8,7},{9,8},{10,9},{11,1... | collective-permute-start | bytes 36872 | tf_op jit(solution)/shard_map/ppermute | solution.py:25
  172.6 104.8 %collective-permute-start.8 = (f32[2,8,24,8]{2,1,0,3:T(8,128)}, f32[2,8,24,8]{2,1,0,3:T(8,128)}, u32[]{:S(2)}, u32[]{:S(2)}) collective-permute-start(f32[2,8,24,8]{2,1,0,3:T(8,128)} %multiply_add_fusion.4), channel_id=1, source_target_pairs={{0,1},{1,2},{2,3},{3,4},{4,5},{5,6},{6,7},{7,8},{8,9},{9,10},{10,1... | collective-permute-start | bytes 36872 | tf_op jit(solution)/shard_map/ppermute | solution.py:24
  191.6 17.4 %copy-start.30 = (f32[8,96,32]{1,0,2:T(8,128)S(1)}, f32[8,96,32]{1,0,2:T(8,128)}, u32[]{:S(2)}) copy-start(f32[8,96,32]{1,0,2:T(8,128)} %get-tuple-element.219) | copy-start | bytes 294916
  191.6 17.4 %copy-start.31 = (f32[8,96,32]{1,0,2:T(8,128)S(1)}, f32[8,96,32]{1,0,2:T(8,128)}, u32[]{:S(2)}) copy-start(f32[8,96,32]{1,0,2:T(8,128)} %get-tuple-element.220) | copy-start | bytes 294916
  191.6 17.4 %copy-start.32 = (f32[8,96,32]{1,0,2:T(8,128)S(1)}, f32[8,96,32]{1,0,2:T(8,128)}, u32[]{:S(2)}) copy-start(f32[8,96,32]{1,0,2:T(8,128)} %get-tuple-element.221) | copy-start | bytes 294916
  191.6 17.4 %copy-start.33 = (f32[8,96,32]{1,0,2:T(8,128)S(1)}, f32[8,96,32]{1,0,2:T(8,128)}, u32[]{:S(2)}) copy-start(f32[8,96,32]{1,0,2:T(8,128)} %get-tuple-element.222) | copy-start | bytes 294916
  191.6 17.4 %copy-start.34 = (f32[8,96,32]{1,0,2:T(8,128)S(1)}, f32[8,96,32]{1,0,2:T(8,128)}, u32[]{:S(2)}) copy-start(f32[8,96,32]{1,0,2:T(8,128)} %get-tuple-element.223) | copy-start | bytes 294916
  191.6 17.4 %copy-start.35 = (f32[8,96,32]{1,0,2:T(8,128)S(1)}, f32[8,96,32]{1,0,2:T(8,128)}, u32[]{:S(2)}) copy-start(f32[8,96,32]{1,0,2:T(8,128)} %get-tuple-element.224) | copy-start | bytes 294916
  191.6 17.4 %copy-start.36 = (f32[8,96,32]{1,0,2:T(8,128)S(1)}, f32[8,96,32]{1,0,2:T(8,128)}, u32[]{:S(2)}) copy-start(f32[8,96,32]{1,0,2:T(8,128)} %get-tuple-element.225) | copy-start | bytes 294916
  191.7 17.4 %copy-start.37 = (f32[8,96,32]{1,0,2:T(8,128)S(1)}, f32[8,96,32]{1,0,2:T(8,128)}, u32[]{:S(2)}) copy-start(f32[8,96,32]{1,0,2:T(8,128)} %get-tuple-element.226) | copy-start | bytes 294916
  191.7 17.4 %copy-start.38 = (f32[8,96,32]{1,0,2:T(8,128)S(1)}, f32[8,96,32]{1,0,2:T(8,128)}, u32[]{:S(2)}) copy-start(f32[8,96,32]{1,0,2:T(8,128)} %get-tuple-element.227) | copy-start | bytes 294916
  191.7 17.4 %copy-start.39 = (f32[8,96,32]{1,0,2:T(8,128)S(1)}, f32[8,96,32]{1,0,2:T(8,128)}, u32[]{:S(2)}) copy-start(f32[8,96,32]{1,0,2:T(8,128)} %get-tuple-element.228) | copy-start | bytes 294916
  191.7 17.4 %copy-start.40 = (f32[8,96,32]{1,0,2:T(8,128)S(1)}, f32[8,96,32]{1,0,2:T(8,128)}, u32[]{:S(2)}) copy-start(f32[8,96,32]{1,0,2:T(8,128)} %get-tuple-element.229) | copy-start | bytes 294916
  191.7 17.4 %copy-start.41 = (f32[8,96,32]{1,0,2:T(8,128)S(1)}, f32[8,96,32]{1,0,2:T(8,128)}, u32[]{:S(2)}) copy-start(f32[8,96,32]{1,0,2:T(8,128)} %get-tuple-element.230) | copy-start | bytes 294916
  191.7 17.4 %copy-start.42 = (f32[8,96,32]{1,0,2:T(8,128)S(1)}, f32[8,96,32]{1,0,2:T(8,128)}, u32[]{:S(2)}) copy-start(f32[8,96,32]{1,0,2:T(8,128)} %get-tuple-element.231) | copy-start | bytes 294916
  191.7 17.4 %copy-start.43 = (f32[8,96,32]{1,0,2:T(8,128)S(1)}, f32[8,96,32]{1,0,2:T(8,128)}, u32[]{:S(2)}) copy-start(f32[8,96,32]{1,0,2:T(8,128)} %get-tuple-element.232) | copy-start | bytes 294916
  191.7 17.4 %copy-start.44 = (f32[8,96,32]{1,0,2:T(8,128)S(1)}, f32[8,96,32]{1,0,2:T(8,128)}, u32[]{:S(2)}) copy-start(f32[8,96,32]{1,0,2:T(8,128)} %get-tuple-element.233) | copy-start | bytes 294916
  201.6 81.5 %collective-permute-start.6 = (f32[2,8,48,8]{2,1,0,3:T(8,128)}, f32[2,8,48,8]{2,1,0,3:T(8,128)}, u32[]{:S(2)}, u32[]{:S(2)}) collective-permute-start(f32[2,8,48,8]{2,1,0,3:T(8,128)} %get-tuple-element.234), channel_id=1, source_target_pairs={{0,1},{1,2},{2,3},{3,4},{4,5},{5,6},{6,7},{7,8},{8,9},{9,10},{10,1... | collective-permute-start | bytes 73736 | tf_op jit(solution)/shard_map/ppermute | solution.py:24
  203.7 84.9 %collective-permute-start.7 = (f32[2,8,48,8]{2,1,0,3:T(8,128)}, f32[2,8,48,8]{2,1,0,3:T(8,128)}, u32[]{:S(2)}, u32[]{:S(2)}) collective-permute-start(f32[2,8,48,8]{2,1,0,3:T(8,128)} %get-tuple-element.235), channel_id=1, source_target_pairs={{1,0},{2,1},{3,2},{4,3},{5,4},{6,5},{7,6},{8,7},{9,8},{10,9},{11,1... | collective-permute-start | bytes 73736 | tf_op jit(solution)/shard_map/ppermute | solution.py:25
  211.0 83.9 %collective-permute-start.4 = (f32[2,8,96,8]{2,1,0,3:T(8,128)}, f32[2,8,96,8]{2,1,0,3:T(8,128)}, u32[]{:S(2)}, u32[]{:S(2)}) collective-permute-start(f32[2,8,96,8]{2,1,0,3:T(8,128)} %get-tuple-element.216), channel_id=1, source_target_pairs={{0,1},{1,2},{2,3},{3,4},{4,5},{5,6},{6,7},{7,8},{8,9},{9,10},{10,1... | collective-permute-start | bytes 147464 | tf_op jit(solution)/shard_map/ppermute | solution.py:24
  254.6 13.3 %copy-start.1 = (f32[8,192,64]{1,0,2:T(8,128)S(1)}, f32[8,192,64]{1,0,2:T(8,128)}, u32[]{:S(2)}) copy-start(f32[8,192,64]{1,0,2:T(8,128)} %copy-done) | copy-start | bytes 1179652
  254.6 13.3 %copy-start.12 = (f32[8,192,64]{1,0,2:T(8,128)S(1)}, f32[8,192,64]{1,0,2:T(8,128)}, u32[]{:S(2)}) copy-start(f32[8,192,64]{1,0,2:T(8,128)} %get-tuple-element.200) | copy-start | bytes 1179652
  254.6 13.3 %copy-start.13 = (f32[8,192,64]{1,0,2:T(8,128)S(1)}, f32[8,192,64]{1,0,2:T(8,128)}, u32[]{:S(2)}) copy-start(f32[8,192,64]{1,0,2:T(8,128)} %get-tuple-element.201) | copy-start | bytes 1179652
  254.6 13.3 %copy-start.14 = (f32[8,192,64]{1,0,2:T(8,128)S(1)}, f32[8,192,64]{1,0,2:T(8,128)}, u32[]{:S(2)}) copy-start(f32[8,192,64]{1,0,2:T(8,128)} %get-tuple-element.202) | copy-start | bytes 1179652
  254.6 13.3 %copy-start.15 = (f32[8,192,64]{1,0,2:T(8,128)S(1)}, f32[8,192,64]{1,0,2:T(8,128)}, u32[]{:S(2)}) copy-start(f32[8,192,64]{1,0,2:T(8,128)} %get-tuple-element.203) | copy-start | bytes 1179652
  268.1 22.4 %copy-start.46 = (f32[2,8,48,16]{2,1,0,3:T(8,128)S(1)}, f32[2,8,48,16]{2,1,0,3:T(8,128)}, u32[]{:S(2)}) copy-start(f32[2,8,48,16]{2,1,0,3:T(8,128)} %copy-done.45) | copy-start | bytes 147460
  268.2 22.4 %copy-start.130 = (f32[2]{0:T(128)S(1)}, f32[2]{0:T(128)}, u32[]{:S(2)}) copy-start(f32[2]{0:T(128)} %get-tuple-element.112) | copy-start | bytes 28
  268.2 22.4 %copy-start.131 = (f32[2]{0:T(128)S(1)}, f32[2]{0:T(128)}, u32[]{:S(2)}) copy-start(f32[2]{0:T(128)} %get-tuple-element.113) | copy-start | bytes 28
  268.2 22.4 %copy-start.132 = (f32[2]{0:T(128)S(1)}, f32[2]{0:T(128)}, u32[]{:S(2)}) copy-start(f32[2]{0:T(128)} %get-tuple-element.114) | copy-start | bytes 28
  268.2 22.4 %copy-start.133 = (f32[2]{0:T(128)S(1)}, f32[2]{0:T(128)}, u32[]{:S(2)}) copy-start(f32[2]{0:T(128)} %get-tuple-element.115) | copy-start | bytes 28
  268.2 22.4 %copy-start.134 = (f32[2]{0:T(128)S(1)}, f32[2]{0:T(128)}, u32[]{:S(2)}) copy-start(f32[2]{0:T(128)} %get-tuple-element.116) | copy-start | bytes 28
  268.2 22.4 %copy-start.135 = (f32[2]{0:T(128)S(1)}, f32[2]{0:T(128)}, u32[]{:S(2)}) copy-start(f32[2]{0:T(128)} %get-tuple-element.117) | copy-start | bytes 28
  268.2 22.4 %copy-start.136 = (f32[2]{0:T(128)S(1)}, f32[2]{0:T(128)}, u32[]{:S(2)}) copy-start(f32[2]{0:T(128)} %get-tuple-element.118) | copy-start | bytes 28
  268.2 22.4 %copy-start.137 = (f32[2]{0:T(128)S(1)}, f32[2]{0:T(128)}, u32[]{:S(2)}) copy-start(f32[2]{0:T(128)} %get-tuple-element.119) | copy-start | bytes 28
  268.2 22.4 %copy-start.138 = (f32[2]{0:T(128)S(1)}, f32[2]{0:T(128)}, u32[]{:S(2)}) copy-start(f32[2]{0:T(128)} %get-tuple-element.120) | copy-start | bytes 28
  271.9 28.4 %collective-permute-start.5 = (f32[2,8,96,8]{2,1,0,3:T(8,128)}, f32[2,8,96,8]{2,1,0,3:T(8,128)}, u32[]{:S(2)}, u32[]{:S(2)}) collective-permute-start(f32[2,8,96,8]{2,1,0,3:T(8,128)} %get-tuple-element.217), channel_id=1, source_target_pairs={{1,0},{2,1},{3,2},{4,3},{5,4},{6,5},{7,6},{8,7},{9,8},{10,9},{11,1... | collective-permute-start | bytes 147464 | tf_op jit(solution)/shard_map/ppermute | solution.py:25
  277.4 33.0 %collective-permute-start.2 = (f32[2,8,192,8]{2,1,0,3:T(8,128)}, f32[2,8,192,8]{2,1,0,3:T(8,128)}, u32[]{:S(2)}, u32[]{:S(2)}) collective-permute-start(f32[2,8,192,8]{2,1,0,3:T(8,128)} %get-tuple-element.198), channel_id=1, source_target_pairs={{0,1},{1,2},{2,3},{3,4},{4,5},{5,6},{6,7},{7,8},{8,9},{9,10},{10,1... | collective-permute-start | bytes 294920 | tf_op jit(solution)/shard_map/ppermute | solution.py:24
  283.1 27.2 %collective-permute-start.3 = (f32[2,8,192,8]{2,1,0,3:T(8,128)}, f32[2,8,192,8]{2,1,0,3:T(8,128)}, u32[]{:S(2)}, u32[]{:S(2)}) collective-permute-start(f32[2,8,192,8]{2,1,0,3:T(8,128)} %get-tuple-element.199), channel_id=1, source_target_pairs={{1,0},{2,1},{3,2},{4,3},{5,4},{6,5},{7,6},{8,7},{9,8},{10,9},{11,1... | collective-permute-start | bytes 294920 | tf_op jit(solution)/shard_map/ppermute | solution.py:25
  288.6 46.0 %collective-permute-start = (f32[2,8,384,8]{2,3,1,0:T(8,128)}, f32[2,8,384,8]{2,3,1,0:T(8,128)}, u32[]{:S(2)}, u32[]{:S(2)}) collective-permute-start(f32[2,8,384,8]{2,3,1,0:T(8,128)} %get-tuple-element.180), channel_id=1, source_target_pairs={{0,1},{1,2},{2,3},{3,4},{4,5},{5,6},{6,7},{7,8},{8,9},{9,10},{10,1... | collective-permute-start | bytes 589832 | tf_op jit(solution)/shard_map/ppermute | solution.py:24
  294.9 39.7 %collective-permute-start.1 = (f32[2,8,384,8]{2,3,1,0:T(8,128)}, f32[2,8,384,8]{2,3,1,0:T(8,128)}, u32[]{:S(2)}, u32[]{:S(2)}) collective-permute-start(f32[2,8,384,8]{2,3,1,0:T(8,128)} %get-tuple-element.181), channel_id=1, source_target_pairs={{1,0},{2,1},{3,2},{4,3},{5,4},{6,5},{7,6},{8,7},{9,8},{10,9},{11,1... | collective-permute-start | bytes 589832 | tf_op jit(solution)/shard_map/ppermute | solution.py:25
  381.6 13.6 %copy-start.11 = (f32[8,1024]{0,1:T(8,128)S(1)}, f32[8,1024]{0,1:T(8,128)}, u32[]{:S(2)}) copy-start(f32[8,1024]{0,1:T(8,128)} %copy-done.10) | copy-start | bytes 98308
  386.6 7.4 %all-to-all-start.3 = ((f32[4,96,32]{1,2,0:T(8,128)}), f32[4,96,32]{1,2,0:T(8,128)S(1)}, u32[]{:S(2)}, u32[]{:S(2)}) async-start(f32[4,96,32]{1,2,0:T(8,128)} %copy.163), calls=%async_computation.3 | async-start | bytes 131072 | tf_op jit(solution)/shard_map/all_to_all | solution.py:149
  (112 other events, 807.4 us)
where the time goes:
time: 402 us; the launch traced here: 397 us
  local copies, waits for them, and re-layouts  216 us (54%)
  other arithmetic  84.6 us (21%)
  starting transfers between devices  47.4 us (12%)
  matrix products  32.3 us (8%)
  waiting for transfers between devices  11.8 us (3%)
  between operations  4.13 us (1%)
    slice x37, local copies, waits for them, and re-layouts, across_ranks(): padded[None, :, offset:offset + extent, :]  59.2 us
    reduce_sum x4, other arithmetic, restrict(): charge_field.reshape(planes, rows // 2, 2, columns // 2, 2).sum(axis=(2, 4))  35.8 us
    transpose x2, local copies, waits for them, and re-layouts, body(): charge_grid = tile_grid.reshape(NY // BY, CX // BX, planes, BY, BX).trans...  34.2 us
    ppermute x5, starting transfers between devices, padded_2(): after = lax.ppermute(initial, axis, down)  24 us
    dot_general x5, matrix products, level_term(): return jnp.einsum('rzw,rwyx->zyx', mixing, ranked, precision=precise)  23.8 us
    mul x4, local copies, waits for them, and re-layouts, restrict(): 0.5 * charge_field.reshape(planes, rows // 2, 2, columns // 2, 2).sum(axi...  17.2 us
    add x5, other arithmetic, across_ranks(): summed + kernel[:, offset][:, None, None, None] * padded[None, :, offset:...  17.1 us
    scatter-add x1, other arithmetic, body(): jnp.zeros((TILES, planes, cell_count), jnp.float32).at[tile_ids]  14.9 us
  transfers between devices with their start and end apart: 14, of which 3 were waited for; matrix products, arithmetic and copies ran while one was open for 37% of the time, Pallas kernels for 0%

commit v1 on v0

v1 whole, which is shorter than its diff:
```python
import functools

import jax
import jax.numpy as jnp
from jax import lax
from jax.experimental import pallas as pl
from jax.experimental.pallas import tpu as pltpu
from jax.sharding import PartitionSpec as P

NY = 384
CX = 128
LEVELS = 4
TILES = 384
PLANES = 8
TAPS = 17
REACH = TAPS // 2
SLOTS = 4
BRICKS = 256
CAP = 96
PEERS = 4
CELLS = SLOTS * CAP
PACK = CAP // 2
ROWS = CELLS + PACK
SEGS = BRICKS * SLOTS
HEIGHTS = tuple(NY >> level for level in range(LEVELS + 1))
WIDTHS = tuple(CX >> level for level in range(LEVELS + 1))
LANE_OF = (0, 0, 64, 96, 112)
RIM_ROW = (0, 0, 192, 288, 336)
STEP = (384, 192, 96, 48, 32)
K_OF = (0, 768, 1152, 1344, 1440)
DEPTH = 1536
F32 = jnp.float32
BF16 = jnp.bfloat16


def split(value):
    high = value.astype(BF16)
    return high, (value - high.astype(F32)).astype(BF16)


def dot(left, right):
    return jnp.dot(left, right, preferred_element_type=F32)


def iota(shape, dim):
    return lax.broadcasted_iota(jnp.int32, shape, dim)


def swap_groups(value):
    count = value.shape[0] // 8
    value = value.reshape(count, 8, CX)
    row, group = iota((1, 8, CX), 1), iota((1, 8, CX), 2) // 16
    for bit in range(3):
        step = 1 << bit
        row_bit, group_bit = (row >> bit) & 1, (group >> bit) & 1
        ahead = pltpu.roll(pltpu.roll(value, 8 - step, 1), 16 * step, 2)
        if step == 4:
            behind = ahead
        else:
            behind = pltpu.roll(pltpu.roll(value, step, 1), CX - 16 * step, 2)
        value = jnp.where(row_bit == group_bit, value, jnp.where(group_bit == 1, ahead, behind))
    return value.reshape(count * 8, CX)


def route_kernel(
    count_ref, currents_ref, planes_ref, cells_ref, dest_ref, tile_ref, *refs
):
    outs, slot_ref, feature = refs[:PEERS], refs[PEERS], refs[PEERS + 1]
    me = lax.axis_index("sect")
    turn = dest_ref[...] ^ me
    onehot = iota((16, BRICKS), 0) == turn
    onehot_f = onehot.astype(F32)
    before = (iota((BRICKS, BRICKS), 0) < iota((BRICKS, BRICKS), 1)).astype(F32).astype(BF16)
    earlier = dot(onehot_f.astype(BF16), before)
    base = (iota((16, BRICKS), 0) * CAP).astype(F32)
    slot = jnp.sum(onehot_f * (earlier + base), axis=0, keepdims=True)
    slot_ref[...] = jnp.broadcast_to(slot, slot_ref.shape)
    choose = (iota((PEERS * CAP, BRICKS), 0).astype(F32) == slot).astype(F32).astype(BF16)
    alive = (iota((1, SEGS), 1) // SLOTS < count_ref[0]).astype(F32)
    currents = currents_ref[...] * alive
    lines = jnp.concatenate(
        [planes_ref[...], currents, jnp.zeros((CX - PLANES - 1, SEGS), F32)], axis=0
    )
    for part in range(SEGS // CX):
        feature[part * CX : (part + 1) * CX, :] = lines[:, part * CX : (part + 1) * CX].T
    meta = jnp.zeros((BRICKS, CX), F32)
    for s in range(SLOTS):
        rows = feature[pl.ds(s, BRICKS, stride=SLOTS), :]
        meta = meta + (pltpu.roll(rows, 16 * s, 1) if s else rows)
    tiles = jnp.concatenate(
        [tile_ref[...].astype(F32), jnp.zeros((CX - 1, BRICKS), F32)], axis=0
    )
    tiles = jnp.concatenate([tiles[:, :CX].T, tiles[:, CX:].T], axis=0)
    meta = meta + pltpu.roll(tiles, 9, 1)
    both = dot(choose, jnp.concatenate(split(meta), axis=1))
    both = both[:, :CX] + both[:, CX:]
    for k in range(PEERS):
        lower = both[k * CAP : k * CAP + PACK]
        upper = both[k * CAP + PACK : (k + 1) * CAP]
        outs[k][CELLS:, :] = lower + pltpu.roll(upper, CX // 2, 1)
    for s in range(SLOTS):
        high, low = split(cells_ref[pl.ds(s, BRICKS, stride=SLOTS), :])
        moved = dot(choose, jnp.concatenate([high, low], axis=1))
        moved = moved[:, :CX] + moved[:, CX:]
        for k in range(PEERS):
            outs[k][s * CAP : (s + 1) * CAP, :] = moved[k * CAP : (k + 1) * CAP]


def prep_kernel(across_ref, along_ref, along_high, along_low, across_high, across_low):
    for level in range(LEVELS + 1):
        lane, width = LANE_OF[level], WIDTHS[level]
        row = iota((2 * CX, 1), 0)
        own = row - lane
        own = jnp.where((row < CX) & (own >= 0) & (own < width), own, 4 * NY)
        first, second = row - CX, row - CX - CX // 2
        before = first if level == 0 else second
        after = second if level == 0 else first
        place = jnp.where((before >= 0) & (before < REACH), before - REACH, own)
        place = jnp.where((after >= 0) & (after < REACH), after + width, place)
        shift = place - (iota((2 * CX, CX), 1) >> level) + REACH
        for r in range(2):
            taps = jnp.zeros((2 * CX, CX), F32)
            for t in range(TAPS):
                taps = jnp.where(shift == t, along_ref[level, r, t], taps)
            high, low = split(taps * (0.5**level))
            along_high[level, :, r * CX : (r + 1) * CX] = high
            along_low[level, :, r * CX : (r + 1) * CX] = low
    for part in range(DEPTH // CX):
        column = iota((1, CX), 1) + part * CX
        pieces = []
        for level in range(LEVELS + 1):
            for r in range(2):
                start = K_OF[level] + r * STEP[level]
                if start < (part + 1) * CX and start + HEIGHTS[level] > part * CX:
                    pieces.append((level, r, start))
        held = []
        far = jnp.full((1, CX), 4 * NY, jnp.int32)
        offset, levels = far, jnp.zeros((1, CX), jnp.int32)
        for level, r, start in pieces:
            inside = (column >= start) & (column < start + HEIGHTS[level])
            held.append(inside)
            offset = jnp.where(inside, column - start + REACH, offset)
            levels = jnp.where(inside, level, levels)
        shift = offset - (iota((NY, CX), 0) >> jnp.broadcast_to(levels, (NY, CX)))
        taps = jnp.zeros((NY, CX), F32)
        for t in range(TAPS):
            line = jnp.zeros((1, CX), F32)
            for (level, r, start), inside in zip(pieces, held):
                line = jnp.where(inside, across_ref[level, r, t], line)
            taps = jnp.where(shift == t, line, taps)
        high, low = split(taps)
        across_high[:, part * CX : (part + 1) * CX] = high
        across_low[:, part * CX : (part + 1) * CX] = low


def unpack_meta(ref):
    packed = ref[CELLS:, :]
    return jnp.concatenate([packed, pltpu.roll(packed, CX // 2, 1)], axis=0)


def charge_kernel(r0, r1, r2, r3, q0, s1, s2, s3, s4, to_right, to_left, hot, bricks, narrow):
    half = PLANES * CX
    for j, ref in enumerate((r0, r1, r2, r3)):
        meta = unpack_meta(ref)
        charged = [
            ref[s * CAP : (s + 1) * CAP, :] * meta[:, 16 * s + 8 : 16 * s + 9] for s in range(SLOTS)
        ]
        for z in range(PLANES):
            total = charged[0] * meta[:, z : z + 1]
            for s in range(1, SLOTS):
                total = total + charged[s] * meta[:, 16 * s + z : 16 * s + z + 1]
            high, low = split(total)
            bricks[j * CX : j * CX + CAP, z * CX : (z + 1) * CX] = high
            bricks[j * CX : j * CX + CAP, half + z * CX : half + (z + 1) * CX] = low
        bricks[j * CX + CAP : (j + 1) * CX, :] = jnp.zeros((CX - CAP, 2 * half), BF16)
        whole = jnp.concatenate([meta, jnp.zeros((CX - CAP, CX), F32)], axis=0)
        names = whole.T[9:10, :]
        names = jnp.where(iota((1, CX), 1) < CAP, names, -1.0)
        match = (iota((TILES, CX), 0).astype(F32) == names).astype(F32).astype(BF16)
        hot[:, j * CX : (j + 1) * CX] = match
    lane, row = iota((CX, CX), 1), iota((CX, CX), 0)
    fold = jnp.zeros((CX, CX), F32)
    for level in range(1, LEVELS + 1):
        start = LANE_OF[level]
        mine = (lane >= start) & (lane < start + WIDTHS[level]) & ((row >> level) == lane - start)
        fold = jnp.where(mine, 0.5**level, fold)
    fold = fold.astype(BF16)
    fold = jnp.concatenate([fold, fold], axis=0)
    for z in range(PLANES):
        found = dot(hot[...], bricks[:, z * CX : (z + 1) * CX]) + dot(
            hot[...], bricks[:, half + z * CX : half + (z + 1) * CX]
        )
        field = swap_groups(found)
        q0[z] = field
        narrow[z * NY : (z + 1) * NY, :] = dot(jnp.concatenate(split(field), axis=1), fold)
    source = narrow
    for target in (s1, s2, s3, s4):
        size = target.shape[0]
        target[...] = source[pl.ds(0, size, stride=2), :] + source[pl.ds(1, size, stride=2), :]
        source = target
    lanes = iota((1, CX), 1)
    right = jnp.zeros((NY, CX), F32)
    left = jnp.zeros((NY, CX), F32)
    for z in range(PLANES):
        field = q0[z]
        low = (lanes >= 8 * z) & (lanes < 8 * z + 8)
        high = (lanes >= 64 + 8 * z) & (lanes < 72 + 8 * z)
        right = jnp.where(low, pltpu.roll(field, (8 * z - (CX - REACH)) % CX, 1), right)
        left = jnp.where(high, pltpu.roll(field, (64 + 8 * z) % CX, 1), left)
    to_right[...] = right
    to_left[...] = left
    for level, source in zip(range(1, LEVELS + 1), (s1, s2, s3, s4)):
        size, start, width = HEIGHTS[level], LANE_OF[level], WIDTHS[level]
        rows = slice(RIM_ROW[level], RIM_ROW[level] + size)
        right, left = to_right[rows, :], to_left[rows, :]
        for z in range(PLANES):
            field = source[z * size : (z + 1) * size, :]
            low = (lanes >= 8 * z) & (lanes < 8 * z + 8)
            high = (lanes >= 64 + 8 * z) & (lanes < 72 + 8 * z)
            right = jnp.where(
                high, pltpu.roll(field, (64 + 8 * z - (start + width - REACH)) % CX, 1), right
            )
            left = jnp.where(low, pltpu.roll(field, (8 * z - start) % CX, 1), left)
        to_right[rows, :] = right
        to_left[rows, :] = left


def field_kernel(
    mix_ref, q0, s1, s2, s3, s4, from_left, from_right, along_high, along_low, across_high,
    across_low, r0, r1, r2, r3, grid_ref, b0, b1, b2, b3, ranked, high_ref, low_ref, tiles, picked
):
    half = PLANES * CX
    lanes = iota((1, CX), 1)
    sources = (q0, s1, s2, s3, s4)
    for level in range(LEVELS + 1):
        size, step = HEIGHTS[level], STEP[level]
        if level == 0:
            rims = jnp.where(lanes < CX // 2, from_left[...], from_right[...])
        else:
            rows = slice(RIM_ROW[level], RIM_ROW[level] + size)
            rims = jnp.where(lanes < CX // 2, from_right[rows, :], from_left[rows, :])
        for z in range(PLANES):
            own = q0[z] if level == 0 else sources[level][z * size : (z + 1) * size, :]
            turned = pltpu.roll(rims, (CX - 8 * z) % CX, 1) if z else rims
            high, low = split(jnp.concatenate([own, turned], axis=1))
            ranked[z, :size, :] = (
                dot(high, along_high[level]) + dot(low, along_high[level])
                + dot(high, along_low[level])
            )
        chunk = {384: 32, 192: 32, 96: 32, 48: 16, 24: 24}[size]

        def mixed(index, carry, level=level, chunk=chunk, step=step):
            start = index * chunk
            if chunk % 8 == 0 and not isinstance(start, int):
                start = pl.multiple_of(start, chunk)
            for r in range(2):
                parts = [
                    ranked[w, pl.ds(start, chunk), r * CX : (r + 1) * CX] for w in range(PLANES)
                ]
                for z in range(PLANES):
                    total = parts[0] * mix_ref[level, r, z, 0]
                    for w in range(1, PLANES):
                        total = total + parts[w] * mix_ref[level, r, z, w]
                    if chunk == 24:
                        total = jnp.concatenate([total, jnp.zeros((8, CX), F32)], axis=0)
                    high, low = split(total)
                    length = 32 if chunk == 24 else chunk
                    place = K_OF[level] + r * step + start
                    high_ref[pl.ds(place, length), z * CX : (z + 1) * CX] = high
                    low_ref[pl.ds(place, length), z * CX : (z + 1) * CX] = low
            return carry

        if size // chunk == 1:
            mixed(0, 0)
        else:
            lax.fori_loop(0, size // chunk, mixed, 0)
    spare = K_OF[LEVELS] + 2 * STEP[LEVELS]
    high_ref[spare:, :] = jnp.zeros((DEPTH - spare, half), BF16)
    low_ref[spare:, :] = jnp.zeros((DEPTH - spare, half), BF16)
    for pair in range(PLANES // 2):
        part = slice(pair * 2 * CX, (pair + 1) * 2 * CX)
        total = dot(across_high[...], high_ref[:, part]) + dot(across_high[...], low_ref[:, part])
        total = total + dot(across_low[...], high_ref[:, part])
        for i in range(2):
            z = 2 * pair + i
            plane = total[:, i * CX : (i + 1) * CX]
            grid_ref[z] = plane
            high, low = split(swap_groups(plane))
            tiles[:, z * CX : (z + 1) * CX] = high
            tiles[:, half + z * CX : half + (z + 1) * CX] = low
    for ref, out in zip((r0, r1, r2, r3), (b0, b1, b2, b3)):
        meta = unpack_meta(ref)
        match = (iota((CAP, TILES), 1).astype(F32) == meta[:, 9:10]).astype(F32).astype(BF16)
        picked[...] = dot(match, tiles[:, :half]) + dot(match, tiles[:, half:])
        values = jnp.zeros((CAP, CX), F32)
        for s in range(SLOTS):
            total = picked[:, :CX] * meta[:, 16 * s : 16 * s + 1]
            for z in range(1, PLANES):
                total = total + picked[:, z * CX : (z + 1) * CX] * meta[:, 16 * s + z : 16 * s + z + 1]
            total = jnp.sum(total * ref[s * CAP : (s + 1) * CAP, :], axis=1, keepdims=True)
            values = jnp.where(lanes == s, total, values)
        values = jnp.concatenate([values, jnp.zeros((CX - CAP, CX), F32)], axis=0)
        out[...] = values.T[:8, :]


def pick_kernel(count_ref, slot_ref, b0, b1, b2, b3, out_ref):
    slot = slot_ref[0:1, :]
    turn = jnp.floor((slot + 0.5) * (1.0 / CAP))
    place = slot + turn * (CX - CAP)
    match = (iota((PEERS * CX, BRICKS), 0).astype(F32) == place).astype(F32).astype(BF16)
    held = jnp.concatenate([b0[...], b1[...], b2[...], b3[...]], axis=1)
    high, low = split(held)
    value = dot(jnp.concatenate([high, low], axis=0), match)
    value = value[:8] + value[8:]
    spread = (iota((BRICKS, SEGS), 1) // SLOTS == iota((BRICKS, SEGS), 0)).astype(F32).astype(BF16)
    high, low = split(value)
    value = dot(jnp.concatenate([high, low], axis=0), spread)
    value = value[:8] + value[8:]
    lane = iota((8, SEGS), 1)
    mine = (lane % SLOTS == iota((8, SEGS), 0)) & (lane // SLOTS < count_ref[0])
    out_ref[...] = jnp.sum(jnp.where(mine, value, 0.0), axis=0, keepdims=True)


VMEM = pl.BlockSpec(memory_space=pltpu.VMEM)
SMEM = pl.BlockSpec(memory_space=pltpu.SMEM)


def shape(*dims, kind=F32):
    return jax.ShapeDtypeStruct(dims, kind)


def call(kernel, inputs, outputs, scratch=(), megabytes=32):
    return pl.pallas_call(
        kernel,
        in_specs=list(inputs),
        out_specs=[VMEM] * len(outputs),
        out_shape=list(outputs),
        scratch_shapes=list(scratch),
        compiler_params=pltpu.CompilerParams(vmem_limit_bytes=megabytes << 20),
    )


def body(
    currents, plane_weights, cell_weights, brick_dest, brick_tile, brick_count, kern_across,
    kern_along, plane_mix,
):
    *sends, slots = call(
        route_kernel,
        [SMEM] + [VMEM] * 5,
        [shape(ROWS, CX)] * PEERS + [shape(8, BRICKS)],
        [pltpu.VMEM((SEGS, CX), F32)],
    )(
        brick_count,
        currents.reshape(1, SEGS),
        plane_weights,
        cell_weights,
        brick_dest.reshape(1, BRICKS),
        brick_tile.reshape(1, BRICKS),
    )
    swaps = [[(i, i ^ k) for i in range(PEERS)] for k in range(PEERS)]
    held = [sends[0]] + [lax.ppermute(sends[k], "sect", swaps[k]) for k in range(1, PEERS)]
    along_high, along_low, across_high, across_low = call(
        prep_kernel,
        [SMEM, SMEM],
        [shape(LEVELS + 1, 2 * CX, 2 * CX, kind=BF16)] * 2 + [shape(NY, DEPTH, kind=BF16)] * 2,
    )(kern_across, kern_along)
    *fields, to_right, to_left = call(
        charge_kernel,
        [VMEM] * 4,
        [shape(PLANES, NY, CX)]
        + [shape(PLANES * HEIGHTS[level], CX) for level in range(1, LEVELS + 1)]
        + [shape(NY, CX)] * 2,
        [
            pltpu.VMEM((TILES, PEERS * CX), BF16),
            pltpu.VMEM((PEERS * CX, 2 * PLANES * CX), BF16),
            pltpu.VMEM((PLANES * NY, CX), F32),
        ],
    )(*held)
    axes = ("strip", "sect")
    devices = lax.axis_size(axes)
    up = [(i, i + 1) for i in range(devices - 1)]
    down = [(i + 1, i) for i in range(devices - 1)]
    from_left = lax.ppermute(to_right, axes, up)
    from_right = lax.ppermute(to_left, axes, down)
    grid, *samples = call(
        field_kernel,
        [SMEM] + [VMEM] * 15,
        [shape(PLANES, NY, CX)] + [shape(8, CX)] * PEERS,
        [
            pltpu.VMEM((PLANES, NY, 2 * CX), F32),
            pltpu.VMEM((DEPTH, PLANES * CX), BF16),
            pltpu.VMEM((DEPTH, PLANES * CX), BF16),
            pltpu.VMEM((TILES, 2 * PLANES * CX), BF16),
            pltpu.VMEM((CAP, PLANES * CX), F32),
        ],
        megabytes=56,
    )(
        plane_mix, *fields, from_left, from_right, along_high, along_low, across_high, across_low,
        *held,
    )
    back = [samples[0]] + [lax.ppermute(samples[k], "sect", swaps[k]) for k in range(1, PEERS)]
    (segments,) = call(
        pick_kernel, [SMEM] + [VMEM] * 5, [shape(1, SEGS)]
    )(brick_count, slots, *back)
    return grid, segments.reshape(SEGS)


def solution(mesh):
    flat = ("strip", "sect")
    placed = (
        P(flat), P(None, flat), P(flat, None), P(flat, None), P(flat), P(flat), P(), P(), P(),
    )
    return jax.shard_map(
        body,
        mesh=mesh,
        in_specs=placed,
        out_specs=(P(None, None, flat), P(flat)),
        check_vma=False,
    )
```

time: 402 us -> 75 us (0.19)
  the two profiles are of different devices: /device:TPU:24 before, /device:TPU:0 now
where the time goes in v1:
time: 75 us; the launch traced here: 74.5 us
  Pallas kernels  34.3 us (46%)
  local copies, waits for them, and re-layouts  14.6 us (19%)
  waiting for transfers between devices  13.6 us (18%)
  starting transfers between devices  10.6 us (14%)
  between operations  1.42 us (2%)
    pallas_call x1, Pallas kernels, body(): call(field_kernel, [SMEM] + [VMEM] * 15, [shape(PLANES, NY, CX)] + [shape...  19.5 us
    unnamed x46, local copies, waits for them, and re-layouts  14.6 us
    ppermute x3, waiting for transfers between devices, body(): lax.ppermute(sends[k], 'sect', swaps[k])  10.4 us
    pallas_call x1, Pallas kernels, body(): call(charge_kernel, [VMEM] * 4, [shape(PLANES, NY, CX)] + [shape(PLANES *...  9.08 us
    ppermute x3, starting transfers between devices, body(): lax.ppermute(samples[k], 'sect', swaps[k])  3.95 us
    pallas_call x1, Pallas kernels, body(): call(prep_kernel, [SMEM, SMEM], [shape(LEVELS + 1, 2 * CX, 2 * CX, kind=B...  3.95 us
    ppermute x3, starting transfers between devices, body(): lax.ppermute(sends[k], 'sect', swaps[k])  3.18 us
    ppermute x3, waiting for transfers between devices, body(): lax.ppermute(samples[k], 'sect', swaps[k])  3.16 us
  transfers between devices with their start and end apart: 8, of which 4 were waited for; matrix products, arithmetic and copies ran while one was open for 0% of the time, Pallas kernels for 5%

profile of v1, /device:TPU:0, one launch (start us, length us, event | category | flops | bytes accessed | tf_op | source)
XLA Modules:
  0.0 74.5 jit_solution(6524276808859424615)
XLA Ops:
  1.3 0.0 copy-start.10
  1.3 1.0 %copy-done.10 = f32[1024,128]{1,0:T(8,128)S(1)} copy-done((f32[1024,128]{1,0:T(8,128)S(1)}, f32[1024,128]{1,0:T(8,128)}, u32[]{:S(2)}) %copy-start.10) | copy-done | bytes 524312
  2.3 0.8 %copy-done.14 = f32[8,1024]{1,0:T(8,128)S(1)} copy-done((f32[8,1024]{1,0:T(8,128)S(1)}, f32[8,1024]{1,0:T(8,128)}, u32[]{:S(2)}) %copy-start.14) | copy-done | bytes 32792
  3.1 0.7 copy-done.17
  3.8 0.7 copy-done.19
  4.4 0.7 copy-done.20
  5.1 0.8 %shard_map.104 = (f32[432,128]{1,0:T(8,128)S(1)}, f32[432,128]{1,0:T(8,128)S(1)}, f32[432,128]{1,0:T(8,128)S(1)}, f32[432,128]{1,0:T(8,128)S(1)}, f32[8,256]{1,0:T(8,128)S(1)}) custom-call(s32[1]{0:T(128)S(6)} %copy.11.count_ref, f32[1,1024]{1,0:T(1,128)S(1)} %bitcast.4, f32[8,1024]{1,0:T(8,128)S(1)} %copy-done.14, f32[1024,128]{1,0:T(8,128)S(1)} %copy-done.10, ...), custom_call_target="tpu_custom_call" | custom-call | tf_op jit(solution)/shard_map/pallas_call | solution.py:347
  6.0 0.0 copy-start.3
  6.0 0.5 collective-permute-start
  6.5 2.6 %collective-permute-start.1 = (f32[432,128]{1,0:T(8,128)S(1)}, f32[432,128]{1,0:T(8,128)S(1)}, u32[]{:S(2)}, u32[]{:S(2)}) collective-permute-start(f32[432,128]{1,0:T(8,128)S(1)} %get-tuple-element.25), channel_id=1, source_target_pairs={{0,2},{1,3},{2,0},{3,1},{4,6},{5,7},{6,4},{7,5},{8,10},{9,11},{10,... | collective-permute-start | bytes 663560 | tf_op jit(solution)/shard_map/ppermute | solution.py:361
  9.1 0.1 collective-permute-start.2
  9.2 0.0 collective-permute-done.r1
  9.2 6.2 %collective-permute-done.1.r2 = f32[432,128]{1,0:T(8,128)S(1)} collective-permute-done((f32[432,128]{1,0:T(8,128)S(1)}, f32[432,128]{1,0:T(8,128)S(1)}, u32[]{:S(2)}, u32[]{:S(2)}) %collective-permute-start.1) | collective-permute-done | bytes 221216 | tf_op jit(solution)/shard_map/ppermute | solution.py:361
  15.4 4.2 %collective-permute-done.2.r3 = f32[432,128]{1,0:T(8,128)S(1)} collective-permute-done((f32[432,128]{1,0:T(8,128)S(1)}, f32[432,128]{1,0:T(8,128)S(1)}, u32[]{:S(2)}, u32[]{:S(2)}) %collective-permute-start.2) | collective-permute-done | bytes 221216 | tf_op jit(solution)/shard_map/ppermute | solution.py:361
  19.6 9.1 %shard_map.105 = (f32[8,384,128]{2,1,0:T(8,128)S(1)}, f32[1536,128]{1,0:T(8,128)S(1)}, f32[768,128]{1,0:T(8,128)S(1)}, f32[384,128]{1,0:T(8,128)S(1)}, f32[192,1...) custom-call(f32[432,128]{1,0:T(8,128)S(1)} %get-tuple-element.23.r0, ...), custom_call_target="tpu_custom_call" | custom-call | tf_op jit(solution)/shard_map/pallas_call | solution.py:367
  28.7 0.0 copy-start
  28.7 1.2 %copy-done = f32[8,384,128]{2,1,0:T(8,128)} copy-done((f32[8,384,128]{2,1,0:T(8,128)}, f32[8,384,128]{2,1,0:T(8,128)S(1)}, u32[]{:S(2)}) %copy-start) | copy-done | bytes 1572888
  29.9 0.9 %copy-done.7 = f32[1536,128]{1,0:T(8,128)} copy-done((f32[1536,128]{1,0:T(8,128)}, f32[1536,128]{1,0:T(8,128)S(1)}, u32[]{:S(2)}) %copy-start.7) | copy-done | bytes 786456
  30.8 0.8 %copy-done.11 = f32[768,128]{1,0:T(8,128)} copy-done((f32[768,128]{1,0:T(8,128)}, f32[768,128]{1,0:T(8,128)S(1)}, u32[]{:S(2)}) %copy-start.11) | copy-done | bytes 393240
  31.5 0.7 copy-done.12
  32.2 0.6 copy-done.13
  32.8 2.0 %collective-permute-start.3 = (f32[384,128]{1,0:T(8,128)S(1)}, f32[384,128]{1,0:T(8,128)S(1)}, u32[]{:S(2)}, u32[]{:S(2)}) collective-permute-start(f32[384,128]{1,0:T(8,128)S(1)} %get-tuple-element.32), channel_id=1, source_target_pairs={{0,1},{1,2},{2,3},{3,4},{4,5},{5,6},{6,7},{7,8},{8,9},{9,10},{10,1... | collective-permute-start | bytes 589832 | tf_op jit(solution)/shard_map/ppermute | solution.py:383
  34.9 1.5 %collective-permute-start.4 = (f32[384,128]{1,0:T(8,128)S(1)}, f32[384,128]{1,0:T(8,128)S(1)}, u32[]{:S(2)}, u32[]{:S(2)}) collective-permute-start(f32[384,128]{1,0:T(8,128)S(1)} %get-tuple-element.33), channel_id=1, source_target_pairs={{1,0},{2,1},{3,2},{4,3},{5,4},{6,5},{7,6},{8,7},{9,8},{10,9},{11,1... | collective-permute-start | bytes 589832 | tf_op jit(solution)/shard_map/ppermute | solution.py:384
  36.4 0.0 copy-start.15
  36.4 0.7 copy-done.15
  37.0 0.7 copy-done.16
  37.7 3.9 %shard_map.106 = (bf16[5,256,256]{2,1,0:T(8,128)(2,1)S(1)}, bf16[5,256,256]{2,1,0:T(8,128)(2,1)S(1)}, bf16[384,1536]{1,0:T(8,128)(2,1)S(1)}, bf16[384,1536]{1,0:T(8,128)(2,1)S(1)}) custom-call(f32[5,2,17]{2,1,0:T(2,128)S(1)} %copy-done.15, f32[5,2,17]{2,1,0:T(2,128)S(1)} %copy-done.16), custom_call_target="tpu_custom_call" | custom-call | tf_op jit(solution)/shard_map/pallas_call | solution.py:362
  41.7 0.0 copy-start.1
  41.7 1.0 %copy-done.1 = bf16[384,1536]{1,0:T(8,128)(2,1)} copy-done((bf16[384,1536]{1,0:T(8,128)(2,1)}, bf16[384,1536]{1,0:T(8,128)(2,1)S(1)}, u32[]{:S(2)}) %copy-start.1) | copy-done | bytes 1179672
  42.7 1.0 %copy-done.2 = bf16[384,1536]{1,0:T(8,128)(2,1)} copy-done((bf16[384,1536]{1,0:T(8,128)(2,1)}, bf16[384,1536]{1,0:T(8,128)(2,1)S(1)}, u32[]{:S(2)}) %copy-start.2) | copy-done | bytes 1179672
  43.8 0.9 %copy-done.8 = bf16[5,256,256]{2,1,0:T(8,128)(2,1)} copy-done((bf16[5,256,256]{2,1,0:T(8,128)(2,1)}, bf16[5,256,256]{2,1,0:T(8,128)(2,1)S(1)}, u32[]{:S(2)}) %copy-start.8) | copy-done | bytes 655384
  44.7 0.9 %copy-done.9 = bf16[5,256,256]{2,1,0:T(8,128)(2,1)} copy-done((bf16[5,256,256]{2,1,0:T(8,128)(2,1)}, bf16[5,256,256]{2,1,0:T(8,128)(2,1)S(1)}, u32[]{:S(2)}) %copy-start.9) | copy-done | bytes 655384
  45.5 0.0 collective-permute-done.3.from_left
  45.5 0.0 collective-permute-done.4.from_right
  45.5 0.0 copy-start.22
  45.5 0.0 copy-done.3
  45.5 0.0 copy-done.4
  45.6 0.6 copy-done.21
  46.2 0.1 copy-done.22
  46.3 19.5 %shard_map.107 = (f32[8,384,128]{2,1,0:T(8,128)}, f32[8,128]{1,0:T(8,128)}, f32[8,128]{1,0:T(8,128)}, f32[8,128]{1,0:T(8,128)}, f32[8,128]{1,0:T(8,128)}) custom-call(f32[5,2,8,8]{3,2,1,0:T(8,128)} %mix_ref.1, f32[8,384,128]{2,1,0:T(8,128)} %copy-done, f32[1536,128]{1,0:T(8,128)} %copy-done.7, f32[768,128]{1,0:T(8,128)} %copy-done.11, ...), custom_call_target="tpu_custom_call" | custom-call | tf_op jit(solution)/shard_map/pallas_call | solution.py:385
  65.8 2.2 %collective-permute-start.5 = (f32[8,128]{1,0:T(8,128)}, f32[8,128]{1,0:T(8,128)S(1)}, u32[]{:S(2)}, u32[]{:S(2)}) collective-permute-start(f32[8,128]{1,0:T(8,128)} %get-tuple-element.41), channel_id=1, source_target_pairs={{0,1},{1,0},{2,3},{3,2},{4,5},{5,4},{6,7},{7,6},{8,9},{9,8},{10,11... | collective-permute-start | bytes 12296 | tf_op jit(solution)/shard_map/ppermute | solution.py:401
  68.0 1.7 %collective-permute-start.6 = (f32[8,128]{1,0:T(8,128)}, f32[8,128]{1,0:T(8,128)S(1)}, u32[]{:S(2)}, u32[]{:S(2)}) collective-permute-start(f32[8,128]{1,0:T(8,128)} %get-tuple-element.42), channel_id=1, source_target_pairs={{0,2},{1,3},{2,0},{3,1},{4,6},{5,7},{6,4},{7,5},{8,10},{9,11},{10,... | collective-permute-start | bytes 12296 | tf_op jit(solution)/shard_map/ppermute | solution.py:401
  69.7 0.1 collective-permute-start.7
  69.7 0.0 collective-permute-done.5.b1
  69.7 2.1 %collective-permute-done.6.b2 = f32[8,128]{1,0:T(8,128)S(1)} collective-permute-done((f32[8,128]{1,0:T(8,128)}, f32[8,128]{1,0:T(8,128)S(1)}, u32[]{:S(2)}, u32[]{:S(2)}) %collective-permute-start.6) | collective-permute-done | bytes 4128 | tf_op jit(solution)/shard_map/ppermute | solution.py:401
  71.8 1.1 %collective-permute-done.7.b3 = f32[8,128]{1,0:T(8,128)S(1)} collective-permute-done((f32[8,128]{1,0:T(8,128)}, f32[8,128]{1,0:T(8,128)S(1)}, u32[]{:S(2)}, u32[]{:S(2)}) %collective-permute-start.7) | collective-permute-done | bytes 4128 | tf_op jit(solution)/shard_map/ppermute | solution.py:401
  72.9 0.7 copy-done.18
  73.6 1.0 %shard_map.108 = f32[1,1024]{1,0:T(1,128)} custom-call(s32[1]{0:T(128)S(6)} %copy.11.count_ref, f32[8,256]{1,0:T(8,128)S(1)} %get-tuple-element.39.slot_ref, f32[8,128]{1,0:T(8,128)S(1)} %copy-done.18, f32[8,128]{1,0:T(8,128)S(1)} %collective-permute-done.5.b1, f32[8,128]{1,0:T(8,128)S(1)} %collective-permute-done.6.b2, f32[8,128]{1,0:T(8,128)S(1)} %collective-permute-done.7.b3), custom_call_target="tpu_custom_call" | custom-call | tf_op jit(solution)/shard_map/pallas_call | solution.py:402
  (19 shorter events, 0.0 us)
Async XLA Ops:
  1.3 1.0 %copy-start.10 = (f32[1024,128]{1,0:T(8,128)S(1)}, f32[1024,128]{1,0:T(8,128)}, u32[]{:S(2)}) copy-start(f32[1024,128]{1,0:T(8,128)} %cells_ref.1) | copy-start | bytes 1572868
  2.3 0.8 %copy-start.14 = (f32[8,1024]{1,0:T(8,128)S(1)}, f32[8,1024]{1,0:T(8,128)}, u32[]{:S(2)}) copy-start(f32[8,1024]{1,0:T(8,128)} %planes_ref.1) | copy-start | bytes 98308
  3.1 0.7 copy-start.17
  3.8 0.7 copy-start.19
  4.4 0.7 copy-start.20
  6.0 39.6 %copy-start.3 = (f32[432,128]{1,0:T(8,128)}, f32[432,128]{1,0:T(8,128)S(1)}, u32[]{:S(2)}) copy-start(f32[432,128]{1,0:T(8,128)S(1)} %get-tuple-element.23.r0) | copy-start | bytes 663556
  6.0 3.2 %collective-permute-start = (f32[432,128]{1,0:T(8,128)S(1)}, f32[432,128]{1,0:T(8,128)S(1)}, u32[]{:S(2)}, u32[]{:S(2)}) collective-permute-start(f32[432,128]{1,0:T(8,128)S(1)} %get-tuple-element.24), channel_id=1, source_target_pairs={{0,1},{1,0},{2,3},{3,2},{4,5},{5,4},{6,7},{7,6},{8,9},{9,8},{10,11... | collective-permute-start | bytes 663560 | tf_op jit(solution)/shard_map/ppermute | solution.py:361
  6.5 8.9 %collective-permute-start.1 = (f32[432,128]{1,0:T(8,128)S(1)}, f32[432,128]{1,0:T(8,128)S(1)}, u32[]{:S(2)}, u32[]{:S(2)}) collective-permute-start(f32[432,128]{1,0:T(8,128)S(1)} %get-tuple-element.25), channel_id=1, source_target_pairs={{0,2},{1,3},{2,0},{3,1},{4,6},{5,7},{6,4},{7,5},{8,10},{9,11},{10,... | collective-permute-start | bytes 663560 | tf_op jit(solution)/shard_map/ppermute | solution.py:361
  9.1 10.5 %collective-permute-start.2 = (f32[432,128]{1,0:T(8,128)S(1)}, f32[432,128]{1,0:T(8,128)S(1)}, u32[]{:S(2)}, u32[]{:S(2)}) collective-permute-start(f32[432,128]{1,0:T(8,128)S(1)} %get-tuple-element.26), channel_id=1, source_target_pairs={{0,3},{1,2},{2,1},{3,0},{4,7},{5,6},{6,5},{7,4},{8,11},{9,10},{10,... | collective-permute-start | bytes 663560 | tf_op jit(solution)/shard_map/ppermute | solution.py:361
  9.2 36.4 %copy-start.4 = (f32[432,128]{1,0:T(8,128)}, f32[432,128]{1,0:T(8,128)S(1)}, u32[]{:S(2)}) copy-start(f32[432,128]{1,0:T(8,128)S(1)} %collective-permute-done.r1) | copy-start | bytes 663556
  15.4 30.2 %copy-start.5 = (f32[432,128]{1,0:T(8,128)}, f32[432,128]{1,0:T(8,128)S(1)}, u32[]{:S(2)}) copy-start(f32[432,128]{1,0:T(8,128)S(1)} %collective-permute-done.1.r2) | copy-start | bytes 663556
  19.6 26.0 %copy-start.6 = (f32[432,128]{1,0:T(8,128)}, f32[432,128]{1,0:T(8,128)S(1)}, u32[]{:S(2)}) copy-start(f32[432,128]{1,0:T(8,128)S(1)} %collective-permute-done.2.r3) | copy-start | bytes 663556
  28.7 1.2 %copy-start = (f32[8,384,128]{2,1,0:T(8,128)}, f32[8,384,128]{2,1,0:T(8,128)S(1)}, u32[]{:S(2)}) copy-start(f32[8,384,128]{2,1,0:T(8,128)S(1)} %get-tuple-element.27.q0) | copy-start | bytes 4718596
  29.9 0.9 %copy-start.7 = (f32[1536,128]{1,0:T(8,128)}, f32[1536,128]{1,0:T(8,128)S(1)}, u32[]{:S(2)}) copy-start(f32[1536,128]{1,0:T(8,128)S(1)} %get-tuple-element.28.s1) | copy-start | bytes 2359300
  30.8 0.8 %copy-start.11 = (f32[768,128]{1,0:T(8,128)}, f32[768,128]{1,0:T(8,128)S(1)}, u32[]{:S(2)}) copy-start(f32[768,128]{1,0:T(8,128)S(1)} %get-tuple-element.29.s2) | copy-start | bytes 1179652
  31.5 0.7 copy-start.12
  32.2 0.6 copy-start.13
  32.8 12.7 %collective-permute-start.3 = (f32[384,128]{1,0:T(8,128)S(1)}, f32[384,128]{1,0:T(8,128)S(1)}, u32[]{:S(2)}, u32[]{:S(2)}) collective-permute-start(f32[384,128]{1,0:T(8,128)S(1)} %get-tuple-element.32), channel_id=1, source_target_pairs={{0,1},{1,2},{2,3},{3,4},{4,5},{5,6},{6,7},{7,8},{8,9},{9,10},{10,1... | collective-permute-start | bytes 589832 | tf_op jit(solution)/shard_map/ppermute | solution.py:383
  34.9 10.7 %collective-permute-start.4 = (f32[384,128]{1,0:T(8,128)S(1)}, f32[384,128]{1,0:T(8,128)S(1)}, u32[]{:S(2)}, u32[]{:S(2)}) collective-permute-start(f32[384,128]{1,0:T(8,128)S(1)} %get-tuple-element.33), channel_id=1, source_target_pairs={{1,0},{2,1},{3,2},{4,3},{5,4},{6,5},{7,6},{8,7},{9,8},{10,9},{11,1... | collective-permute-start | bytes 589832 | tf_op jit(solution)/shard_map/ppermute | solution.py:384
  36.4 0.7 copy-start.15
  37.0 0.7 copy-start.16
  41.7 1.0 %copy-start.1 = (bf16[384,1536]{1,0:T(8,128)(2,1)}, bf16[384,1536]{1,0:T(8,128)(2,1)S(1)}, u32[]{:S(2)}) copy-start(bf16[384,1536]{1,0:T(8,128)(2,1)S(1)} %get-tuple-element.36.across_high) | copy-start | bytes 3538948
  42.7 1.0 %copy-start.2 = (bf16[384,1536]{1,0:T(8,128)(2,1)}, bf16[384,1536]{1,0:T(8,128)(2,1)S(1)}, u32[]{:S(2)}) copy-start(bf16[384,1536]{1,0:T(8,128)(2,1)S(1)} %get-tuple-element.37.across_low) | copy-start | bytes 3538948
  43.8 0.9 %copy-start.8 = (bf16[5,256,256]{2,1,0:T(8,128)(2,1)}, bf16[5,256,256]{2,1,0:T(8,128)(2,1)S(1)}, u32[]{:S(2)}) copy-start(bf16[5,256,256]{2,1,0:T(8,128)(2,1)S(1)} %get-tuple-element.34.along_high) | copy-start | bytes 1966084
  44.6 0.9 %copy-start.9 = (bf16[5,256,256]{2,1,0:T(8,128)(2,1)}, bf16[5,256,256]{2,1,0:T(8,128)(2,1)S(1)}, u32[]{:S(2)}) copy-start(bf16[5,256,256]{2,1,0:T(8,128)(2,1)S(1)} %get-tuple-element.35.along_low) | copy-start | bytes 1966084
  45.5 0.7 copy-start.21
  45.5 0.8 %copy-start.22 = (f32[384,128]{1,0:T(8,128)}, f32[384,128]{1,0:T(8,128)S(1)}, u32[]{:S(2)}) copy-start(f32[384,128]{1,0:T(8,128)S(1)} %collective-permute-done.4.from_right) | copy-start | bytes 589828
  65.8 4.0 %collective-permute-start.5 = (f32[8,128]{1,0:T(8,128)}, f32[8,128]{1,0:T(8,128)S(1)}, u32[]{:S(2)}, u32[]{:S(2)}) collective-permute-start(f32[8,128]{1,0:T(8,128)} %get-tuple-element.41), channel_id=1, source_target_pairs={{0,1},{1,0},{2,3},{3,2},{4,5},{5,4},{6,7},{7,6},{8,9},{9,8},{10,11... | collective-permute-start | bytes 12296 | tf_op jit(solution)/shard_map/ppermute | solution.py:401
  68.0 3.8 %collective-permute-start.6 = (f32[8,128]{1,0:T(8,128)}, f32[8,128]{1,0:T(8,128)S(1)}, u32[]{:S(2)}, u32[]{:S(2)}) collective-permute-start(f32[8,128]{1,0:T(8,128)} %get-tuple-element.42), channel_id=1, source_target_pairs={{0,2},{1,3},{2,0},{3,1},{4,6},{5,7},{6,4},{7,5},{8,10},{9,11},{10,... | collective-permute-start | bytes 12296 | tf_op jit(solution)/shard_map/ppermute | solution.py:401
  69.7 3.2 %collective-permute-start.7 = (f32[8,128]{1,0:T(8,128)}, f32[8,128]{1,0:T(8,128)S(1)}, u32[]{:S(2)}, u32[]{:S(2)}) collective-permute-start(f32[8,128]{1,0:T(8,128)} %get-tuple-element.43), channel_id=1, source_target_pairs={{0,3},{1,2},{2,1},{3,0},{4,7},{5,6},{6,5},{7,4},{8,11},{9,10},{10,... | collective-permute-start | bytes 12296 | tf_op jit(solution)/shard_map/ppermute | solution.py:401
  72.9 0.7 copy-start.18

commit v2 on v1

v2 whole, which is shorter than its diff:
```python
import jax
import jax.numpy as jnp
from jax import lax
from jax.experimental import pallas as pl
from jax.experimental.pallas import tpu as pltpu
from jax.sharding import PartitionSpec as P

NY = 384
CX = 128
LEVELS = 4
TILES = 384
PLANES = 8
TAPS = 17
REACH = TAPS // 2
SLOTS = 4
BRICKS = 256
CAP = 96
PEERS = 4
CELLS = SLOTS * CAP
PACK = CAP // 2
ROWS = CELLS + PACK
SEGS = BRICKS * SLOTS
BAND = NY // 8
HALF = PLANES * CX
HEIGHTS = tuple(NY >> level for level in range(LEVELS + 1))
WIDTHS = tuple(CX >> level for level in range(LEVELS + 1))
STEP = (384, 192, 96, 48, 32)
ROW_OF = (0, 384, 576, 672, 720)
ALL_ROWS = 752
K_OF = (0, 768, 1152, 1344, 1440)
ALL_K = 1504
RIM_ROW = (0, 0, 192, 288, 384)
RIM_ROWS = NY + HEIGHTS[LEVELS]
F32 = jnp.float32
BF16 = jnp.bfloat16


def split(value):
    high = value.astype(BF16)
    return high, (value - high.astype(F32)).astype(BF16)


def dot(left, right):
    return jnp.dot(left, right, preferred_element_type=F32)


def iota(shape, dim):
    return lax.broadcasted_iota(jnp.int32, shape, dim)


def flags(condition):
    return condition.astype(F32).astype(BF16)


def turn(value, amount):
    amount = amount % CX
    return pltpu.roll(value, amount, 1) if amount else value


def swap_groups(bands):
    group = iota((1, CX), 1) // 16
    for bit in range(3):
        step = 1 << bit
        upper = ((group >> bit) & 1) == 1
        fresh = []
        for i in range(8):
            other = bands[i ^ step]
            if i & step:
                fresh.append(jnp.where(upper, bands[i], turn(other, -16 * step)))
            else:
                fresh.append(jnp.where(upper, turn(other, 16 * step), bands[i]))
        bands = fresh
    return bands


def route_kernel(
    count_ref, currents_hbm, planes_hbm, cells_hbm, dest_hbm, tile_hbm, *refs
):
    outs, slot_ref = refs[:PEERS], refs[PEERS]
    feature, currents_ref, planes_ref, cells_ref, dest_ref, tile_ref, sems = refs[PEERS + 1 :]
    pairs = (
        (dest_hbm, dest_ref), (tile_hbm, tile_ref), (currents_hbm, currents_ref),
        (planes_hbm, planes_ref), (cells_hbm, cells_ref),
    )
    copies = [pltpu.make_async_copy(a, b, sems.at[i]) for i, (a, b) in enumerate(pairs)]
    for copy in copies:
        copy.start()
    for copy in copies[:4]:
        copy.wait()
    me = lax.axis_index("sect")
    away = dest_ref[...] ^ me
    onehot = (iota((16, BRICKS), 0) == away).astype(F32)
    before = flags(iota((BRICKS, BRICKS), 0) < iota((BRICKS, BRICKS), 1))
    earlier = dot(onehot.astype(BF16), before)
    base = (iota((16, BRICKS), 0) * CAP).astype(F32)
    slot = jnp.sum(onehot * (earlier + base), axis=0, keepdims=True)
    slot_ref[...] = jnp.broadcast_to(slot, slot_ref.shape)
    choose = flags(iota((PEERS * CAP, BRICKS), 0).astype(F32) == slot)
    alive = (iota((1, SEGS), 1) // SLOTS < count_ref[0]).astype(F32)
    currents = currents_ref[...] * alive
    lines = jnp.concatenate(
        [planes_ref[...], currents, jnp.zeros((CX - PLANES - 1, SEGS), F32)], axis=0
    )
    for part in range(SEGS // CX):
        feature[part * CX : (part + 1) * CX, :] = lines[:, part * CX : (part + 1) * CX].T
    meta = jnp.zeros((BRICKS, CX), F32)
    for s in range(SLOTS):
        meta = meta + turn(feature[pl.ds(s, BRICKS, stride=SLOTS), :], 16 * s)
    tile = tile_ref[...]
    tile = (tile & 7) * BAND + (tile >> 3)
    tiles = jnp.concatenate([tile.astype(F32), jnp.zeros((CX - 1, BRICKS), F32)], axis=0)
    tiles = jnp.concatenate([tiles[:, :CX].T, tiles[:, CX:].T], axis=0)
    meta = meta + turn(tiles, 9)
    both = dot(choose, jnp.concatenate(split(meta), axis=1))
    both = both[:, :CX] + both[:, CX:]
    for k in range(PEERS):
        lower = both[k * CAP : k * CAP + PACK]
        upper = both[k * CAP + PACK : (k + 1) * CAP]
        outs[k][CELLS:, :] = lower + turn(upper, CX // 2)
    copies[4].wait()
    for s in range(SLOTS):
        high, low = split(cells_ref[pl.ds(s, BRICKS, stride=SLOTS), :])
        moved = dot(choose, jnp.concatenate([high, low], axis=1))
        moved = moved[:, :CX] + moved[:, CX:]
        for k in range(PEERS):
            outs[k][s * CAP : (s + 1) * CAP, :] = moved[k * CAP : (k + 1) * CAP]


def height_of(place, level):
    if level == LEVELS:
        return place
    band = (place * 1366) >> 16
    return (place - band * BAND) * (8 >> level) + band


def rim_of(lane, level):
    if level == LEVELS:
        j, rest = lane >> 4, lane & 15
        return rest & 7, jnp.where(rest < 8, j - REACH, j + WIDTHS[level])
    spot = lane if level == 0 else lane ^ (CX // 2)
    log = level + 3
    rest = spot & ((8 << level) - 1)
    j, offset = rest >> level, rest & ((1 << level) - 1)
    first = spot < CX // 2
    block = jnp.where(first, spot >> log, (CX - 1 - spot) >> log)
    return (block << level) + offset, jnp.where(first, j + WIDTHS[level], j - REACH)


def prep_kernel(
    across_ref, along_ref, mix_ref, own_ref, own_low_ref, across_high, across_low, blend_high,
    blend_low, rim_high, rim_low
):
    exact = lax.Precision.HIGHEST
    for level in range(LEVELS + 1):
        scale = 0.25**level
        row = iota((CX, 1), 0)
        mark = jnp.where((row & ((1 << level) - 1)) == 0, row >> level, 4 * NY)
        lane_z, lane_place = rim_of(row, level)
        line_z, line_place = rim_of(iota((1, CX), 1), level)
        column = iota((CX, CX), 1) >> level
        shift = mark - column + REACH
        rim_shift = lane_place - column + REACH
        same = lane_place == line_place
        pick = (lane_z == iota((CX, 8), 1)).astype(F32)
        pick_t = (line_z == iota((8, CX), 0)).astype(F32)
        for r in range(2):
            part = slice(r * CX, (r + 1) * CX)
            taps = jnp.zeros((CX, CX), F32)
            rims = jnp.zeros((CX, CX), F32)
            for t in range(TAPS):
                tap = along_ref[level, r, t]
                taps = jnp.where(shift == t, tap, taps)
                rims = jnp.where(rim_shift == t, tap, rims)
            high, low = split(taps * scale)
            own_ref[level, :CX, part] = high
            own_ref[level, CX:, part] = high
            own_low_ref[level, :, part] = low
            high, low = split(rims * scale)
            for z in range(PLANES):
                mine = jnp.broadcast_to((lane_z == z).astype(F32), (CX, CX)).astype(BF16)
                rim_high[level, part, z * CX : (z + 1) * CX] = high * mine
                rim_low[level, part, z * CX : (z + 1) * CX] = low * mine
            mixes = lax.dot_general(
                pick, mix_ref[level, r], (((1,), (1,)), ((), ())), precision=exact,
                preferred_element_type=F32,
            )
            mixes = jnp.dot(mixes, pick_t, precision=exact, preferred_element_type=F32)
            high, low = split(jnp.where(same, mixes, 0.0))
            blend_high[level, :, part] = high
            blend_low[level, :, part] = low
        size, step = HEIGHTS[level], STEP[level]
        rows = slice(ROW_OF[level], ROW_OF[level] + size)
        mine = height_of(iota((size, 1), 0), level)
        for start in range(0, 2 * step, CX):
            lanes = min(CX, 2 * step - start)
            place = iota((1, lanes), 1) + start
            second = place >= step
            place = jnp.where(second, place - step, place)
            other = jnp.where(place < size, height_of(place, level), 4 * NY)
            shift = other - mine + REACH
            taps = jnp.zeros((size, lanes), F32)
            for t in range(TAPS):
                tap = jnp.where(second, across_ref[level, 1, t], across_ref[level, 0, t])
                taps = jnp.where(shift == t, tap, taps)
            high, low = split(taps)
            across_high[rows, start : start + lanes] = high
            across_low[rows, start : start + lanes] = low


def brick_kernel(ref, bricks, hot, match, weights):
    packed = ref[CELLS:, :]
    meta = jnp.concatenate([packed, turn(packed, CX // 2)], axis=0)
    cells = [ref[s * CAP : (s + 1) * CAP, :] for s in range(SLOTS)]
    totals = [None] * PLANES
    for s in range(SLOTS):
        current = meta[:, 16 * s + 8 : 16 * s + 9]
        for z in range(PLANES):
            piece = cells[s] * meta[:, 16 * s + z : 16 * s + z + 1]
            weights[s * PLANES + z] = piece
            piece = piece * current
            totals[z] = piece if s == 0 else totals[z] + piece
    for z in range(PLANES):
        high, low = split(totals[z])
        bricks[:CAP, z * CX : (z + 1) * CX] = high
        bricks[:CAP, HALF + z * CX : HALF + (z + 1) * CX] = low
    bricks[CAP:, :] = jnp.zeros((CX - CAP, 2 * HALF), BF16)
    whole = jnp.concatenate([meta, jnp.zeros((CX - CAP, CX), F32)], axis=0)
    names = jnp.where(iota((1, CX), 1) < CAP, whole.T[9:10, :], -1.0)
    hot[...] = flags(iota((TILES, CX), 0).astype(F32) == names)
    match[...] = flags(iota((CAP, TILES), 1).astype(F32) == meta[:, 9:10])


def charge_kernel(*refs):
    bricks, hots = refs[:PEERS], refs[PEERS : 2 * PEERS]
    q0, s1, s2, s3, s4, to_right, to_left = refs[2 * PEERS + 1 : -4]
    rims = refs[-4:]
    hot = jnp.concatenate([ref[...] for ref in hots], axis=1)
    lanes = iota((1, CX), 1)
    for pair in range(PLANES // 2):
        part = slice(pair * 2 * CX, (pair + 1) * 2 * CX)
        lower = slice(HALF + pair * 2 * CX, HALF + (pair + 1) * 2 * CX)
        found = dot(hot, jnp.concatenate([ref[:, part] for ref in bricks], axis=0)) + dot(
            hot, jnp.concatenate([ref[:, lower] for ref in bricks], axis=0)
        )
        for i in range(2):
            z = 2 * pair + i
            plane = found[:, i * CX : (i + 1) * CX]
            bands = swap_groups([plane[b * BAND : (b + 1) * BAND] for b in range(8)])
            level = 0
            while True:
                size, log = HEIGHTS[level], level + 3
                target = (q0, s1, s2, s3)[level]
                for b, band in enumerate(bands):
                    rows = slice(b * BAND, (b + 1) * BAND)
                    target[z, rows, :] = band
                    block, offset = z >> level, z & ((1 << level) - 1)
                    first = turn(band, (block << log) + offset)
                    last = turn(band, offset - (block << log)) if block else first
                    mine = (lanes & ((1 << level) - 1)) == offset
                    left = mine & ((lanes >> log) == block) & (lanes < CX // 2)
                    right = mine & (((CX - 1 - lanes) >> log) == block) & (lanes >= CX // 2)
                    held = rims[level][rows, :] if z else jnp.zeros((BAND, CX), F32)
                    held = jnp.where(left, first, jnp.where(right, last, held))
                    rims[level][rows, :] = held
                if level == 3:
                    break
                sums = [bands[2 * b] + bands[2 * b + 1] for b in range(len(bands) // 2)]
                bands = [value + turn(value, -(1 << level)) for value in sums]
                level += 1
    size = HEIGHTS[LEVELS]
    coarse = jnp.zeros((size, CX), F32)
    for z in range(PLANES):
        value = s3[z, pl.ds(0, size, stride=2), :] + s3[z, pl.ds(1, size, stride=2), :]
        value = value + turn(value, -8)
        s4[z] = value
        coarse = jnp.where((lanes & 15) == z, turn(value, z), coarse)
    to_right[NY:, :] = coarse
    to_left[NY:, :] = coarse
    to_right[RIM_ROW[3] + HEIGHTS[3] : NY, :] = rims[0][RIM_ROW[3] + HEIGHTS[3] : NY, :]
    to_left[RIM_ROW[3] + HEIGHTS[3] : NY, :] = rims[0][RIM_ROW[3] + HEIGHTS[3] : NY, :]
    for level in range(1, LEVELS):
        rows = slice(RIM_ROW[level], RIM_ROW[level] + HEIGHTS[level])
        other = turn(rims[level][...], CX // 2)
        to_right[rows, :] = jnp.where(lanes < CX // 2, other, rims[0][rows, :])
        to_left[rows, :] = jnp.where(lanes < CX // 2, rims[0][rows, :], other)


def inner_kernel(
    mix_ref, q0, s1, s2, s3, s4, own_ref, own_low_ref, across_high, across_low, out_ref, ranked,
    high_ref, low_ref
):
    for level, source in enumerate((q0, s1, s2, s3, s4)):
        size, step = HEIGHTS[level], STEP[level]
        for z in range(PLANES):
            high, low = split(source[z])
            ranked[z, :size, :] = dot(
                jnp.concatenate([high, low], axis=1), own_ref[level]
            ) + dot(high, own_low_ref[level])
        chunk = {384: 32, 192: 32, 96: 32, 48: 16, 24: 24}[size]

        def mixed(index, carry, level=level, chunk=chunk, step=step):
            start = index * chunk
            if not isinstance(start, int):
                start = pl.multiple_of(start, chunk)
            for r in range(2):
                parts = [
                    ranked[w, pl.ds(start, chunk), r * CX : (r + 1) * CX] for w in range(PLANES)
                ]
                for z in range(PLANES):
                    total = parts[0] * mix_ref[level, r, z, 0]
                    for w in range(1, PLANES):
                        total = total + parts[w] * mix_ref[level, r, z, w]
                    if chunk == 24:
                        total = jnp.concatenate([total, jnp.zeros((8, CX), F32)], axis=0)
                    high, low = split(total)
                    place = pl.ds(r * step + start, high.shape[0])
                    high_ref[place, z * CX : (z + 1) * CX] = high
                    low_ref[place, z * CX : (z + 1) * CX] = low
            return carry

        if size == chunk:
            mixed(0, 0)
        else:
            lax.fori_loop(0, size // chunk, mixed, 0)
        rows = slice(ROW_OF[level], ROW_OF[level] + size)
        heavy, light = across_high[rows, : 2 * step], across_low[rows, : 2 * step]
        for pair in range(PLANES // 2):
            part = slice(pair * 2 * CX, (pair + 1) * 2 * CX)
            high = high_ref[: 2 * step, part]
            out_ref[rows, part] = (
                dot(heavy, high) + dot(heavy, low_ref[: 2 * step, part]) + dot(light, high)
            )


def outer_kernel(*refs):
    inner, from_left, from_right, across_high, across_low = refs[:5]
    blend_high, blend_low, rim_high, rim_low = refs[5:9]
    matches, weights = refs[9 : 9 + PEERS], refs[9 + PEERS : 9 + 2 * PEERS]
    grid_ref = refs[9 + 2 * PEERS]
    outs = refs[10 + 2 * PEERS : 10 + 3 * PEERS]
    high_ref, low_ref, tiles, picked, doubled = refs[10 + 3 * PEERS :]
    lanes = iota((1, CX), 1)
    high_ref[...] = jnp.zeros((ALL_K, 2 * CX), BF16)
    low_ref[...] = jnp.zeros((ALL_K, 2 * CX), BF16)
    sums = []
    for level in range(LEVELS + 1):
        size, step = HEIGHTS[level], STEP[level]
        rows = slice(RIM_ROW[level], RIM_ROW[level] + size)
        if level == 0:
            rims = jnp.where(lanes < CX // 2, from_right[rows, :], from_left[rows, :])
        elif level < LEVELS:
            rims = jnp.where(lanes < CX // 2, from_left[rows, :], from_right[rows, :])
        else:
            rims = jnp.where((lanes & 15) < 8, from_left[rows, :], turn(from_right[rows, :], 8))
        high, low = split(rims)
        mixed = dot(high, blend_high[level]) + dot(low, blend_high[level])
        mixed = mixed + dot(high, blend_low[level])
        if size < step:
            mixed = jnp.concatenate([mixed, jnp.zeros((step - size, 2 * CX), F32)], axis=0)
        high, low = split(mixed)
        for r in range(2):
            part = slice(r * CX, (r + 1) * CX)
            place = slice(K_OF[level] + r * step, K_OF[level] + (r + 1) * step)
            high_ref[place, part] = high[:, part]
            low_ref[place, part] = low[:, part]
        rows = slice(ROW_OF[level], ROW_OF[level] + size)
        place = slice(K_OF[level], K_OF[level] + 2 * step)
        heavy, light = across_high[rows, : 2 * step], across_low[rows, : 2 * step]
        total = dot(heavy, high_ref[place, :]) + dot(heavy, low_ref[place, :])
        sums.append(split(total + dot(light, high_ref[place, :])))
    for pair in range(PLANES // 2):
        part = slice(pair * 2 * CX, (pair + 1) * 2 * CX)
        above = None
        for level in range(LEVELS, -1, -1):
            high, low = sums[level]
            heavy, light = rim_high[level, :, part], rim_low[level, :, part]
            value = dot(high, heavy) + dot(low, heavy) + dot(high, light)
            value = value + inner[ROW_OF[level] : ROW_OF[level] + HEIGHTS[level], part]
            if level == LEVELS:
                doubled[pl.ds(0, HEIGHTS[level], stride=2), :] = value[:, :CX]
                doubled[pl.ds(1, HEIGHTS[level], stride=2), :] = value[:, :CX]
                doubled[pl.ds(BAND, HEIGHTS[level], stride=2), :] = value[:, CX:]
                doubled[pl.ds(BAND + 1, HEIGHTS[level], stride=2), :] = value[:, CX:]
                above = [jnp.concatenate([doubled[:BAND, :], doubled[BAND:, :]], axis=1)]
                continue
            bands = 8 >> level
            fresh = []
            for b in range(bands):
                fresh.append(value[b * BAND : (b + 1) * BAND] + above[b * len(above) // bands])
            above = fresh
        for i in range(2):
            z = 2 * pair + i
            planes = [band[:, i * CX : (i + 1) * CX] for band in above]
            for b in range(8):
                grid_ref[z, pl.ds(b, BAND, stride=8), :] = planes[b]
            for b, band in enumerate(swap_groups(planes)):
                high, low = split(band)
                rows = slice(b * BAND, (b + 1) * BAND)
                tiles[rows, z * CX : (z + 1) * CX] = high
                tiles[rows, HALF + z * CX : HALF + (z + 1) * CX] = low
    for j in range(PEERS):
        match = matches[j][...]
        for pair in range(PLANES // 2):
            part = slice(pair * 2 * CX, (pair + 1) * 2 * CX)
            lower = slice(HALF + pair * 2 * CX, HALF + (pair + 1) * 2 * CX)
            picked[:, part] = dot(match, tiles[:, part]) + dot(match, tiles[:, lower])
        values = jnp.zeros((CAP, CX), F32)
        for s in range(SLOTS):
            total = picked[:, :CX] * weights[j][s * PLANES]
            for z in range(1, PLANES):
                total = total + picked[:, z * CX : (z + 1) * CX] * weights[j][s * PLANES + z]
            values = jnp.where(lanes == s, jnp.sum(total, axis=1, keepdims=True), values)
        values = jnp.concatenate([values, jnp.zeros((CX - CAP, CX), F32)], axis=0)
        outs[j][...] = values.T[:8, :]


def pick_kernel(count_ref, slot_ref, b0, b1, b2, b3, out_ref):
    slot = slot_ref[0:1, :]
    away = jnp.floor((slot + 0.5) * (1.0 / CAP))
    place = slot + away * (CX - CAP)
    match = (iota((PEERS * CX, BRICKS), 0).astype(F32) == place).astype(F32).astype(BF16)
    held = jnp.concatenate([b0[...], b1[...], b2[...], b3[...]], axis=1)
    high, low = split(held)
    value = dot(jnp.concatenate([high, low], axis=0), match)
    value = value[:8] + value[8:]
    spread = (iota((BRICKS, SEGS), 1) // SLOTS == iota((BRICKS, SEGS), 0)).astype(F32).astype(BF16)
    high, low = split(value)
    value = dot(jnp.concatenate([high, low], axis=0), spread)
    value = value[:8] + value[8:]
    lane = iota((8, SEGS), 1)
    mine = (lane % SLOTS == iota((8, SEGS), 0)) & (lane // SLOTS < count_ref[0])
    out_ref[...] = jnp.sum(jnp.where(mine, value, 0.0), axis=0, keepdims=True)


VMEM = pl.BlockSpec(memory_space=pltpu.VMEM)
SMEM = pl.BlockSpec(memory_space=pltpu.SMEM)
ANY = pl.BlockSpec(memory_space=pl.ANY)


def shape(*dims, kind=F32):
    return jax.ShapeDtypeStruct(dims, kind)


def call(kernel, inputs, outputs, scratch=(), megabytes=16):
    return pl.pallas_call(
        kernel,
        in_specs=list(inputs),
        out_specs=[VMEM] * len(outputs),
        out_shape=list(outputs),
        scratch_shapes=list(scratch),
        compiler_params=pltpu.CompilerParams(vmem_limit_bytes=megabytes << 20),
    )


def body(
    currents, plane_weights, cell_weights, brick_dest, brick_tile, brick_count, kern_across,
    kern_along, plane_mix,
):
    *sends, slots = call(
        route_kernel,
        [SMEM] + [ANY] * 5,
        [shape(ROWS, CX)] * PEERS + [shape(8, BRICKS)],
        [
            pltpu.VMEM((SEGS, CX), F32),
            pltpu.VMEM((1, SEGS), F32),
            pltpu.VMEM((PLANES, SEGS), F32),
            pltpu.VMEM((SEGS, CX), F32),
            pltpu.VMEM((1, BRICKS), jnp.int32),
            pltpu.VMEM((1, BRICKS), jnp.int32),
            pltpu.SemaphoreType.DMA((5,)),
        ],
    )(
        brick_count,
        currents.reshape(1, SEGS),
        plane_weights,
        cell_weights,
        brick_dest.reshape(1, BRICKS),
        brick_tile.reshape(1, BRICKS),
    )
    swaps = [[(i, i ^ k) for i in range(PEERS)] for k in range(PEERS)]
    held = [sends[0]] + [lax.ppermute(sends[k], "sect", swaps[k]) for k in range(1, PEERS)]
    prepared = call(
        prep_kernel,
        [SMEM, SMEM, VMEM],
        [
            shape(LEVELS + 1, 2 * CX, 2 * CX, kind=BF16),
            shape(LEVELS + 1, CX, 2 * CX, kind=BF16),
            shape(ALL_ROWS, 2 * NY, kind=BF16),
            shape(ALL_ROWS, 2 * NY, kind=BF16),
            shape(LEVELS + 1, CX, 2 * CX, kind=BF16),
            shape(LEVELS + 1, CX, 2 * CX, kind=BF16),
            shape(LEVELS + 1, 2 * CX, HALF, kind=BF16),
            shape(LEVELS + 1, 2 * CX, HALF, kind=BF16),
        ],
    )(kern_across, kern_along, plane_mix)
    own, own_low, across_high, across_low, *outer = prepared
    parts = [
        call(
            brick_kernel,
            [VMEM],
            [
                shape(CX, 2 * HALF, kind=BF16),
                shape(TILES, CX, kind=BF16),
                shape(CAP, TILES, kind=BF16),
                shape(SLOTS * PLANES, CAP, CX),
            ],
        )(value)
        for value in held
    ]
    bricks, hots, matches, weights = zip(*parts)
    *fields, to_right, to_left = call(
        charge_kernel,
        [VMEM] * 8 + [ANY],
        [shape(PLANES, size, CX) for size in HEIGHTS] + [shape(RIM_ROWS, CX)] * 2,
        [pltpu.VMEM((size, CX), F32) for size in HEIGHTS[:LEVELS]],
    )(*bricks, *hots, own)
    axes = ("strip", "sect")
    devices = lax.axis_size(axes)
    up = [(i, i + 1) for i in range(devices - 1)]
    down = [(i + 1, i) for i in range(devices - 1)]
    from_left = lax.ppermute(to_right, axes, up)
    from_right = lax.ppermute(to_left, axes, down)
    (inner,) = call(
        inner_kernel,
        [SMEM] + [VMEM] * 9,
        [shape(ALL_ROWS, HALF)],
        [
            pltpu.VMEM((PLANES, NY, 2 * CX), F32),
            pltpu.VMEM((2 * NY, HALF), BF16),
            pltpu.VMEM((2 * NY, HALF), BF16),
        ],
    )(plane_mix, *fields, own, own_low, across_high, across_low)
    grid, *samples = call(
        outer_kernel,
        [VMEM] * (9 + 2 * PEERS),
        [shape(PLANES, NY, CX)] + [shape(8, CX)] * PEERS,
        [
            pltpu.VMEM((ALL_K, 2 * CX), BF16),
            pltpu.VMEM((ALL_K, 2 * CX), BF16),
            pltpu.VMEM((TILES, 2 * HALF), BF16),
            pltpu.VMEM((CAP, HALF), F32),
            pltpu.VMEM((2 * BAND, CX), F32),
        ],
    )(inner, from_left, from_right, across_high, across_low, *outer, *matches, *weights)
    back = [samples[0]] + [lax.ppermute(samples[k], "sect", swaps[k]) for k in range(1, PEERS)]
    (segments,) = call(
        pick_kernel, [SMEM] + [VMEM] * 5, [shape(1, SEGS)]
    )(brick_count, slots, *back)
    return grid, segments.reshape(SEGS)


def solution(mesh):
    flat = ("strip", "sect")
    placed = (
        P(flat), P(None, flat), P(flat, None), P(flat, None), P(flat), P(flat), P(), P(), P(),
    )
    return jax.shard_map(
        body,
        mesh=mesh,
        in_specs=placed,
        out_specs=(P(None, None, flat), P(flat)),
        check_vma=False,
    )
```

time: 75 us -> 56.6 us (0.75)
  waiting for transfers between devices: 13.6 us -> 2.91 us
  local copies, waits for them, and re-layouts: 14.6 us -> 5.99 us
    ppermute x3, waiting for transfers between devices: 10.4 us -> 0.02 us  [body(): lax.ppermute(sends[k], 'sect', swaps[k])]
    unnamed x46 -> x16, local copies, waits for them, and re-layouts: 14.6 us -> 5.99 us
    pallas_call x4 -> x9, Pallas kernels: 33.3 us -> 33.7 us  [the longest x1 11.3 us: body(): call(inner_kernel, [SMEM] + [VMEM] * 9, [shape(ALL_ROWS, HALF)], [pltpu.V...]
  transfers between devices with their start and end apart: 8 -> 8, of which waited for: 4 -> 2; matrix products, arithmetic and copies ran while one was open for 0% -> 0% of each run, Pallas kernels for 5% -> 35%
where the time goes in v2:
time: 56.6 us; the launch traced here: 56.1 us
  Pallas kernels  34.7 us (61%)
  starting transfers between devices  11.1 us (20%)
  local copies, waits for them, and re-layouts  5.99 us (11%)
  waiting for transfers between devices  2.91 us (5%)
  between operations  1.41 us (2%)
    pallas_call x1, Pallas kernels, body(): call(inner_kernel, [SMEM] + [VMEM] * 9, [shape(ALL_ROWS, HALF)], [pltpu.V...  11.3 us
    pallas_call x1, Pallas kernels, body(): call(outer_kernel, [VMEM] * (9 + 2 * PEERS), [shape(PLANES, NY, CX)] + [s...  6.77 us
    pallas_call x1, Pallas kernels, body(): call(prep_kernel, [SMEM, SMEM, VMEM], [shape(LEVELS + 1, 2 * CX, 2 * CX,...  6.54 us
    unnamed x16, local copies, waits for them, and re-layouts  5.99 us
    pallas_call x1, Pallas kernels, body(): call(charge_kernel, [VMEM] * 8 + [ANY], [shape(PLANES, size, CX) for size...  5.31 us
    ppermute x3, starting transfers between devices, body(): lax.ppermute(samples[k], 'sect', swaps[k])  4.32 us
    ppermute x3, starting transfers between devices, body(): lax.ppermute(sends[k], 'sect', swaps[k])  3.15 us
    ppermute x3, waiting for transfers between devices, body(): lax.ppermute(samples[k], 'sect', swaps[k])  2.89 us
  transfers between devices with their start and end apart: 8, of which 2 were waited for; matrix products, arithmetic and copies ran while one was open for 0% of the time, Pallas kernels for 35%

profile of v2, /device:TPU:0, one launch (start us, length us, event | category | flops | bytes accessed | tf_op | source)
XLA Modules:
  0.0 56.1 jit_solution(7247697523180553240)
XLA Ops:
  1.3 0.0 copy-start
  1.3 1.0 %copy-done = f32[1024,128]{1,0:T(8,128)S(1)} copy-done((f32[1024,128]{1,0:T(8,128)S(1)}, f32[1024,128]{1,0:T(8,128)}, u32[]{:S(2)}) %copy-start) | copy-done | bytes 524312
  2.3 0.0 copy-start.2
  2.3 0.8 %copy-done.2 = f32[8,1024]{1,0:T(8,128)S(1)} copy-done((f32[8,1024]{1,0:T(8,128)S(1)}, f32[8,1024]{1,0:T(8,128)}, u32[]{:S(2)}) %copy-start.2) | copy-done | bytes 32792
  3.1 0.0 copy-start.5
  3.1 0.7 %copy-done.5 = f32[1024]{0:T(1024)S(1)} copy-done((f32[1024]{0:T(1024)S(1)}, f32[1024]{0:T(1024)}, u32[]{:S(2)}) %copy-start.5) | copy-done | bytes 4120
  3.8 0.0 copy-start.6
  3.8 0.7 %copy-done.6 = s32[256,1]{0,1:T(1,128)S(1)} copy-done((s32[256,1]{0,1:T(1,128)S(1)}, s32[256,1]{0,1:T(1,128)}, u32[]{:S(2)}) %copy-start.6) | copy-done | bytes 1048
  4.4 0.0 copy-start.7
  4.4 0.7 %copy-done.7 = s32[256]{0:T(256)S(1)} copy-done((s32[256]{0:T(256)S(1)}, s32[256]{0:T(256)}, u32[]{:S(2)}) %copy-start.7) | copy-done | bytes 1048
  5.1 1.2 %shard_map.104 = (f32[432,128]{1,0:T(8,128)S(1)}, f32[432,128]{1,0:T(8,128)S(1)}, f32[432,128]{1,0:T(8,128)S(1)}, f32[432,128]{1,0:T(8,128)S(1)}, f32[8,256]{1,0:T(8,128)S(1)}) custom-call(s32[1]{0:T(128)S(6)} %copy.11.count_ref, f32[1,1024]{1,0:T(1,128)S(1)} %bitcast.4, f32[8,1024]{1,0:T(8,128)S(1)} %copy-done.2, f32[1024,128]{1,0:T(8,128)S(1)} %copy-done, ...), custom_call_target="tpu_custom_call" | custom-call | tf_op jit(solution)/shard_map/pallas_call | solution.py:459
  6.3 2.5 %collective-permute-start.2 = (f32[432,128]{1,0:T(8,128)S(1)}, f32[432,128]{1,0:T(8,128)S(1)}, u32[]{:S(2)}, u32[]{:S(2)}) collective-permute-start(f32[432,128]{1,0:T(8,128)S(1)} %get-tuple-element.49), channel_id=1, source_target_pairs={{0,3},{1,2},{2,1},{3,0},{4,7},{5,6},{6,5},{7,4},{8,11},{9,10},{10,... | collective-permute-start | bytes 663560 | tf_op jit(solution)/shard_map/ppermute | solution.py:481
  8.8 0.6 %collective-permute-start.1 = (f32[432,128]{1,0:T(8,128)S(1)}, f32[432,128]{1,0:T(8,128)S(1)}, u32[]{:S(2)}, u32[]{:S(2)}) collective-permute-start(f32[432,128]{1,0:T(8,128)S(1)} %get-tuple-element.47), channel_id=1, source_target_pairs={{0,2},{1,3},{2,0},{3,1},{4,6},{5,7},{6,4},{7,5},{8,10},{9,11},{10,... | collective-permute-start | bytes 663560 | tf_op jit(solution)/shard_map/ppermute | solution.py:481
  9.4 0.0 collective-permute-start
  9.5 0.7 %shard_map.105 = (bf16[128,2048]{1,0:T(8,128)(2,1)S(1)}, bf16[384,128]{1,0:T(8,128)(2,1)S(1)}, bf16[96,384]{1,0:T(8,128)(2,1)S(1)}, f32[32,96,128]{2,1,0:T(8,128)S(1)}) custom-call(f32[432,128]{1,0:T(8,128)S(1)} %get-tuple-element.43.ref), custom_call_target="tpu_custom_call" | custom-call | tf_op jit(solution)/shard_map/pallas_call | solution.py:498
  10.1 0.0 copy-start.1
  10.1 0.8 %copy-done.1 = f32[5,2,8,8]{3,2,1,0:T(8,128)S(1)} copy-done((f32[5,2,8,8]{3,2,1,0:T(8,128)S(1)}, f32[5,2,8,8]{3,2,1,0:T(8,128)}, u32[]{:S(2)}) %copy-start.1) | copy-done | bytes 2584
  10.9 0.0 copy-start.3
  10.9 0.7 %copy-done.3 = f32[5,2,17]{2,1,0:T(2,128)S(1)} copy-done((f32[5,2,17]{2,1,0:T(2,128)S(1)}, f32[5,2,17]{2,1,0:T(2,128)}, u32[]{:S(2)}) %copy-start.3) | copy-done | bytes 704
  11.6 0.0 copy-start.4
  11.6 0.7 %copy-done.4 = f32[5,2,17]{2,1,0:T(2,128)S(1)} copy-done((f32[5,2,17]{2,1,0:T(2,128)S(1)}, f32[5,2,17]{2,1,0:T(2,128)}, u32[]{:S(2)}) %copy-start.4) | copy-done | bytes 704
  12.3 6.5 %shard_map.109 = (bf16[5,256,256]{2,1,0:T(8,128)(2,1)S(1)}, bf16[5,128,256]{2,1,0:T(8,128)(2,1)S(1)}, bf16[752,768]{1,0:T(8,128)(2,1)S(1)}, bf16[752,768]{1,0:T(...) custom-call(f32[5,2,17]{2,1,0:T(2,128)S(1)} %copy-done.3, ...), custom_call_target="tpu_custom_call" | custom-call | tf_op jit(solution)/shard_map/pallas_call | solution.py:482
  18.8 0.0 collective-permute-done.2.ref
  18.9 0.7 %shard_map.108 = (bf16[128,2048]{1,0:T(8,128)(2,1)S(1)}, bf16[384,128]{1,0:T(8,128)(2,1)S(1)}, bf16[96,384]{1,0:T(8,128)(2,1)S(1)}, f32[32,96,128]{2,1,0:T(8,128)S(1)}) custom-call(f32[432,128]{1,0:T(8,128)S(1)} %collective-permute-done.2.ref), custom_call_target="tpu_custom_call" | custom-call | tf_op jit(solution)/shard_map/pallas_call | solution.py:498
  19.5 0.0 collective-permute-done.1.ref
  19.5 0.7 %shard_map.107 = (bf16[128,2048]{1,0:T(8,128)(2,1)S(1)}, bf16[384,128]{1,0:T(8,128)(2,1)S(1)}, bf16[96,384]{1,0:T(8,128)(2,1)S(1)}, f32[32,96,128]{2,1,0:T(8,128)S(1)}) custom-call(f32[432,128]{1,0:T(8,128)S(1)} %collective-permute-done.1.ref), custom_call_target="tpu_custom_call" | custom-call | tf_op jit(solution)/shard_map/pallas_call | solution.py:498
  20.2 0.0 collective-permute-done.ref
  20.2 0.7 %shard_map.106 = (bf16[128,2048]{1,0:T(8,128)(2,1)S(1)}, bf16[384,128]{1,0:T(8,128)(2,1)S(1)}, bf16[96,384]{1,0:T(8,128)(2,1)S(1)}, f32[32,96,128]{2,1,0:T(8,128)S(1)}) custom-call(f32[432,128]{1,0:T(8,128)S(1)} %collective-permute-done.ref), custom_call_target="tpu_custom_call" | custom-call | tf_op jit(solution)/shard_map/pallas_call | solution.py:498
  20.9 5.3 %shard_map.110 = (f32[8,384,128]{2,1,0:T(8,128)S(1)}, f32[8,192,128]{2,1,0:T(8,128)S(1)}, f32[8,96,128]{2,1,0:T(8,128)S(1)}, f32[8,48,128]{2,1,0:T(8,128)S(1)}, ...) custom-call(bf16[128,2048]{1,0:T(8,128)(2,1)S(1)} %get-tuple-element.44.refs_0_, ...), custom_call_target="tpu_custom_call" | custom-call | tf_op jit(solution)/shard_map/pallas_call | solution.py:511
  26.2 2.4 %collective-permute-start.3 = (f32[408,128]{1,0:T(8,128)S(1)}, f32[408,128]{1,0:T(8,128)S(1)}, u32[]{:S(2)}, u32[]{:S(2)}) collective-permute-start(f32[408,128]{1,0:T(8,128)S(1)} %get-tuple-element.64), channel_id=1, source_target_pairs={{0,1},{1,2},{2,3},{3,4},{4,5},{5,6},{6,7},{7,8},{8,9},{9,10},{10,1... | collective-permute-start | bytes 626696 | tf_op jit(solution)/shard_map/ppermute | solution.py:521
  28.6 1.3 %collective-permute-start.4 = (f32[408,128]{1,0:T(8,128)S(1)}, f32[408,128]{1,0:T(8,128)S(1)}, u32[]{:S(2)}, u32[]{:S(2)}) collective-permute-start(f32[408,128]{1,0:T(8,128)S(1)} %get-tuple-element.65), channel_id=1, source_target_pairs={{1,0},{2,1},{3,2},{4,3},{5,4},{6,5},{7,6},{8,7},{9,8},{10,9},{11,1... | collective-permute-start | bytes 626696 | tf_op jit(solution)/shard_map/ppermute | solution.py:522
  29.9 11.3 %shard_map.111.refs_0_ = f32[752,1024]{1,0:T(8,128)S(1)} custom-call(f32[5,2,8,8]{3,2,1,0:T(8,128)S(1)} %copy-done.1, f32[8,384,128]{2,1,0:T(8,128)S(1)} %get-tuple-element.56.q0, f32[8,192,128]{2,1,0:T(8,128)S(1)} %get-tuple-element.57.s1, f32[8,96,128]{2,1,0:T(8,128)S(1)} %get-tuple-element.58.s2, f32[8,48,128]{2,1,0:T(8,128)S(1)} %get-tuple-element.59.s3, ...), custom_call_target="tpu_custom_call" | custom-call | tf_op jit(solution)/shard_map/pallas_call | solution.py:523
  41.1 0.0 collective-permute-done.3.refs_1_
  41.2 0.0 collective-permute-done.4.refs_2_
  41.2 6.8 %shard_map.112 = (f32[8,384,128]{2,1,0:T(8,128)}, f32[8,128]{1,0:T(8,128)S(1)}, f32[8,128]{1,0:T(8,128)S(1)}, f32[8,128]{1,0:T(8,128)S(1)}, f32[8,128]{1,0:T(8,128)S(1)}) custom-call(f32[752,1024]{1,0:T(8,128)S(1)} %shard_map.111.refs_0_, f32[408,128]{1,0:T(8,128)S(1)} %collective-permute-done.3.refs_1_, f32[408,128]{1,0:T(8,128)S(1)} %collective-permute-done.4.refs_2_, ...), custom_call_target="tpu_custom_call" | custom-call | tf_op jit(solution)/shard_map/pallas_call | solution.py:533
  47.9 2.6 %collective-permute-start.5 = (f32[8,128]{1,0:T(8,128)S(1)}, f32[8,128]{1,0:T(8,128)S(1)}, u32[]{:S(2)}, u32[]{:S(2)}) collective-permute-start(f32[8,128]{1,0:T(8,128)S(1)} %get-tuple-element.81), channel_id=1, source_target_pairs={{0,1},{1,0},{2,3},{3,2},{4,5},{5,4},{6,7},{7,6},{8,9},{9,8},{10,11... | collective-permute-start | bytes 12296 | tf_op jit(solution)/shard_map/ppermute | solution.py:545
  50.5 1.6 %collective-permute-start.6 = (f32[8,128]{1,0:T(8,128)S(1)}, f32[8,128]{1,0:T(8,128)S(1)}, u32[]{:S(2)}, u32[]{:S(2)}) collective-permute-start(f32[8,128]{1,0:T(8,128)S(1)} %get-tuple-element.82), channel_id=1, source_target_pairs={{0,2},{1,3},{2,0},{3,1},{4,6},{5,7},{6,4},{7,5},{8,10},{9,11},{10,... | collective-permute-start | bytes 12296 | tf_op jit(solution)/shard_map/ppermute | solution.py:545
  52.1 0.1 collective-permute-start.7
  52.3 0.0 collective-permute-done.5.b1
  52.3 1.8 %collective-permute-done.6.b2 = f32[8,128]{1,0:T(8,128)S(1)} collective-permute-done((f32[8,128]{1,0:T(8,128)S(1)}, f32[8,128]{1,0:T(8,128)S(1)}, u32[]{:S(2)}, u32[]{:S(2)}) %collective-permute-start.6) | collective-permute-done | bytes 4128 | tf_op jit(solution)/shard_map/ppermute | solution.py:545
  54.1 1.0 %collective-permute-done.7.b3 = f32[8,128]{1,0:T(8,128)S(1)} collective-permute-done((f32[8,128]{1,0:T(8,128)S(1)}, f32[8,128]{1,0:T(8,128)S(1)}, u32[]{:S(2)}, u32[]{:S(2)}) %collective-permute-start.7) | collective-permute-done | bytes 4128 | tf_op jit(solution)/shard_map/ppermute | solution.py:545
  55.2 1.0 %shard_map.113 = f32[1,1024]{1,0:T(1,128)} custom-call(s32[1]{0:T(128)S(6)} %copy.11.count_ref, f32[8,256]{1,0:T(8,128)S(1)} %get-tuple-element.79.slot_ref, f32[8,128]{1,0:T(8,128)S(1)} %get-tuple-element.80.b0, f32[8,128]{1,0:T(8,128)S(1)} %collective-permute-done.5.b1, f32[8,128]{1,0:T(8,128)S(1)} %collective-permute-done.6.b2, ...), custom_call_target="tpu_custom_call" | custom-call | tf_op jit(solution)/shard_map/pallas_call | solution.py:546
Async XLA Ops:
  1.3 1.0 %copy-start = (f32[1024,128]{1,0:T(8,128)S(1)}, f32[1024,128]{1,0:T(8,128)}, u32[]{:S(2)}) copy-start(f32[1024,128]{1,0:T(8,128)} %cells_hbm.1) | copy-start | bytes 1572868
  2.3 0.8 %copy-start.2 = (f32[8,1024]{1,0:T(8,128)S(1)}, f32[8,1024]{1,0:T(8,128)}, u32[]{:S(2)}) copy-start(f32[8,1024]{1,0:T(8,128)} %planes_hbm.1) | copy-start | bytes 98308
  3.1 0.7 %copy-start.5 = (f32[1024]{0:T(1024)S(1)}, f32[1024]{0:T(1024)}, u32[]{:S(2)}) copy-start(f32[1024]{0:T(1024)} %param.9) | copy-start | bytes 12292
  3.8 0.7 %copy-start.6 = (s32[256,1]{0,1:T(1,128)S(1)}, s32[256,1]{0,1:T(1,128)}, u32[]{:S(2)}) copy-start(s32[256,1]{0,1:T(1,128)} %param.12) | copy-start | bytes 3076
  4.4 0.7 %copy-start.7 = (s32[256]{0:T(256)S(1)}, s32[256]{0:T(256)}, u32[]{:S(2)}) copy-start(s32[256]{0:T(256)} %param.13) | copy-start | bytes 3076
  6.3 12.5 %collective-permute-start.2 = (f32[432,128]{1,0:T(8,128)S(1)}, f32[432,128]{1,0:T(8,128)S(1)}, u32[]{:S(2)}, u32[]{:S(2)}) collective-permute-start(f32[432,128]{1,0:T(8,128)S(1)} %get-tuple-element.49), channel_id=1, source_target_pairs={{0,3},{1,2},{2,1},{3,0},{4,7},{5,6},{6,5},{7,4},{8,11},{9,10},{10,... | collective-permute-start | bytes 663560 | tf_op jit(solution)/shard_map/ppermute | solution.py:481
  8.8 10.7 %collective-permute-start.1 = (f32[432,128]{1,0:T(8,128)S(1)}, f32[432,128]{1,0:T(8,128)S(1)}, u32[]{:S(2)}, u32[]{:S(2)}) collective-permute-start(f32[432,128]{1,0:T(8,128)S(1)} %get-tuple-element.47), channel_id=1, source_target_pairs={{0,2},{1,3},{2,0},{3,1},{4,6},{5,7},{6,4},{7,5},{8,10},{9,11},{10,... | collective-permute-start | bytes 663560 | tf_op jit(solution)/shard_map/ppermute | solution.py:481
  9.4 10.8 %collective-permute-start = (f32[432,128]{1,0:T(8,128)S(1)}, f32[432,128]{1,0:T(8,128)S(1)}, u32[]{:S(2)}, u32[]{:S(2)}) collective-permute-start(f32[432,128]{1,0:T(8,128)S(1)} %get-tuple-element.45), channel_id=1, source_target_pairs={{0,1},{1,0},{2,3},{3,2},{4,5},{5,4},{6,7},{7,6},{8,9},{9,8},{10,11... | collective-permute-start | bytes 663560 | tf_op jit(solution)/shard_map/ppermute | solution.py:481
  10.1 0.8 %copy-start.1 = (f32[5,2,8,8]{3,2,1,0:T(8,128)S(1)}, f32[5,2,8,8]{3,2,1,0:T(8,128)}, u32[]{:S(2)}) copy-start(f32[5,2,8,8]{3,2,1,0:T(8,128)} %mix_ref.3) | copy-start | bytes 7684
  10.9 0.7 %copy-start.3 = (f32[5,2,17]{2,1,0:T(2,128)S(1)}, f32[5,2,17]{2,1,0:T(2,128)}, u32[]{:S(2)}) copy-start(f32[5,2,17]{2,1,0:T(2,128)} %across_ref.1) | copy-start | bytes 2044
  11.6 0.7 %copy-start.4 = (f32[5,2,17]{2,1,0:T(2,128)S(1)}, f32[5,2,17]{2,1,0:T(2,128)}, u32[]{:S(2)}) copy-start(f32[5,2,17]{2,1,0:T(2,128)} %along_ref.1) | copy-start | bytes 2044
  26.2 15.0 %collective-permute-start.3 = (f32[408,128]{1,0:T(8,128)S(1)}, f32[408,128]{1,0:T(8,128)S(1)}, u32[]{:S(2)}, u32[]{:S(2)}) collective-permute-start(f32[408,128]{1,0:T(8,128)S(1)} %get-tuple-element.64), channel_id=1, source_target_pairs={{0,1},{1,2},{2,3},{3,4},{4,5},{5,6},{6,7},{7,8},{8,9},{9,10},{10,1... | collective-permute-start | bytes 626696 | tf_op jit(solution)/shard_map/ppermute | solution.py:521
  28.6 12.6 %collective-permute-start.4 = (f32[408,128]{1,0:T(8,128)S(1)}, f32[408,128]{1,0:T(8,128)S(1)}, u32[]{:S(2)}, u32[]{:S(2)}) collective-permute-start(f32[408,128]{1,0:T(8,128)S(1)} %get-tuple-element.65), channel_id=1, source_target_pairs={{1,0},{2,1},{3,2},{4,3},{5,4},{6,5},{7,6},{8,7},{9,8},{10,9},{11,1... | collective-permute-start | bytes 626696 | tf_op jit(solution)/shard_map/ppermute | solution.py:522
  47.9 4.3 %collective-permute-start.5 = (f32[8,128]{1,0:T(8,128)S(1)}, f32[8,128]{1,0:T(8,128)S(1)}, u32[]{:S(2)}, u32[]{:S(2)}) collective-permute-start(f32[8,128]{1,0:T(8,128)S(1)} %get-tuple-element.81), channel_id=1, source_target_pairs={{0,1},{1,0},{2,3},{3,2},{4,5},{5,4},{6,7},{7,6},{8,9},{9,8},{10,11... | collective-permute-start | bytes 12296 | tf_op jit(solution)/shard_map/ppermute | solution.py:545
  50.5 3.6 %collective-permute-start.6 = (f32[8,128]{1,0:T(8,128)S(1)}, f32[8,128]{1,0:T(8,128)S(1)}, u32[]{:S(2)}, u32[]{:S(2)}) collective-permute-start(f32[8,128]{1,0:T(8,128)S(1)} %get-tuple-element.82), channel_id=1, source_target_pairs={{0,2},{1,3},{2,0},{3,1},{4,6},{5,7},{6,4},{7,5},{8,10},{9,11},{10,... | collective-permute-start | bytes 12296 | tf_op jit(solution)/shard_map/ppermute | solution.py:545
  52.1 3.0 %collective-permute-start.7 = (f32[8,128]{1,0:T(8,128)S(1)}, f32[8,128]{1,0:T(8,128)S(1)}, u32[]{:S(2)}, u32[]{:S(2)}) collective-permute-start(f32[8,128]{1,0:T(8,128)S(1)} %get-tuple-element.83), channel_id=1, source_target_pairs={{0,3},{1,2},{2,1},{3,0},{4,7},{5,6},{6,5},{7,4},{8,11},{9,10},{10,... | collective-permute-start | bytes 12296 | tf_op jit(solution)/shard_map/ppermute | solution.py:545

commit v3 on v2

--- a/solution.py
+++ b/solution.py
@@ -146,11 +146,22 @@
     return (block << level) + offset, jnp.where(first, j + WIDTHS[level], j - REACH)
 
 
+def taps_at(table, shift):
+    spot = jnp.where((shift >= 0) & (shift < TAPS), shift, CX - 1)
+    return jnp.take_along_axis(jnp.broadcast_to(table, spot.shape), spot, axis=1)
+
+
 def prep_kernel(
     across_ref, along_ref, mix_ref, own_ref, own_low_ref, across_high, across_low, blend_high,
-    blend_low, rim_high, rim_low
+    blend_low, rim_high, rim_low, table
 ):
     exact = lax.Precision.HIGHEST
+    table[...] = jnp.zeros(table.shape, F32)
+    for level in range(LEVELS + 1):
+        for r in range(2):
+            line = 4 * level + r
+            table[line : line + 1, :TAPS] = along_ref[level, r : r + 1, :]
+            table[line + 2 : line + 3, :TAPS] = across_ref[level, r : r + 1, :]
     for level in range(LEVELS + 1):
         scale = 0.25**level
         row = iota((CX, 1), 0)
@@ -163,23 +174,21 @@
         same = lane_place == line_place
         pick = (lane_z == iota((CX, 8), 1)).astype(F32)
         pick_t = (line_z == iota((8, CX), 0)).astype(F32)
+        masks = [
+            jnp.broadcast_to((lane_z == z).astype(F32), (CX, CX)).astype(BF16)
+            for z in range(PLANES)
+        ]
         for r in range(2):
             part = slice(r * CX, (r + 1) * CX)
-            taps = jnp.zeros((CX, CX), F32)
-            rims = jnp.zeros((CX, CX), F32)
-            for t in range(TAPS):
-                tap = along_ref[level, r, t]
-                taps = jnp.where(shift == t, tap, taps)
-                rims = jnp.where(rim_shift == t, tap, rims)
-            high, low = split(taps * scale)
+            line = table[4 * level + r : 4 * level + r + 1, :]
+            high, low = split(taps_at(line, shift) * scale)
             own_ref[level, :CX, part] = high
             own_ref[level, CX:, part] = high
             own_low_ref[level, :, part] = low
-            high, low = split(rims * scale)
+            high, low = split(taps_at(line, rim_shift) * scale)
             for z in range(PLANES):
-                mine = jnp.broadcast_to((lane_z == z).astype(F32), (CX, CX)).astype(BF16)
-                rim_high[level, part, z * CX : (z + 1) * CX] = high * mine
-                rim_low[level, part, z * CX : (z + 1) * CX] = low * mine
+                rim_high[level, part, z * CX : (z + 1) * CX] = high * masks[z]
+                rim_low[level, part, z * CX : (z + 1) * CX] = low * masks[z]
             mixes = lax.dot_general(
                 pick, mix_ref[level, r], (((1,), (1,)), ((), ())), precision=exact,
                 preferred_element_type=F32,
@@ -191,18 +200,20 @@
         size, step = HEIGHTS[level], STEP[level]
         rows = slice(ROW_OF[level], ROW_OF[level] + size)
         mine = height_of(iota((size, 1), 0), level)
+        first = table[4 * level + 2 : 4 * level + 3, :]
+        both = first + turn(table[4 * level + 3 : 4 * level + 4, :], 32)
         for start in range(0, 2 * step, CX):
             lanes = min(CX, 2 * step - start)
-            place = iota((1, lanes), 1) + start
+            place = iota((1, CX), 1) + start
             second = place >= step
             place = jnp.where(second, place - step, place)
             other = jnp.where(place < size, height_of(place, level), 4 * NY)
             shift = other - mine + REACH
-            taps = jnp.zeros((size, lanes), F32)
-            for t in range(TAPS):
-                tap = jnp.where(second, across_ref[level, 1, t], across_ref[level, 0, t])
-                taps = jnp.where(shift == t, tap, taps)
-            high, low = split(taps)
+            spot = jnp.where(
+                (shift >= 0) & (shift < TAPS), shift + jnp.where(second, 32, 0), CX - 1
+            )
+            taps = jnp.take_along_axis(jnp.broadcast_to(both, spot.shape), spot, axis=1)
+            high, low = split(taps[:, :lanes])
             across_high[rows, start : start + lanes] = high
             across_low[rows, start : start + lanes] = low
 
@@ -232,7 +243,7 @@
 
 def charge_kernel(*refs):
     bricks, hots = refs[:PEERS], refs[PEERS : 2 * PEERS]
-    q0, s1, s2, s3, s4, to_right, to_left = refs[2 * PEERS + 1 : -4]
+    q0, s1, s2, s3, s4, to_pair, to_next = refs[2 * PEERS + 1 : -4]
     rims = refs[-4:]
     hot = jnp.concatenate([ref[...] for ref in hots], axis=1)
     lanes = iota((1, CX), 1)
@@ -274,15 +285,20 @@
         value = value + turn(value, -8)
         s4[z] = value
         coarse = jnp.where((lanes & 15) == z, turn(value, z), coarse)
-    to_right[NY:, :] = coarse
-    to_left[NY:, :] = coarse
-    to_right[RIM_ROW[3] + HEIGHTS[3] : NY, :] = rims[0][RIM_ROW[3] + HEIGHTS[3] : NY, :]
-    to_left[RIM_ROW[3] + HEIGHTS[3] : NY, :] = rims[0][RIM_ROW[3] + HEIGHTS[3] : NY, :]
-    for level in range(1, LEVELS):
-        rows = slice(RIM_ROW[level], RIM_ROW[level] + HEIGHTS[level])
-        other = turn(rims[level][...], CX // 2)
-        to_right[rows, :] = jnp.where(lanes < CX // 2, other, rims[0][rows, :])
-        to_left[rows, :] = jnp.where(lanes < CX // 2, rims[0][rows, :], other)
+    even = (lax.axis_index("sect") & 1) == 0
+    to_pair[NY:, :] = coarse
+    to_next[NY:, :] = coarse
+    for level in range(1, LEVELS + 1):
+        if level < LEVELS:
+            rows = slice(RIM_ROW[level], RIM_ROW[level] + HEIGHTS[level])
+            other = turn(rims[level][...], CX // 2)
+        else:
+            rows = slice(RIM_ROW[3] + HEIGHTS[3], NY)
+            other = jnp.zeros((NY - RIM_ROW[3] - HEIGHTS[3], CX), F32)
+        right = jnp.where(lanes < CX // 2, other, rims[0][rows, :])
+        left = jnp.where(lanes < CX // 2, rims[0][rows, :], other)
+        to_pair[rows, :] = jnp.where(even, right, left)
+        to_next[rows, :] = jnp.where(even, left, right)
 
 
 def inner_kernel(
@@ -296,35 +312,28 @@
             ranked[z, :size, :] = dot(
                 jnp.concatenate([high, low], axis=1), own_ref[level]
             ) + dot(high, own_low_ref[level])
-        chunk = {384: 32, 192: 32, 96: 32, 48: 16, 24: 24}[size]
-
-        def mixed(index, carry, level=level, chunk=chunk, step=step):
-            start = index * chunk
-            if not isinstance(start, int):
-                start = pl.multiple_of(start, chunk)
-            for r in range(2):
-                parts = [
-                    ranked[w, pl.ds(start, chunk), r * CX : (r + 1) * CX] for w in range(PLANES)
-                ]
-                for z in range(PLANES):
-                    total = parts[0] * mix_ref[level, r, z, 0]
-                    for w in range(1, PLANES):
-                        total = total + parts[w] * mix_ref[level, r, z, w]
-                    if chunk == 24:
-                        total = jnp.concatenate([total, jnp.zeros((8, CX), F32)], axis=0)
-                    high, low = split(total)
-                    place = pl.ds(r * step + start, high.shape[0])
-                    high_ref[place, z * CX : (z + 1) * CX] = high
-                    low_ref[place, z * CX : (z + 1) * CX] = low
-            return carry
-
-        if size == chunk:
-            mixed(0, 0)
-        else:
-            lax.fori_loop(0, size // chunk, mixed, 0)
+        chunk = {384: 64, 192: 64, 96: 48, 48: 48, 24: 24}[size]
         rows = slice(ROW_OF[level], ROW_OF[level] + size)
         heavy, light = across_high[rows, : 2 * step], across_low[rows, : 2 * step]
         for pair in range(PLANES // 2):
+            for r in range(2):
+                weights = [
+                    [mix_ref[level, r, 2 * pair + i, w] for w in range(PLANES)] for i in range(2)
+                ]
+                for start in range(0, size, chunk):
+                    for i in range(2):
+                        total = None
+                        for w in range(PLANES):
+                            part = ranked[w, start : start + chunk, r * CX : (r + 1) * CX]
+                            part = part * weights[i][w]
+                            total = part if w == 0 else total + part
+                        if chunk == 24:
+                            total = jnp.concatenate([total, jnp.zeros((8, CX), F32)], axis=0)
+                        high, low = split(total)
+                        place = slice(r * step + start, r * step + start + high.shape[0])
+                        column = slice((2 * pair + i) * CX, (2 * pair + i + 1) * CX)
+                        high_ref[place, column] = high
+                        low_ref[place, column] = low
             part = slice(pair * 2 * CX, (pair + 1) * 2 * CX)
             high = high_ref[: 2 * step, part]
             out_ref[rows, part] = (
@@ -333,25 +342,28 @@
 
 
 def outer_kernel(*refs):
-    inner, from_left, from_right, across_high, across_low = refs[:5]
+    inner, by_pair, by_next, across_high, across_low = refs[:5]
     blend_high, blend_low, rim_high, rim_low = refs[5:9]
     matches, weights = refs[9 : 9 + PEERS], refs[9 + PEERS : 9 + 2 * PEERS]
     grid_ref = refs[9 + 2 * PEERS]
     outs = refs[10 + 2 * PEERS : 10 + 3 * PEERS]
     high_ref, low_ref, tiles, picked, doubled = refs[10 + 3 * PEERS :]
     lanes = iota((1, CX), 1)
+    even = (lax.axis_index("sect") & 1) == 0
     high_ref[...] = jnp.zeros((ALL_K, 2 * CX), BF16)
     low_ref[...] = jnp.zeros((ALL_K, 2 * CX), BF16)
     sums = []
     for level in range(LEVELS + 1):
         size, step = HEIGHTS[level], STEP[level]
         rows = slice(RIM_ROW[level], RIM_ROW[level] + size)
+        from_left = jnp.where(even, by_next[rows, :], by_pair[rows, :])
+        from_right = jnp.where(even, by_pair[rows, :], by_next[rows, :])
         if level == 0:
-            rims = jnp.where(lanes < CX // 2, from_right[rows, :], from_left[rows, :])
+            rims = jnp.where(lanes < CX // 2, from_right, from_left)
         elif level < LEVELS:
-            rims = jnp.where(lanes < CX // 2, from_left[rows, :], from_right[rows, :])
+            rims = jnp.where(lanes < CX // 2, from_left, from_right)
         else:
-            rims = jnp.where((lanes & 15) < 8, from_left[rows, :], turn(from_right[rows, :], 8))
+            rims = jnp.where((lanes & 15) < 8, from_left, turn(from_right, 8))
         high, low = split(rims)
         mixed = dot(high, blend_high[level]) + dot(low, blend_high[level])
         mixed = mixed + dot(high, blend_low[level])
@@ -435,6 +447,7 @@
 VMEM = pl.BlockSpec(memory_space=pltpu.VMEM)
 SMEM = pl.BlockSpec(memory_space=pltpu.SMEM)
 ANY = pl.BlockSpec(memory_space=pl.ANY)
+HBM = pl.BlockSpec(memory_space=pltpu.HBM)
 
 
 def shape(*dims, kind=F32):
@@ -458,7 +471,7 @@
 ):
     *sends, slots = call(
         route_kernel,
-        [SMEM] + [ANY] * 5,
+        [SMEM] + [HBM] * 5,
         [shape(ROWS, CX)] * PEERS + [shape(8, BRICKS)],
         [
             pltpu.VMEM((SEGS, CX), F32),
@@ -481,7 +494,7 @@
     held = [sends[0]] + [lax.ppermute(sends[k], "sect", swaps[k]) for k in range(1, PEERS)]
     prepared = call(
         prep_kernel,
-        [SMEM, SMEM, VMEM],
+        [VMEM, VMEM, VMEM],
         [
             shape(LEVELS + 1, 2 * CX, 2 * CX, kind=BF16),
             shape(LEVELS + 1, CX, 2 * CX, kind=BF16),
@@ -492,6 +505,7 @@
             shape(LEVELS + 1, 2 * CX, HALF, kind=BF16),
             shape(LEVELS + 1, 2 * CX, HALF, kind=BF16),
         ],
+        [pltpu.VMEM((24, CX), F32)],
     )(kern_across, kern_along, plane_mix)
     own, own_low, across_high, across_low, *outer = prepared
     parts = [
@@ -508,7 +522,7 @@
         for value in held
     ]
     bricks, hots, matches, weights = zip(*parts)
-    *fields, to_right, to_left = call(
+    *fields, to_pair, to_next = call(
         charge_kernel,
         [VMEM] * 8 + [ANY],
         [shape(PLANES, size, CX) for size in HEIGHTS] + [shape(RIM_ROWS, CX)] * 2,
@@ -516,10 +530,10 @@
     )(*bricks, *hots, own)
     axes = ("strip", "sect")
     devices = lax.axis_size(axes)
-    up = [(i, i + 1) for i in range(devices - 1)]
-    down = [(i + 1, i) for i in range(devices - 1)]
-    from_left = lax.ppermute(to_right, axes, up)
-    from_right = lax.ppermute(to_left, axes, down)
+    paired = [(i, i ^ 1) for i in range(devices)]
+    crossed = [(i, ((i + 1) ^ 1) - 1) for i in range(1, devices - 1)]
+    by_pair = lax.ppermute(to_pair, axes, paired)
+    by_next = lax.ppermute(to_next, axes, crossed)
     (inner,) = call(
         inner_kernel,
         [SMEM] + [VMEM] * 9,
@@ -541,7 +555,7 @@
             pltpu.VMEM((CAP, HALF), F32),
             pltpu.VMEM((2 * BAND, CX), F32),
         ],
-    )(inner, from_left, from_right, across_high, across_low, *outer, *matches, *weights)
+    )(inner, by_pair, by_next, across_high, across_low, *outer, *matches, *weights)
     back = [samples[0]] + [lax.ppermute(samples[k], "sect", swaps[k]) for k in range(1, PEERS)]
     (segments,) = call(
         pick_kernel, [SMEM] + [VMEM] * 5, [shape(1, SEGS)]

time: 56.6 us -> 52.9 us (0.935)
  Pallas kernels: 34.7 us -> 29.1 us
  waiting for transfers between devices: 2.91 us -> 6.81 us
  starting transfers between devices: 11.1 us -> 9.18 us
    ppermute x3, waiting for transfers between devices: 0.02 us -> 3.77 us  [body(): lax.ppermute(sends[k], 'sect', swaps[k])]
    pallas_call x2, Pallas kernels: 7.73 us -> 3.97 us  [the longest x1 2.78 us: body(): call(prep_kernel, [VMEM, VMEM, VMEM], [shape(LEVELS + 1, 2 * CX, 2 * CX,...]
    ppermute x2, starting transfers between devices: 3.68 us -> 0.93 us  [the longest x1 0.85 us: body(): by_next = lax.ppermute(to_next, axes, crossed)]
    pallas_call x1, Pallas kernels: 11.3 us -> 9.61 us  [body(): call(inner_kernel, [SMEM] + [VMEM] * 9, [shape(ALL_ROWS, HALF)], [pltpu.V...]
    ppermute x3, starting transfers between devices: 4.32 us -> 5.11 us  [body(): lax.ppermute(samples[k], 'sect', swaps[k])]
  transfers between devices with their start and end apart: 8 -> 8, of which waited for: 2 -> 3; matrix products, arithmetic and copies ran while one was open for 0% -> 0% of each run, Pallas kernels for 35% -> 27%
where the time goes in v3:
time: 52.9 us; the launch traced here: 52.5 us
  Pallas kernels  29.1 us (55%)
  starting transfers between devices  9.18 us (17%)
  waiting for transfers between devices  6.81 us (13%)
  local copies, waits for them, and re-layouts  5.99 us (11%)
  between operations  1.41 us (3%)
    pallas_call x1, Pallas kernels, body(): call(inner_kernel, [SMEM] + [VMEM] * 9, [shape(ALL_ROWS, HALF)], [pltpu.V...  9.61 us
    pallas_call x1, Pallas kernels, body(): call(outer_kernel, [VMEM] * (9 + 2 * PEERS), [shape(PLANES, NY, CX)] + [s...  6.78 us
    unnamed x16, local copies, waits for them, and re-layouts  5.99 us
    pallas_call x1, Pallas kernels, body(): call(charge_kernel, [VMEM] * 8 + [ANY], [shape(PLANES, size, CX) for size...  5.17 us
    ppermute x3, starting transfers between devices, body(): lax.ppermute(samples[k], 'sect', swaps[k])  5.11 us
    ppermute x3, waiting for transfers between devices, body(): lax.ppermute(sends[k], 'sect', swaps[k])  3.77 us
    ppermute x3, starting transfers between devices, body(): lax.ppermute(sends[k], 'sect', swaps[k])  3.15 us
    ppermute x3, waiting for transfers between devices, body(): lax.ppermute(samples[k], 'sect', swaps[k])  3.03 us
  transfers between devices with their start and end apart: 8, of which 3 were waited for; matrix products, arithmetic and copies ran while one was open for 0% of the time, Pallas kernels for 27%

profile of v3, /device:TPU:0, one launch (start us, length us, event | category | flops | bytes accessed | tf_op | source)
XLA Modules:
  0.0 52.5 jit_solution(3186349911115860790)
XLA Ops:
  1.3 0.0 copy-start
  1.3 1.0 %copy-done = f32[1024,128]{1,0:T(8,128)S(1)} copy-done((f32[1024,128]{1,0:T(8,128)S(1)}, f32[1024,128]{1,0:T(8,128)}, u32[]{:S(2)}) %copy-start) | copy-done | bytes 524312
  2.3 0.0 copy-start.2
  2.3 0.8 %copy-done.2 = f32[8,1024]{1,0:T(8,128)S(1)} copy-done((f32[8,1024]{1,0:T(8,128)S(1)}, f32[8,1024]{1,0:T(8,128)}, u32[]{:S(2)}) %copy-start.2) | copy-done | bytes 32792
  3.1 0.0 copy-start.5
  3.1 0.7 %copy-done.5 = f32[1024]{0:T(1024)S(1)} copy-done((f32[1024]{0:T(1024)S(1)}, f32[1024]{0:T(1024)}, u32[]{:S(2)}) %copy-start.5) | copy-done | bytes 4120
  3.8 0.0 copy-start.6
  3.8 0.7 %copy-done.6 = s32[256,1]{0,1:T(1,128)S(1)} copy-done((s32[256,1]{0,1:T(1,128)S(1)}, s32[256,1]{0,1:T(1,128)}, u32[]{:S(2)}) %copy-start.6) | copy-done | bytes 1048
  4.4 0.0 copy-start.7
  4.4 0.7 %copy-done.7 = s32[256]{0:T(256)S(1)} copy-done((s32[256]{0:T(256)S(1)}, s32[256]{0:T(256)}, u32[]{:S(2)}) %copy-start.7) | copy-done | bytes 1048
  5.1 1.2 %shard_map.104 = (f32[432,128]{1,0:T(8,128)S(1)}, f32[432,128]{1,0:T(8,128)S(1)}, f32[432,128]{1,0:T(8,128)S(1)}, f32[432,128]{1,0:T(8,128)S(1)}, f32[8,256]{1,0:T(8,128)S(1)}) custom-call(s32[1]{0:T(128)S(6)} %copy.11.count_ref, f32[1,1024]{1,0:T(1,128)S(1)} %bitcast.4, f32[8,1024]{1,0:T(8,128)S(1)} %copy-done.2, f32[1024,128]{1,0:T(8,128)S(1)} %copy-done, ...), custom_call_target="tpu_custom_call" | custom-call | tf_op jit(solution)/shard_map/pallas_call | solution.py:472
  6.3 2.5 %collective-permute-start.2 = (f32[432,128]{1,0:T(8,128)S(1)}, f32[432,128]{1,0:T(8,128)S(1)}, u32[]{:S(2)}, u32[]{:S(2)}) collective-permute-start(f32[432,128]{1,0:T(8,128)S(1)} %get-tuple-element.49), channel_id=1, source_target_pairs={{0,3},{1,2},{2,1},{3,0},{4,7},{5,6},{6,5},{7,4},{8,11},{9,10},{10,... | collective-permute-start | bytes 663560 | tf_op jit(solution)/shard_map/ppermute | solution.py:494
  8.8 0.6 %collective-permute-start.1 = (f32[432,128]{1,0:T(8,128)S(1)}, f32[432,128]{1,0:T(8,128)S(1)}, u32[]{:S(2)}, u32[]{:S(2)}) collective-permute-start(f32[432,128]{1,0:T(8,128)S(1)} %get-tuple-element.47), channel_id=1, source_target_pairs={{0,2},{1,3},{2,0},{3,1},{4,6},{5,7},{6,4},{7,5},{8,10},{9,11},{10,... | collective-permute-start | bytes 663560 | tf_op jit(solution)/shard_map/ppermute | solution.py:494
  9.4 0.0 collective-permute-start
  9.5 0.7 %shard_map.105 = (bf16[128,2048]{1,0:T(8,128)(2,1)S(1)}, bf16[384,128]{1,0:T(8,128)(2,1)S(1)}, bf16[96,384]{1,0:T(8,128)(2,1)S(1)}, f32[32,96,128]{2,1,0:T(8,128)S(1)}) custom-call(f32[432,128]{1,0:T(8,128)S(1)} %get-tuple-element.43.ref), custom_call_target="tpu_custom_call" | custom-call | tf_op jit(solution)/shard_map/pallas_call | solution.py:512
  10.1 0.0 copy-start.1
  10.1 0.8 %copy-done.1 = f32[5,2,8,8]{3,2,1,0:T(8,128)S(1)} copy-done((f32[5,2,8,8]{3,2,1,0:T(8,128)S(1)}, f32[5,2,8,8]{3,2,1,0:T(8,128)}, u32[]{:S(2)}) %copy-start.1) | copy-done | bytes 2584
  10.9 0.0 copy-start.3
  10.9 0.7 %copy-done.3 = f32[5,2,17]{2,1,0:T(2,128)S(1)} copy-done((f32[5,2,17]{2,1,0:T(2,128)S(1)}, f32[5,2,17]{2,1,0:T(2,128)}, u32[]{:S(2)}) %copy-start.3) | copy-done | bytes 704
  11.6 0.0 copy-start.4
  11.6 0.7 %copy-done.4 = f32[5,2,17]{2,1,0:T(2,128)S(1)} copy-done((f32[5,2,17]{2,1,0:T(2,128)S(1)}, f32[5,2,17]{2,1,0:T(2,128)}, u32[]{:S(2)}) %copy-start.4) | copy-done | bytes 704
  12.3 2.8 %shard_map.109 = (bf16[5,256,256]{2,1,0:T(8,128)(2,1)S(1)}, bf16[5,128,256]{2,1,0:T(8,128)(2,1)S(1)}, bf16[752,768]{1,0:T(8,128)(2,1)S(1)}, bf16[752,768]{1,0:T(...) custom-call(f32[5,2,17]{2,1,0:T(2,128)S(1)} %copy-done.3, ...), custom_call_target="tpu_custom_call" | custom-call | tf_op jit(solution)/shard_map/pallas_call | solution.py:495
  15.1 0.0 collective-permute-done.2.ref
  15.1 0.7 %shard_map.108 = (bf16[128,2048]{1,0:T(8,128)(2,1)S(1)}, bf16[384,128]{1,0:T(8,128)(2,1)S(1)}, bf16[96,384]{1,0:T(8,128)(2,1)S(1)}, f32[32,96,128]{2,1,0:T(8,128)S(1)}) custom-call(f32[432,128]{1,0:T(8,128)S(1)} %collective-permute-done.2.ref), custom_call_target="tpu_custom_call" | custom-call | tf_op jit(solution)/shard_map/pallas_call | solution.py:512
  15.8 3.8 %collective-permute-done.1.ref = f32[432,128]{1,0:T(8,128)S(1)} collective-permute-done((f32[432,128]{1,0:T(8,128)S(1)}, f32[432,128]{1,0:T(8,128)S(1)}, u32[]{:S(2)}, u32[]{:S(2)}) %collective-permute-start.1) | collective-permute-done | bytes 221216 | tf_op jit(solution)/shard_map/ppermute | solution.py:494
  19.5 0.7 %shard_map.107 = (bf16[128,2048]{1,0:T(8,128)(2,1)S(1)}, bf16[384,128]{1,0:T(8,128)(2,1)S(1)}, bf16[96,384]{1,0:T(8,128)(2,1)S(1)}, f32[32,96,128]{2,1,0:T(8,128)S(1)}) custom-call(f32[432,128]{1,0:T(8,128)S(1)} %collective-permute-done.1.ref), custom_call_target="tpu_custom_call" | custom-call | tf_op jit(solution)/shard_map/pallas_call | solution.py:512
  20.2 0.0 collective-permute-done.ref
  20.2 0.7 %shard_map.106 = (bf16[128,2048]{1,0:T(8,128)(2,1)S(1)}, bf16[384,128]{1,0:T(8,128)(2,1)S(1)}, bf16[96,384]{1,0:T(8,128)(2,1)S(1)}, f32[32,96,128]{2,1,0:T(8,128)S(1)}) custom-call(f32[432,128]{1,0:T(8,128)S(1)} %collective-permute-done.ref), custom_call_target="tpu_custom_call" | custom-call | tf_op jit(solution)/shard_map/pallas_call | solution.py:512
  20.9 5.2 %shard_map.110 = (f32[8,384,128]{2,1,0:T(8,128)S(1)}, f32[8,192,128]{2,1,0:T(8,128)S(1)}, f32[8,96,128]{2,1,0:T(8,128)S(1)}, f32[8,48,128]{2,1,0:T(8,128)S(1)}, ...) custom-call(bf16[128,2048]{1,0:T(8,128)(2,1)S(1)} %get-tuple-element.44.refs_0_, ...), custom_call_target="tpu_custom_call" | custom-call | tf_op jit(solution)/shard_map/pallas_call | solution.py:525
  26.0 0.1 collective-permute-start.3
  26.1 0.9 %collective-permute-start.4 = (f32[408,128]{1,0:T(8,128)S(1)}, f32[408,128]{1,0:T(8,128)S(1)}, u32[]{:S(2)}, u32[]{:S(2)}) collective-permute-start(f32[408,128]{1,0:T(8,128)S(1)} %get-tuple-element.65), channel_id=1, source_target_pairs={{1,2},{2,1},{3,4},{4,3},{5,6},{6,5},{7,8},{8,7},{9,10},{10,9},{11,... | collective-permute-start | bytes 626696 | tf_op jit(solution)/shard_map/ppermute | solution.py:536
  27.0 9.6 %shard_map.111.refs_0_ = f32[752,1024]{1,0:T(8,128)S(1)} custom-call(f32[5,2,8,8]{3,2,1,0:T(8,128)S(1)} %copy-done.1, f32[8,384,128]{2,1,0:T(8,128)S(1)} %get-tuple-element.56.q0, f32[8,192,128]{2,1,0:T(8,128)S(1)} %get-tuple-element.57.s1, f32[8,96,128]{2,1,0:T(8,128)S(1)} %get-tuple-element.58.s2, f32[8,48,128]{2,1,0:T(8,128)S(1)} %get-tuple-element.59.s3, ...), custom_call_target="tpu_custom_call" | custom-call | tf_op jit(solution)/shard_map/pallas_call | solution.py:537
  36.6 0.0 collective-permute-done.3.refs_1_
  36.6 0.0 collective-permute-done.4.refs_2_
  36.6 6.8 %shard_map.112 = (f32[8,384,128]{2,1,0:T(8,128)}, f32[8,128]{1,0:T(8,128)S(1)}, f32[8,128]{1,0:T(8,128)S(1)}, f32[8,128]{1,0:T(8,128)S(1)}, f32[8,128]{1,0:T(8,128)S(1)}) custom-call(f32[752,1024]{1,0:T(8,128)S(1)} %shard_map.111.refs_0_, f32[408,128]{1,0:T(8,128)S(1)} %collective-permute-done.3.refs_1_, f32[408,128]{1,0:T(8,128)S(1)} %collective-permute-done.4.refs_2_, ...), custom_call_target="tpu_custom_call" | custom-call | tf_op jit(solution)/shard_map/pallas_call | solution.py:547
  43.4 3.7 %collective-permute-start.5 = (f32[8,128]{1,0:T(8,128)S(1)}, f32[8,128]{1,0:T(8,128)S(1)}, u32[]{:S(2)}, u32[]{:S(2)}) collective-permute-start(f32[8,128]{1,0:T(8,128)S(1)} %get-tuple-element.81), channel_id=1, source_target_pairs={{0,1},{1,0},{2,3},{3,2},{4,5},{5,4},{6,7},{7,6},{8,9},{9,8},{10,11... | collective-permute-start | bytes 12296 | tf_op jit(solution)/shard_map/ppermute | solution.py:559
  47.1 1.4 %collective-permute-start.6 = (f32[8,128]{1,0:T(8,128)S(1)}, f32[8,128]{1,0:T(8,128)S(1)}, u32[]{:S(2)}, u32[]{:S(2)}) collective-permute-start(f32[8,128]{1,0:T(8,128)S(1)} %get-tuple-element.82), channel_id=1, source_target_pairs={{0,2},{1,3},{2,0},{3,1},{4,6},{5,7},{6,4},{7,5},{8,10},{9,11},{10,... | collective-permute-start | bytes 12296 | tf_op jit(solution)/shard_map/ppermute | solution.py:559
  48.5 0.0 collective-permute-start.7
  48.5 0.0 collective-permute-done.5.b1
  48.5 2.2 %collective-permute-done.6.b2 = f32[8,128]{1,0:T(8,128)S(1)} collective-permute-done((f32[8,128]{1,0:T(8,128)S(1)}, f32[8,128]{1,0:T(8,128)S(1)}, u32[]{:S(2)}, u32[]{:S(2)}) %collective-permute-start.6) | collective-permute-done | bytes 4128 | tf_op jit(solution)/shard_map/ppermute | solution.py:559
  50.7 0.8 %collective-permute-done.7.b3 = f32[8,128]{1,0:T(8,128)S(1)} collective-permute-done((f32[8,128]{1,0:T(8,128)S(1)}, f32[8,128]{1,0:T(8,128)S(1)}, u32[]{:S(2)}, u32[]{:S(2)}) %collective-permute-start.7) | collective-permute-done | bytes 4128 | tf_op jit(solution)/shard_map/ppermute | solution.py:559
  51.5 1.0 %shard_map.113 = f32[1,1024]{1,0:T(1,128)} custom-call(s32[1]{0:T(128)S(6)} %copy.11.count_ref, f32[8,256]{1,0:T(8,128)S(1)} %get-tuple-element.79.slot_ref, f32[8,128]{1,0:T(8,128)S(1)} %get-tuple-element.80.b0, f32[8,128]{1,0:T(8,128)S(1)} %collective-permute-done.5.b1, f32[8,128]{1,0:T(8,128)S(1)} %collective-permute-done.6.b2, ...), custom_call_target="tpu_custom_call" | custom-call | tf_op jit(solution)/shard_map/pallas_call | solution.py:560
Async XLA Ops:
  1.3 1.0 %copy-start = (f32[1024,128]{1,0:T(8,128)S(1)}, f32[1024,128]{1,0:T(8,128)}, u32[]{:S(2)}) copy-start(f32[1024,128]{1,0:T(8,128)} %cells_hbm.1) | copy-start | bytes 1572868
  2.3 0.8 %copy-start.2 = (f32[8,1024]{1,0:T(8,128)S(1)}, f32[8,1024]{1,0:T(8,128)}, u32[]{:S(2)}) copy-start(f32[8,1024]{1,0:T(8,128)} %planes_hbm.1) | copy-start | bytes 98308
  3.1 0.7 %copy-start.5 = (f32[1024]{0:T(1024)S(1)}, f32[1024]{0:T(1024)}, u32[]{:S(2)}) copy-start(f32[1024]{0:T(1024)} %param.9) | copy-start | bytes 12292
  3.8 0.7 %copy-start.6 = (s32[256,1]{0,1:T(1,128)S(1)}, s32[256,1]{0,1:T(1,128)}, u32[]{:S(2)}) copy-start(s32[256,1]{0,1:T(1,128)} %param.12) | copy-start | bytes 3076
  4.4 0.7 %copy-start.7 = (s32[256]{0:T(256)S(1)}, s32[256]{0:T(256)}, u32[]{:S(2)}) copy-start(s32[256]{0:T(256)} %param.13) | copy-start | bytes 3076
  6.3 8.8 %collective-permute-start.2 = (f32[432,128]{1,0:T(8,128)S(1)}, f32[432,128]{1,0:T(8,128)S(1)}, u32[]{:S(2)}, u32[]{:S(2)}) collective-permute-start(f32[432,128]{1,0:T(8,128)S(1)} %get-tuple-element.49), channel_id=1, source_target_pairs={{0,3},{1,2},{2,1},{3,0},{4,7},{5,6},{6,5},{7,4},{8,11},{9,10},{10,... | collective-permute-start | bytes 663560 | tf_op jit(solution)/shard_map/ppermute | solution.py:494
  8.8 10.7 %collective-permute-start.1 = (f32[432,128]{1,0:T(8,128)S(1)}, f32[432,128]{1,0:T(8,128)S(1)}, u32[]{:S(2)}, u32[]{:S(2)}) collective-permute-start(f32[432,128]{1,0:T(8,128)S(1)} %get-tuple-element.47), channel_id=1, source_target_pairs={{0,2},{1,3},{2,0},{3,1},{4,6},{5,7},{6,4},{7,5},{8,10},{9,11},{10,... | collective-permute-start | bytes 663560 | tf_op jit(solution)/shard_map/ppermute | solution.py:494
  9.4 10.8 %collective-permute-start = (f32[432,128]{1,0:T(8,128)S(1)}, f32[432,128]{1,0:T(8,128)S(1)}, u32[]{:S(2)}, u32[]{:S(2)}) collective-permute-start(f32[432,128]{1,0:T(8,128)S(1)} %get-tuple-element.45), channel_id=1, source_target_pairs={{0,1},{1,0},{2,3},{3,2},{4,5},{5,4},{6,7},{7,6},{8,9},{9,8},{10,11... | collective-permute-start | bytes 663560 | tf_op jit(solution)/shard_map/ppermute | solution.py:494
  10.1 0.8 %copy-start.1 = (f32[5,2,8,8]{3,2,1,0:T(8,128)S(1)}, f32[5,2,8,8]{3,2,1,0:T(8,128)}, u32[]{:S(2)}) copy-start(f32[5,2,8,8]{3,2,1,0:T(8,128)} %mix_ref.3) | copy-start | bytes 7684
  10.9 0.7 %copy-start.3 = (f32[5,2,17]{2,1,0:T(2,128)S(1)}, f32[5,2,17]{2,1,0:T(2,128)}, u32[]{:S(2)}) copy-start(f32[5,2,17]{2,1,0:T(2,128)} %across_ref.1) | copy-start | bytes 2044
  11.6 0.7 %copy-start.4 = (f32[5,2,17]{2,1,0:T(2,128)S(1)}, f32[5,2,17]{2,1,0:T(2,128)}, u32[]{:S(2)}) copy-start(f32[5,2,17]{2,1,0:T(2,128)} %along_ref.1) | copy-start | bytes 2044
  26.0 10.6 %collective-permute-start.3 = (f32[408,128]{1,0:T(8,128)S(1)}, f32[408,128]{1,0:T(8,128)S(1)}, u32[]{:S(2)}, u32[]{:S(2)}) collective-permute-start(f32[408,128]{1,0:T(8,128)S(1)} %get-tuple-element.64), channel_id=1, source_target_pairs={{0,1},{1,0},{2,3},{3,2},{4,5},{5,4},{6,7},{7,6},{8,9},{9,8},{10,11... | collective-permute-start | bytes 626696 | tf_op jit(solution)/shard_map/ppermute | solution.py:535
  26.1 10.5 %collective-permute-start.4 = (f32[408,128]{1,0:T(8,128)S(1)}, f32[408,128]{1,0:T(8,128)S(1)}, u32[]{:S(2)}, u32[]{:S(2)}) collective-permute-start(f32[408,128]{1,0:T(8,128)S(1)} %get-tuple-element.65), channel_id=1, source_target_pairs={{1,2},{2,1},{3,4},{4,3},{5,6},{6,5},{7,8},{8,7},{9,10},{10,9},{11,... | collective-permute-start | bytes 626696 | tf_op jit(solution)/shard_map/ppermute | solution.py:536
  43.4 5.1 %collective-permute-start.5 = (f32[8,128]{1,0:T(8,128)S(1)}, f32[8,128]{1,0:T(8,128)S(1)}, u32[]{:S(2)}, u32[]{:S(2)}) collective-permute-start(f32[8,128]{1,0:T(8,128)S(1)} %get-tuple-element.81), channel_id=1, source_target_pairs={{0,1},{1,0},{2,3},{3,2},{4,5},{5,4},{6,7},{7,6},{8,9},{9,8},{10,11... | collective-permute-start | bytes 12296 | tf_op jit(solution)/shard_map/ppermute | solution.py:559
  47.1 3.6 %collective-permute-start.6 = (f32[8,128]{1,0:T(8,128)S(1)}, f32[8,128]{1,0:T(8,128)S(1)}, u32[]{:S(2)}, u32[]{:S(2)}) collective-permute-start(f32[8,128]{1,0:T(8,128)S(1)} %get-tuple-element.82), channel_id=1, source_target_pairs={{0,2},{1,3},{2,0},{3,1},{4,6},{5,7},{6,4},{7,5},{8,10},{9,11},{10,... | collective-permute-start | bytes 12296 | tf_op jit(solution)/shard_map/ppermute | solution.py:559
  48.5 3.0 %collective-permute-start.7 = (f32[8,128]{1,0:T(8,128)S(1)}, f32[8,128]{1,0:T(8,128)S(1)}, u32[]{:S(2)}, u32[]{:S(2)}) collective-permute-start(f32[8,128]{1,0:T(8,128)S(1)} %get-tuple-element.83), channel_id=1, source_target_pairs={{0,3},{1,2},{2,1},{3,0},{4,7},{5,6},{6,5},{7,4},{8,11},{9,10},{10,... | collective-permute-start | bytes 12296 | tf_op jit(solution)/shard_map/ppermute | solution.py:559

commit v4 on v3

--- a/solution.py
+++ b/solution.py
@@ -27,10 +27,12 @@
 STEP = (384, 192, 96, 48, 32)
 ROW_OF = (0, 384, 576, 672, 720)
 ALL_ROWS = 752
+TAP_ROW = (0, 768, 1152, 1344, 1440)
 K_OF = (0, 768, 1152, 1344, 1440)
 ALL_K = 1504
-RIM_ROW = (0, 0, 192, 288, 384)
-RIM_ROWS = NY + HEIGHTS[LEVELS]
+RIM_ROW = (0, 0, 192, 288, 336)
+MIX_ROW = tuple(PLANES * sum(HEIGHTS[:level]) for level in range(LEVELS + 1))
+MIX_ROWS = PLANES * sum(HEIGHTS)
 F32 = jnp.float32
 BF16 = jnp.bfloat16
 
@@ -59,18 +61,11 @@
 
 def swap_groups(bands):
     group = iota((1, CX), 1) // 16
+    bands = [turn(band, 16 * i) for i, band in enumerate(bands)]
     for bit in range(3):
-        step = 1 << bit
         upper = ((group >> bit) & 1) == 1
-        fresh = []
-        for i in range(8):
-            other = bands[i ^ step]
-            if i & step:
-                fresh.append(jnp.where(upper, bands[i], turn(other, -16 * step)))
-            else:
-                fresh.append(jnp.where(upper, turn(other, 16 * step), bands[i]))
-        bands = fresh
-    return bands
+        bands = [jnp.where(upper, bands[(i + (1 << bit)) % 8], bands[i]) for i in range(8)]
+    return [turn(bands[-i % 8], -16 * i) for i in range(8)]
 
 
 def route_kernel(
@@ -134,16 +129,9 @@
 
 
 def rim_of(lane, level):
-    if level == LEVELS:
-        j, rest = lane >> 4, lane & 15
-        return rest & 7, jnp.where(rest < 8, j - REACH, j + WIDTHS[level])
-    spot = lane if level == 0 else lane ^ (CX // 2)
-    log = level + 3
-    rest = spot & ((8 << level) - 1)
-    j, offset = rest >> level, rest & ((1 << level) - 1)
-    first = spot < CX // 2
-    block = jnp.where(first, spot >> log, (CX - 1 - spot) >> log)
-    return (block << level) + offset, jnp.where(first, j + WIDTHS[level], j - REACH)
+    j = lane & 7
+    before = (lane < CX // 2) == (level == 0)
+    return (lane >> 3) & 7, jnp.where(before, j - REACH, j + WIDTHS[level])
 
 
 def taps_at(table, shift):
@@ -152,8 +140,8 @@
 
 
 def prep_kernel(
-    across_ref, along_ref, mix_ref, own_ref, own_low_ref, across_high, across_low, blend_high,
-    blend_low, rim_high, rim_low, table
+    across_ref, along_ref, mix_ref, own_ref, own_low_ref, across, blend_high, blend_low,
+    rim_high, rim_low, gather, table
 ):
     exact = lax.Precision.HIGHEST
     table[...] = jnp.zeros(table.shape, F32)
@@ -165,13 +153,18 @@
     for level in range(LEVELS + 1):
         scale = 0.25**level
         row = iota((CX, 1), 0)
-        mark = jnp.where((row & ((1 << level) - 1)) == 0, row >> level, 4 * NY)
+        mark = row >> level
         lane_z, lane_place = rim_of(row, level)
         line_z, line_place = rim_of(iota((1, CX), 1), level)
         column = iota((CX, CX), 1) >> level
         shift = mark - column + REACH
         rim_shift = lane_place - column + REACH
         same = lane_place == line_place
+        edge = jnp.where(line_place < 0, line_place + WIDTHS[level], line_place - WIDTHS[level])
+        for z in range(PLANES):
+            chosen = flags((mark == edge) & (line_z == z))
+            gather[level * PLANES + z, :CX, :] = chosen
+            gather[level * PLANES + z, CX:, :] = chosen
         pick = (lane_z == iota((CX, 8), 1)).astype(F32)
         pick_t = (line_z == iota((8, CX), 0)).astype(F32)
         masks = [
@@ -198,7 +191,8 @@
             blend_high[level, :, part] = high
             blend_low[level, :, part] = low
         size, step = HEIGHTS[level], STEP[level]
-        rows = slice(ROW_OF[level], ROW_OF[level] + size)
+        upper = slice(TAP_ROW[level], TAP_ROW[level] + size)
+        lower = slice(TAP_ROW[level] + step, TAP_ROW[level] + step + size)
         mine = height_of(iota((size, 1), 0), level)
         first = table[4 * level + 2 : 4 * level + 3, :]
         both = first + turn(table[4 * level + 3 : 4 * level + 4, :], 32)
@@ -214,11 +208,11 @@
             )
             taps = jnp.take_along_axis(jnp.broadcast_to(both, spot.shape), spot, axis=1)
             high, low = split(taps[:, :lanes])
-            across_high[rows, start : start + lanes] = high
-            across_low[rows, start : start + lanes] = low
-
-
-def brick_kernel(ref, bricks, hot, match, weights):
+            across[upper, start : start + lanes] = high
+            across[lower, start : start + lanes] = low
+
+
+def brick_products(ref, match, weights, bricks):
     packed = ref[CELLS:, :]
     meta = jnp.concatenate([packed, turn(packed, CX // 2)], axis=0)
     cells = [ref[s * CAP : (s + 1) * CAP, :] for s in range(SLOTS)]
@@ -230,124 +224,137 @@
             weights[s * PLANES + z] = piece
             piece = piece * current
             totals[z] = piece if s == 0 else totals[z] + piece
+    blank = jnp.zeros((CX - CAP, HALF), BF16)
+    bricks[CAP:CX, :] = blank
+    bricks[CX + CAP :, :] = blank
     for z in range(PLANES):
         high, low = split(totals[z])
         bricks[:CAP, z * CX : (z + 1) * CX] = high
-        bricks[:CAP, HALF + z * CX : HALF + (z + 1) * CX] = low
-    bricks[CAP:, :] = jnp.zeros((CX - CAP, 2 * HALF), BF16)
+        bricks[CX : CX + CAP, z * CX : (z + 1) * CX] = low
     whole = jnp.concatenate([meta, jnp.zeros((CX - CAP, CX), F32)], axis=0)
     names = jnp.where(iota((1, CX), 1) < CAP, whole.T[9:10, :], -1.0)
-    hot[...] = flags(iota((TILES, CX), 0).astype(F32) == names)
     match[...] = flags(iota((CAP, TILES), 1).astype(F32) == meta[:, 9:10])
-
-
-def charge_kernel(*refs):
-    bricks, hots = refs[:PEERS], refs[PEERS : 2 * PEERS]
-    q0, s1, s2, s3, s4, to_pair, to_next = refs[2 * PEERS + 1 : -4]
-    rims = refs[-4:]
-    hot = jnp.concatenate([ref[...] for ref in hots], axis=1)
+    hot = flags(iota((TILES, CX), 0).astype(F32) == names)
+    return jnp.concatenate([hot, hot], axis=1)
+
+
+def brick_kernel(ref, *refs):
+    match, weights, total, bricks = refs[-4:]
+    hot = brick_products(ref, match, weights, bricks)
+    for pair in range(PLANES // 2):
+        part = slice(pair * 2 * CX, (pair + 1) * 2 * CX)
+        found = dot(hot, bricks[:, part])
+        total[:, part] = refs[0][:, part] + found if len(refs) > 4 else found
+
+
+def charge_kernel(
+    ref, partial, gather, match, weights, q0, s1, s2, s3, s4, to_pair, to_next, bricks, *rims
+):
+    hot = brick_products(ref, match, weights, bricks)
     lanes = iota((1, CX), 1)
     for pair in range(PLANES // 2):
         part = slice(pair * 2 * CX, (pair + 1) * 2 * CX)
-        lower = slice(HALF + pair * 2 * CX, HALF + (pair + 1) * 2 * CX)
-        found = dot(hot, jnp.concatenate([ref[:, part] for ref in bricks], axis=0)) + dot(
-            hot, jnp.concatenate([ref[:, lower] for ref in bricks], axis=0)
-        )
+        found = partial[:, part] + dot(hot, bricks[:, part])
         for i in range(2):
             z = 2 * pair + i
             plane = found[:, i * CX : (i + 1) * CX]
             bands = swap_groups([plane[b * BAND : (b + 1) * BAND] for b in range(8)])
-            level = 0
-            while True:
-                size, log = HEIGHTS[level], level + 3
-                target = (q0, s1, s2, s3)[level]
-                for b, band in enumerate(bands):
-                    rows = slice(b * BAND, (b + 1) * BAND)
-                    target[z, rows, :] = band
-                    block, offset = z >> level, z & ((1 << level) - 1)
-                    first = turn(band, (block << log) + offset)
-                    last = turn(band, offset - (block << log)) if block else first
-                    mine = (lanes & ((1 << level) - 1)) == offset
-                    left = mine & ((lanes >> log) == block) & (lanes < CX // 2)
-                    right = mine & (((CX - 1 - lanes) >> log) == block) & (lanes >= CX // 2)
-                    held = rims[level][rows, :] if z else jnp.zeros((BAND, CX), F32)
-                    held = jnp.where(left, first, jnp.where(right, last, held))
-                    rims[level][rows, :] = held
-                if level == 3:
-                    break
-                sums = [bands[2 * b] + bands[2 * b + 1] for b in range(len(bands) // 2)]
-                bands = [value + turn(value, -(1 << level)) for value in sums]
-                level += 1
+            for level in range(LEVELS):
+                plain = jnp.concatenate(bands, axis=0)
+                (q0, s1, s2, s3)[level][z] = plain
+                found_rims = dot(
+                    jnp.concatenate(split(plain), axis=1), gather[level * PLANES + z]
+                )
+                rims[level][...] = rims[level][...] + found_rims if z else found_rims
+                bands = [bands[2 * b] + bands[2 * b + 1] for b in range(len(bands) // 2)]
     size = HEIGHTS[LEVELS]
     coarse = jnp.zeros((size, CX), F32)
     for z in range(PLANES):
         value = s3[z, pl.ds(0, size, stride=2), :] + s3[z, pl.ds(1, size, stride=2), :]
-        value = value + turn(value, -8)
         s4[z] = value
-        coarse = jnp.where((lanes & 15) == z, turn(value, z), coarse)
+        coarse = coarse + dot(
+            jnp.concatenate(split(value), axis=1), gather[LEVELS * PLANES + z]
+        )
     even = (lax.axis_index("sect") & 1) == 0
-    to_pair[NY:, :] = coarse
-    to_next[NY:, :] = coarse
-    for level in range(1, LEVELS + 1):
+    for level in range(1, LEVELS + 2):
         if level < LEVELS:
             rows = slice(RIM_ROW[level], RIM_ROW[level] + HEIGHTS[level])
-            other = turn(rims[level][...], CX // 2)
+            other = rims[level][...]
+        elif level == LEVELS:
+            rows, other = slice(RIM_ROW[level], RIM_ROW[level] + size), coarse
         else:
-            rows = slice(RIM_ROW[3] + HEIGHTS[3], NY)
-            other = jnp.zeros((NY - RIM_ROW[3] - HEIGHTS[3], CX), F32)
-        right = jnp.where(lanes < CX // 2, other, rims[0][rows, :])
-        left = jnp.where(lanes < CX // 2, rims[0][rows, :], other)
+            rows = slice(RIM_ROW[LEVELS] + size, NY)
+            other = jnp.zeros((NY - RIM_ROW[LEVELS] - size, CX), F32)
+        right = jnp.where(lanes < CX // 2, rims[0][rows, :], other)
+        left = jnp.where(lanes < CX // 2, other, rims[0][rows, :])
         to_pair[rows, :] = jnp.where(even, right, left)
         to_next[rows, :] = jnp.where(even, left, right)
 
 
 def inner_kernel(
-    mix_ref, q0, s1, s2, s3, s4, own_ref, own_low_ref, across_high, across_low, out_ref, ranked,
-    high_ref, low_ref
+    mix_ref, q0, s1, s2, s3, s4, own_ref, own_low_ref, across, out_ref, ranked, high_ref, low_ref
 ):
-    for level, source in enumerate((q0, s1, s2, s3, s4)):
+    sources = (q0, s1, s2, s3, s4)
+
+    def along(level):
+        size = HEIGHTS[level]
+        for z in range(PLANES):
+            high, low = split(sources[level][z])
+            found = dot(jnp.concatenate([high, low], axis=1), own_ref[level])
+            rows = slice(MIX_ROW[level] + z * size, MIX_ROW[level] + (z + 1) * size)
+            ranked[rows, :] = found + dot(high, own_low_ref[level])
+
+    def blend(level, r):
         size, step = HEIGHTS[level], STEP[level]
-        for z in range(PLANES):
-            high, low = split(source[z])
-            ranked[z, :size, :] = dot(
-                jnp.concatenate([high, low], axis=1), own_ref[level]
-            ) + dot(high, own_low_ref[level])
-        chunk = {384: 64, 192: 64, 96: 48, 48: 48, 24: 24}[size]
+        chunk = 24 if size < 32 else (48 if size == 48 else 32)
+        chunk = 16 if chunk == 48 else chunk
+        for start in range(0, size, chunk):
+            parts = []
+            for w in range(PLANES):
+                line = MIX_ROW[level] + w * size + start
+                parts.append(ranked[line : line + chunk, r * CX : (r + 1) * CX])
+            for z in range(PLANES):
+                total = parts[0] * mix_ref[level, r, z, 0]
+                for w in range(1, PLANES):
+                    total = total + parts[w] * mix_ref[level, r, z, w]
+                if chunk == 24:
+                    total = jnp.concatenate([total, jnp.zeros((8, CX), F32)], axis=0)
+                high, low = split(total)
+                line = TAP_ROW[level] + r * step + start
+                high_ref[line : line + high.shape[0], z * CX : (z + 1) * CX] = high
+                low_ref[line : line + high.shape[0], z * CX : (z + 1) * CX] = low
+
+    def combine(level):
+        size, step = HEIGHTS[level], STEP[level]
         rows = slice(ROW_OF[level], ROW_OF[level] + size)
-        heavy, light = across_high[rows, : 2 * step], across_low[rows, : 2 * step]
+        lines = slice(TAP_ROW[level], TAP_ROW[level] + 2 * step)
+        taps = across[lines, : 2 * step]
         for pair in range(PLANES // 2):
-            for r in range(2):
-                weights = [
-                    [mix_ref[level, r, 2 * pair + i, w] for w in range(PLANES)] for i in range(2)
-                ]
-                for start in range(0, size, chunk):
-                    for i in range(2):
-                        total = None
-                        for w in range(PLANES):
-                            part = ranked[w, start : start + chunk, r * CX : (r + 1) * CX]
-                            part = part * weights[i][w]
-                            total = part if w == 0 else total + part
-                        if chunk == 24:
-                            total = jnp.concatenate([total, jnp.zeros((8, CX), F32)], axis=0)
-                        high, low = split(total)
-                        place = slice(r * step + start, r * step + start + high.shape[0])
-                        column = slice((2 * pair + i) * CX, (2 * pair + i + 1) * CX)
-                        high_ref[place, column] = high
-                        low_ref[place, column] = low
             part = slice(pair * 2 * CX, (pair + 1) * 2 * CX)
-            high = high_ref[: 2 * step, part]
-            out_ref[rows, part] = (
-                dot(heavy, high) + dot(heavy, low_ref[: 2 * step, part]) + dot(light, high)
-            )
+            found = dot(taps, high_ref[lines, part])
+            found = found[:size] + found[step : step + size]
+            out_ref[rows, part] = found + dot(taps[:step], low_ref[lines, part])[:size]
+
+    along(0)
+    blend(0, 0)
+    blend(0, 1)
+    for level in range(1, LEVELS + 1):
+        along(level)
+    combine(0)
+    for level in range(1, LEVELS + 1):
+        blend(level, 0)
+        blend(level, 1)
+    for level in range(1, LEVELS + 1):
+        combine(level)
 
 
 def outer_kernel(*refs):
-    inner, by_pair, by_next, across_high, across_low = refs[:5]
-    blend_high, blend_low, rim_high, rim_low = refs[5:9]
-    matches, weights = refs[9 : 9 + PEERS], refs[9 + PEERS : 9 + 2 * PEERS]
-    grid_ref = refs[9 + 2 * PEERS]
-    outs = refs[10 + 2 * PEERS : 10 + 3 * PEERS]
-    high_ref, low_ref, tiles, picked, doubled = refs[10 + 3 * PEERS :]
+    inner, by_pair, by_next, across = refs[:4]
+    blend_high, blend_low, rim_high, rim_low = refs[4:8]
+    matches, weights = refs[8 : 8 + PEERS], refs[8 + PEERS : 8 + 2 * PEERS]
+    grid_ref = refs[8 + 2 * PEERS]
+    outs = refs[9 + 2 * PEERS : 9 + 3 * PEERS]
+    high_ref, low_ref, tiles, picked, doubled = refs[9 + 3 * PEERS :]
     lanes = iota((1, CX), 1)
     even = (lax.axis_index("sect") & 1) == 0
     high_ref[...] = jnp.zeros((ALL_K, 2 * CX), BF16)
@@ -359,11 +366,9 @@
         from_left = jnp.where(even, by_next[rows, :], by_pair[rows, :])
         from_right = jnp.where(even, by_pair[rows, :], by_next[rows, :])
         if level == 0:
-            rims = jnp.where(lanes < CX // 2, from_right, from_left)
-        elif level < LEVELS:
             rims = jnp.where(lanes < CX // 2, from_left, from_right)
         else:
-            rims = jnp.where((lanes & 15) < 8, from_left, turn(from_right, 8))
+            rims = jnp.where(lanes < CX // 2, from_right, from_left)
         high, low = split(rims)
         mixed = dot(high, blend_high[level]) + dot(low, blend_high[level])
         mixed = mixed + dot(high, blend_low[level])
@@ -375,18 +380,19 @@
             place = slice(K_OF[level] + r * step, K_OF[level] + (r + 1) * step)
             high_ref[place, part] = high[:, part]
             low_ref[place, part] = low[:, part]
-        rows = slice(ROW_OF[level], ROW_OF[level] + size)
         place = slice(K_OF[level], K_OF[level] + 2 * step)
-        heavy, light = across_high[rows, : 2 * step], across_low[rows, : 2 * step]
-        total = dot(heavy, high_ref[place, :]) + dot(heavy, low_ref[place, :])
-        sums.append(split(total + dot(light, high_ref[place, :])))
+        taps = across[TAP_ROW[level] : TAP_ROW[level] + 2 * step, : 2 * step]
+        found = dot(taps, high_ref[place, :])
+        found = found[:step] + found[step:] + dot(taps[:step], low_ref[place, :])
+        sums.append(jnp.concatenate(split(found), axis=0))
     for pair in range(PLANES // 2):
         part = slice(pair * 2 * CX, (pair + 1) * 2 * CX)
         above = None
         for level in range(LEVELS, -1, -1):
-            high, low = sums[level]
-            heavy, light = rim_high[level, :, part], rim_low[level, :, part]
-            value = dot(high, heavy) + dot(low, heavy) + dot(high, light)
+            size, step = HEIGHTS[level], STEP[level]
+            value = dot(sums[level], rim_high[level, :, part])
+            value = value[:size] + value[step : step + size]
+            value = value + dot(sums[level][:step], rim_low[level, :, part])[:size]
             value = value + inner[ROW_OF[level] : ROW_OF[level] + HEIGHTS[level], part]
             if level == LEVELS:
                 doubled[pl.ds(0, HEIGHTS[level], stride=2), :] = value[:, :CX]
@@ -410,17 +416,18 @@
                 rows = slice(b * BAND, (b + 1) * BAND)
                 tiles[rows, z * CX : (z + 1) * CX] = high
                 tiles[rows, HALF + z * CX : HALF + (z + 1) * CX] = low
+    match = jnp.concatenate([ref[...] for ref in matches], axis=0)
+    for pair in range(PLANES // 2):
+        part = slice(pair * 2 * CX, (pair + 1) * 2 * CX)
+        lower = slice(HALF + pair * 2 * CX, HALF + (pair + 1) * 2 * CX)
+        picked[:, part] = dot(match, tiles[:, part]) + dot(match, tiles[:, lower])
     for j in range(PEERS):
-        match = matches[j][...]
-        for pair in range(PLANES // 2):
-            part = slice(pair * 2 * CX, (pair + 1) * 2 * CX)
-            lower = slice(HALF + pair * 2 * CX, HALF + (pair + 1) * 2 * CX)
-            picked[:, part] = dot(match, tiles[:, part]) + dot(match, tiles[:, lower])
+        mine = slice(j * CAP, (j + 1) * CAP)
         values = jnp.zeros((CAP, CX), F32)
         for s in range(SLOTS):
-            total = picked[:, :CX] * weights[j][s * PLANES]
+            total = picked[mine, :CX] * weights[j][s * PLANES]
             for z in range(1, PLANES):
-                total = total + picked[:, z * CX : (z + 1) * CX] * weights[j][s * PLANES + z]
+                total = total + picked[mine, z * CX : (z + 1) * CX] * weights[j][s * PLANES + z]
             values = jnp.where(lanes == s, jnp.sum(total, axis=1, keepdims=True), values)
         values = jnp.concatenate([values, jnp.zeros((CX - CAP, CX), F32)], axis=0)
         outs[j][...] = values.T[:8, :]
@@ -498,36 +505,37 @@
         [
             shape(LEVELS + 1, 2 * CX, 2 * CX, kind=BF16),
             shape(LEVELS + 1, CX, 2 * CX, kind=BF16),
-            shape(ALL_ROWS, 2 * NY, kind=BF16),
-            shape(ALL_ROWS, 2 * NY, kind=BF16),
+            shape(ALL_K, 2 * NY, kind=BF16),
             shape(LEVELS + 1, CX, 2 * CX, kind=BF16),
             shape(LEVELS + 1, CX, 2 * CX, kind=BF16),
             shape(LEVELS + 1, 2 * CX, HALF, kind=BF16),
             shape(LEVELS + 1, 2 * CX, HALF, kind=BF16),
+            shape((LEVELS + 1) * PLANES, 2 * CX, CX, kind=BF16),
         ],
         [pltpu.VMEM((24, CX), F32)],
     )(kern_across, kern_along, plane_mix)
-    own, own_low, across_high, across_low, *outer = prepared
-    parts = [
-        call(
+    own, own_low, across, *outer, gather = prepared
+    kept = [shape(CAP, TILES, kind=BF16), shape(SLOTS * PLANES, CAP, CX)]
+    products = pltpu.VMEM((2 * CX, HALF), BF16)
+    matches, weights, total = [], [], []
+    for value in held[:-1]:
+        match, weight, partial = call(
             brick_kernel,
-            [VMEM],
-            [
-                shape(CX, 2 * HALF, kind=BF16),
-                shape(TILES, CX, kind=BF16),
-                shape(CAP, TILES, kind=BF16),
-                shape(SLOTS * PLANES, CAP, CX),
-            ],
-        )(value)
-        for value in held
-    ]
-    bricks, hots, matches, weights = zip(*parts)
-    *fields, to_pair, to_next = call(
+            [VMEM] * (1 + len(total)),
+            kept + [shape(TILES, HALF)],
+            [products],
+        )(value, *total)
+        matches.append(match)
+        weights.append(weight)
+        total = [partial]
+    match, weight, *fields, to_pair, to_next = call(
         charge_kernel,
-        [VMEM] * 8 + [ANY],
-        [shape(PLANES, size, CX) for size in HEIGHTS] + [shape(RIM_ROWS, CX)] * 2,
-        [pltpu.VMEM((size, CX), F32) for size in HEIGHTS[:LEVELS]],
-    )(*bricks, *hots, own)
+        [VMEM] * 3,
+        kept + [shape(PLANES, size, CX) for size in HEIGHTS] + [shape(NY, CX)] * 2,
+        [products] + [pltpu.VMEM((size, CX), F32) for size in HEIGHTS[:LEVELS]],
+    )(held[-1], *total, gather)
+    matches.append(match)
+    weights.append(weight)
     axes = ("strip", "sect")
     devices = lax.axis_size(axes)
     paired = [(i, i ^ 1) for i in range(devices)]
@@ -536,26 +544,27 @@
     by_next = lax.ppermute(to_next, axes, crossed)
     (inner,) = call(
         inner_kernel,
-        [SMEM] + [VMEM] * 9,
+        [SMEM] + [VMEM] * 8,
         [shape(ALL_ROWS, HALF)],
         [
-            pltpu.VMEM((PLANES, NY, 2 * CX), F32),
-            pltpu.VMEM((2 * NY, HALF), BF16),
-            pltpu.VMEM((2 * NY, HALF), BF16),
+            pltpu.VMEM((MIX_ROWS, 2 * CX), F32),
+            pltpu.VMEM((ALL_K, HALF), BF16),
+            pltpu.VMEM((ALL_K, HALF), BF16),
         ],
-    )(plane_mix, *fields, own, own_low, across_high, across_low)
+        megabytes=24,
+    )(plane_mix, *fields, own, own_low, across)
     grid, *samples = call(
         outer_kernel,
-        [VMEM] * (9 + 2 * PEERS),
+        [VMEM] * (8 + 2 * PEERS),
         [shape(PLANES, NY, CX)] + [shape(8, CX)] * PEERS,
         [
             pltpu.VMEM((ALL_K, 2 * CX), BF16),
             pltpu.VMEM((ALL_K, 2 * CX), BF16),
             pltpu.VMEM((TILES, 2 * HALF), BF16),
-            pltpu.VMEM((CAP, HALF), F32),
+            pltpu.VMEM((PEERS * CAP, HALF), F32),
             pltpu.VMEM((2 * BAND, CX), F32),
         ],
-    )(inner, by_pair, by_next, across_high, across_low, *outer, *matches, *weights)
+    )(inner, by_pair, by_next, across, *outer, *matches, *weights)
     back = [samples[0]] + [lax.ppermute(samples[k], "sect", swaps[k]) for k in range(1, PEERS)]
     (segments,) = call(
         pick_kernel, [SMEM] + [VMEM] * 5, [shape(1, SEGS)]

time: 52.9 us -> 47.1 us (0.89)
  Pallas kernels: 29.1 us -> 25.2 us
  waiting for transfers between devices: 6.81 us -> 5.32 us
    pallas_call x7 -> x6, Pallas kernels: 24.2 us -> 20.2 us  [the longest x1 8.23 us: body(): call(inner_kernel, [SMEM] + [VMEM] * 8, [shape(ALL_ROWS, HALF)], [pltpu.V...]
    ppermute x3, waiting for transfers between devices: 3.77 us -> 2.27 us  [body(): lax.ppermute(sends[k], 'sect', swaps[k])]
    ppermute x3, starting transfers between devices: 5.11 us -> 4.5 us  [body(): lax.ppermute(samples[k], 'sect', swaps[k])]
    unnamed x16 -> x18, local copies, waits for them, and re-layouts: 5.99 us -> 5.99 us
  transfers between devices with their start and end apart: 8 -> 8, of which waited for: 3 -> 3; matrix products, arithmetic and copies ran while one was open for 0% -> 0% of each run, Pallas kernels for 27% -> 30%
where the time goes in v4:
time: 47.1 us; the launch traced here: 46.6 us
  Pallas kernels  25.2 us (54%)
  starting transfers between devices  8.7 us (18%)
  local copies, waits for them, and re-layouts  5.99 us (13%)
  waiting for transfers between devices  5.32 us (11%)
  between operations  1.4 us (3%)
    pallas_call x1, Pallas kernels, body(): call(inner_kernel, [SMEM] + [VMEM] * 8, [shape(ALL_ROWS, HALF)], [pltpu.V...  8.23 us
    unnamed x18, local copies, waits for them, and re-layouts  5.99 us
    pallas_call x1, Pallas kernels, body(): call(outer_kernel, [VMEM] * (8 + 2 * PEERS), [shape(PLANES, NY, CX)] + [s...  5.69 us
    ppermute x3, starting transfers between devices, body(): lax.ppermute(samples[k], 'sect', swaps[k])  4.5 us
    pallas_call x1, Pallas kernels, body(): call(charge_kernel, [VMEM] * 3, kept + [shape(PLANES, size, CX) for size...  3.22 us
    ppermute x3, starting transfers between devices, body(): lax.ppermute(sends[k], 'sect', swaps[k])  3.18 us
    pallas_call x3, Pallas kernels, body(): call(brick_kernel, [VMEM] * (1 + len(total)), kept + [shape(TILES, HALF)]...  3.07 us
    ppermute x3, waiting for transfers between devices, body(): lax.ppermute(samples[k], 'sect', swaps[k])  3.03 us
  transfers between devices with their start and end apart: 8, of which 3 were waited for; matrix products, arithmetic and copies ran while one was open for 0% of the time, Pallas kernels for 30%

profile of v4, /device:TPU:0, one launch (start us, length us, event | category | flops | bytes accessed | tf_op | source)
XLA Modules:
  0.0 46.6 jit_solution(1719979144635224281)
XLA Ops:
  1.3 0.0 copy-start
  1.3 1.0 %copy-done = f32[1024,128]{1,0:T(8,128)S(1)} copy-done((f32[1024,128]{1,0:T(8,128)S(1)}, f32[1024,128]{1,0:T(8,128)}, u32[]{:S(2)}) %copy-start) | copy-done | bytes 524312
  2.3 0.0 copy-start.3
  2.3 0.8 %copy-done.3 = f32[8,1024]{1,0:T(8,128)S(1)} copy-done((f32[8,1024]{1,0:T(8,128)S(1)}, f32[8,1024]{1,0:T(8,128)}, u32[]{:S(2)}) %copy-start.3) | copy-done | bytes 32792
  3.1 0.0 copy-start.6
  3.1 0.7 %copy-done.6 = f32[1024]{0:T(1024)S(1)} copy-done((f32[1024]{0:T(1024)S(1)}, f32[1024]{0:T(1024)}, u32[]{:S(2)}) %copy-start.6) | copy-done | bytes 4120
  3.8 0.0 copy-start.7
  3.8 0.7 %copy-done.7 = s32[256,1]{0,1:T(1,128)S(1)} copy-done((s32[256,1]{0,1:T(1,128)S(1)}, s32[256,1]{0,1:T(1,128)}, u32[]{:S(2)}) %copy-start.7) | copy-done | bytes 1048
  4.4 0.0 copy-start.8
  4.4 0.7 %copy-done.8 = s32[256]{0:T(256)S(1)} copy-done((s32[256]{0:T(256)S(1)}, s32[256]{0:T(256)}, u32[]{:S(2)}) %copy-start.8) | copy-done | bytes 1048
  5.1 1.2 %shard_map.104 = (f32[432,128]{1,0:T(8,128)S(1)}, f32[432,128]{1,0:T(8,128)S(1)}, f32[432,128]{1,0:T(8,128)S(1)}, f32[432,128]{1,0:T(8,128)S(1)}, f32[8,256]{1,0:T(8,128)S(1)}) custom-call(s32[1]{0:T(128)S(6)} %copy.11.count_ref, f32[1,1024]{1,0:T(1,128)S(1)} %bitcast.4, f32[8,1024]{1,0:T(8,128)S(1)} %copy-done.3, f32[1024,128]{1,0:T(8,128)S(1)} %copy-done, ...), custom_call_target="tpu_custom_call" | custom-call | tf_op jit(solution)/shard_map/pallas_call | solution.py:479
  6.3 0.5 %collective-permute-start.2 = (f32[432,128]{1,0:T(8,128)S(1)}, f32[432,128]{1,0:T(8,128)S(1)}, u32[]{:S(2)}, u32[]{:S(2)}) collective-permute-start(f32[432,128]{1,0:T(8,128)S(1)} %get-tuple-element.40), channel_id=1, source_target_pairs={{0,1},{1,0},{2,3},{3,2},{4,5},{5,4},{6,7},{7,6},{8,9},{9,8},{10,11... | collective-permute-start | bytes 663560 | tf_op jit(solution)/shard_map/ppermute | solution.py:501
  6.8 2.6 %collective-permute-start.1 = (f32[432,128]{1,0:T(8,128)S(1)}, f32[432,128]{1,0:T(8,128)S(1)}, u32[]{:S(2)}, u32[]{:S(2)}) collective-permute-start(f32[432,128]{1,0:T(8,128)S(1)} %get-tuple-element.39), channel_id=1, source_target_pairs={{0,2},{1,3},{2,0},{3,1},{4,6},{5,7},{6,4},{7,5},{8,10},{9,11},{10,... | collective-permute-start | bytes 663560 | tf_op jit(solution)/shard_map/ppermute | solution.py:501
  9.4 0.1 collective-permute-start
  9.5 1.0 %shard_map.105 = (bf16[96,384]{1,0:T(8,128)(2,1)S(1)}, f32[32,96,128]{2,1,0:T(8,128)S(1)}, f32[384,1024]{1,0:T(8,128)S(1)}) custom-call(f32[432,128]{1,0:T(8,128)S(1)} %get-tuple-element.41.ref), custom_call_target="tpu_custom_call" | custom-call | tf_op jit(solution)/shard_map/pallas_call | solution.py:522
  10.5 0.0 copy-start.1
  10.5 0.8 %copy-done.1 = f32[5,2,8,8]{3,2,1,0:T(8,128)S(1)} copy-done((f32[5,2,8,8]{3,2,1,0:T(8,128)S(1)}, f32[5,2,8,8]{3,2,1,0:T(8,128)}, u32[]{:S(2)}) %copy-start.1) | copy-done | bytes 2584
  11.3 0.0 copy-start.4
  11.3 0.7 %copy-done.4 = f32[5,2,17]{2,1,0:T(2,128)S(1)} copy-done((f32[5,2,17]{2,1,0:T(2,128)S(1)}, f32[5,2,17]{2,1,0:T(2,128)}, u32[]{:S(2)}) %copy-start.4) | copy-done | bytes 704
  12.0 0.0 copy-start.5
  12.0 0.7 %copy-done.5 = f32[5,2,17]{2,1,0:T(2,128)S(1)} copy-done((f32[5,2,17]{2,1,0:T(2,128)S(1)}, f32[5,2,17]{2,1,0:T(2,128)}, u32[]{:S(2)}) %copy-start.5) | copy-done | bytes 704
  12.7 2.9 %shard_map.108 = (bf16[5,256,256]{2,1,0:T(8,128)(2,1)S(1)}, bf16[5,128,256]{2,1,0:T(8,128)(2,1)S(1)}, bf16[1504,768]{1,0:T(8,128)(2,1)S(1)}, bf16[5,128,256]{2,1...) custom-call(f32[5,2,17]{2,1,0:T(2,128)S(1)} %copy-done.4, ...), custom_call_target="tpu_custom_call" | custom-call | tf_op jit(solution)/shard_map/pallas_call | solution.py:502
  15.6 0.0 collective-permute-done.2.ref
  15.6 1.0 %shard_map.106 = (bf16[96,384]{1,0:T(8,128)(2,1)S(1)}, f32[32,96,128]{2,1,0:T(8,128)S(1)}, f32[384,1024]{1,0:T(8,128)S(1)}) custom-call(f32[432,128]{1,0:T(8,128)S(1)} %collective-permute-done.2.ref, f32[384,1024]{1,0:T(8,128)S(1)} %get-tuple-element.42.refs_0_), custom_call_target="tpu_custom_call" | custom-call | tf_op jit(solution)/shard_map/pallas_call | solution.py:522
  16.6 0.0 collective-permute-done.1.ref
  16.6 1.0 %shard_map.107 = (bf16[96,384]{1,0:T(8,128)(2,1)S(1)}, f32[32,96,128]{2,1,0:T(8,128)S(1)}, f32[384,1024]{1,0:T(8,128)S(1)}) custom-call(f32[432,128]{1,0:T(8,128)S(1)} %collective-permute-done.1.ref, f32[384,1024]{1,0:T(8,128)S(1)} %get-tuple-element.43.refs_0_), custom_call_target="tpu_custom_call" | custom-call | tf_op jit(solution)/shard_map/pallas_call | solution.py:522
  17.7 2.3 %collective-permute-done.ref = f32[432,128]{1,0:T(8,128)S(1)} collective-permute-done((f32[432,128]{1,0:T(8,128)S(1)}, f32[432,128]{1,0:T(8,128)S(1)}, u32[]{:S(2)}, u32[]{:S(2)}) %collective-permute-start) | collective-permute-done | bytes 221216 | tf_op jit(solution)/shard_map/ppermute | solution.py:501
  19.9 0.0 copy-start.2
  19.9 3.2 %shard_map.109 = (bf16[96,384]{1,0:T(8,128)(2,1)S(1)}, f32[32,96,128]{2,1,0:T(8,128)S(1)}, f32[8,384,128]{2,1,0:T(8,128)S(1)}, f32[8,192,128]{2,1,0:T(8,128)S(1)...) custom-call(f32[432,128]{1,0:T(8,128)S(1)} %collective-permute-done., ...), custom_call_target="tpu_custom_call" | custom-call | tf_op jit(solution)/shard_map/pallas_call | solution.py:531
  23.2 0.2 collective-permute-start.3
  23.3 0.8 %collective-permute-start.4 = (f32[384,128]{1,0:T(8,128)S(1)}, f32[384,128]{1,0:T(8,128)S(1)}, u32[]{:S(2)}, u32[]{:S(2)}) collective-permute-start(f32[384,128]{1,0:T(8,128)S(1)} %get-tuple-element.55), channel_id=1, source_target_pairs={{1,2},{2,1},{3,4},{4,3},{5,6},{6,5},{7,8},{8,7},{9,10},{10,9},{11,... | collective-permute-start | bytes 589832 | tf_op jit(solution)/shard_map/ppermute | solution.py:544
  24.2 0.0 copy-done.2
  24.2 8.2 %shard_map.110.refs_0_ = f32[752,1024]{1,0:T(8,128)S(1)} custom-call(f32[5,2,8,8]{3,2,1,0:T(8,128)S(1)} %copy-done.2, f32[8,384,128]{2,1,0:T(8,128)S(1)} %get-tuple-element.46.q0, f32[8,192,128]{2,1,0:T(8,128)S(1)} %get-tuple-element.47.s1, f32[8,96,128]{2,1,0:T(8,128)S(1)} %get-tuple-element.48.s2, f32[8,48,128]{2,1,0:T(8,128)S(1)} %get-tuple-element.49.s3, ...), custom_call_target="tpu_custom_call" | custom-call | tf_op jit(solution)/shard_map/pallas_call | solution.py:545
  32.4 0.0 collective-permute-done.3.refs_1_
  32.4 0.0 collective-permute-done.4.refs_2_
  32.5 5.7 %shard_map.111 = (f32[8,384,128]{2,1,0:T(8,128)}, f32[8,128]{1,0:T(8,128)S(1)}, f32[8,128]{1,0:T(8,128)S(1)}, f32[8,128]{1,0:T(8,128)S(1)}, f32[8,128]{1,0:T(8,128)S(1)}) custom-call(f32[752,1024]{1,0:T(8,128)S(1)} %shard_map.110.refs_0_, f32[384,128]{1,0:T(8,128)S(1)} %collective-permute-done.3.refs_1_, f32[384,128]{1,0:T(8,128)S(1)} %collective-permute-done.4.refs_2_, ...), custom_call_target="tpu_custom_call" | custom-call | tf_op jit(solution)/shard_map/pallas_call | solution.py:556
  38.1 3.1 %collective-permute-start.5 = (f32[8,128]{1,0:T(8,128)S(1)}, f32[8,128]{1,0:T(8,128)S(1)}, u32[]{:S(2)}, u32[]{:S(2)}) collective-permute-start(f32[8,128]{1,0:T(8,128)S(1)} %get-tuple-element.71), channel_id=1, source_target_pairs={{0,1},{1,0},{2,3},{3,2},{4,5},{5,4},{6,7},{7,6},{8,9},{9,8},{10,11... | collective-permute-start | bytes 12296 | tf_op jit(solution)/shard_map/ppermute | solution.py:568
  41.2 1.4 %collective-permute-start.6 = (f32[8,128]{1,0:T(8,128)S(1)}, f32[8,128]{1,0:T(8,128)S(1)}, u32[]{:S(2)}, u32[]{:S(2)}) collective-permute-start(f32[8,128]{1,0:T(8,128)S(1)} %get-tuple-element.72), channel_id=1, source_target_pairs={{0,2},{1,3},{2,0},{3,1},{4,6},{5,7},{6,4},{7,5},{8,10},{9,11},{10,... | collective-permute-start | bytes 12296 | tf_op jit(solution)/shard_map/ppermute | solution.py:568
  42.6 0.0 collective-permute-start.7
  42.6 0.0 collective-permute-done.5.b1
  42.6 2.2 %collective-permute-done.6.b2 = f32[8,128]{1,0:T(8,128)S(1)} collective-permute-done((f32[8,128]{1,0:T(8,128)S(1)}, f32[8,128]{1,0:T(8,128)S(1)}, u32[]{:S(2)}, u32[]{:S(2)}) %collective-permute-start.6) | collective-permute-done | bytes 4128 | tf_op jit(solution)/shard_map/ppermute | solution.py:568
  44.8 0.9 %collective-permute-done.7.b3 = f32[8,128]{1,0:T(8,128)S(1)} collective-permute-done((f32[8,128]{1,0:T(8,128)S(1)}, f32[8,128]{1,0:T(8,128)S(1)}, u32[]{:S(2)}, u32[]{:S(2)}) %collective-permute-start.7) | collective-permute-done | bytes 4128 | tf_op jit(solution)/shard_map/ppermute | solution.py:568
  45.7 1.0 %shard_map.112 = f32[1,1024]{1,0:T(1,128)} custom-call(s32[1]{0:T(128)S(6)} %copy.11.count_ref, f32[8,256]{1,0:T(8,128)S(1)} %get-tuple-element.69.slot_ref, f32[8,128]{1,0:T(8,128)S(1)} %get-tuple-element.70.b0, f32[8,128]{1,0:T(8,128)S(1)} %collective-permute-done.5.b1, f32[8,128]{1,0:T(8,128)S(1)} %collective-permute-done.6.b2, ...), custom_call_target="tpu_custom_call" | custom-call | tf_op jit(solution)/shard_map/pallas_call | solution.py:569
Async XLA Ops:
  1.3 1.0 %copy-start = (f32[1024,128]{1,0:T(8,128)S(1)}, f32[1024,128]{1,0:T(8,128)}, u32[]{:S(2)}) copy-start(f32[1024,128]{1,0:T(8,128)} %cells_hbm.1) | copy-start | bytes 1572868
  2.3 0.8 %copy-start.3 = (f32[8,1024]{1,0:T(8,128)S(1)}, f32[8,1024]{1,0:T(8,128)}, u32[]{:S(2)}) copy-start(f32[8,1024]{1,0:T(8,128)} %planes_hbm.1) | copy-start | bytes 98308
  3.1 0.7 %copy-start.6 = (f32[1024]{0:T(1024)S(1)}, f32[1024]{0:T(1024)}, u32[]{:S(2)}) copy-start(f32[1024]{0:T(1024)} %param.9) | copy-start | bytes 12292
  3.8 0.7 %copy-start.7 = (s32[256,1]{0,1:T(1,128)S(1)}, s32[256,1]{0,1:T(1,128)}, u32[]{:S(2)}) copy-start(s32[256,1]{0,1:T(1,128)} %param.12) | copy-start | bytes 3076
  4.4 0.7 %copy-start.8 = (s32[256]{0:T(256)S(1)}, s32[256]{0:T(256)}, u32[]{:S(2)}) copy-start(s32[256]{0:T(256)} %param.13) | copy-start | bytes 3076
  6.3 9.3 %collective-permute-start.2 = (f32[432,128]{1,0:T(8,128)S(1)}, f32[432,128]{1,0:T(8,128)S(1)}, u32[]{:S(2)}, u32[]{:S(2)}) collective-permute-start(f32[432,128]{1,0:T(8,128)S(1)} %get-tuple-element.40), channel_id=1, source_target_pairs={{0,1},{1,0},{2,3},{3,2},{4,5},{5,4},{6,7},{7,6},{8,9},{9,8},{10,11... | collective-permute-start | bytes 663560 | tf_op jit(solution)/shard_map/ppermute | solution.py:501
  6.8 9.8 %collective-permute-start.1 = (f32[432,128]{1,0:T(8,128)S(1)}, f32[432,128]{1,0:T(8,128)S(1)}, u32[]{:S(2)}, u32[]{:S(2)}) collective-permute-start(f32[432,128]{1,0:T(8,128)S(1)} %get-tuple-element.39), channel_id=1, source_target_pairs={{0,2},{1,3},{2,0},{3,1},{4,6},{5,7},{6,4},{7,5},{8,10},{9,11},{10,... | collective-permute-start | bytes 663560 | tf_op jit(solution)/shard_map/ppermute | solution.py:501
  9.4 10.5 %collective-permute-start = (f32[432,128]{1,0:T(8,128)S(1)}, f32[432,128]{1,0:T(8,128)S(1)}, u32[]{:S(2)}, u32[]{:S(2)}) collective-permute-start(f32[432,128]{1,0:T(8,128)S(1)} %get-tuple-element.38), channel_id=1, source_target_pairs={{0,3},{1,2},{2,1},{3,0},{4,7},{5,6},{6,5},{7,4},{8,11},{9,10},{10,... | collective-permute-start | bytes 663560 | tf_op jit(solution)/shard_map/ppermute | solution.py:501
  10.5 0.8 %copy-start.1 = (f32[5,2,8,8]{3,2,1,0:T(8,128)S(1)}, f32[5,2,8,8]{3,2,1,0:T(8,128)}, u32[]{:S(2)}) copy-start(f32[5,2,8,8]{3,2,1,0:T(8,128)} %mix_ref.3) | copy-start | bytes 7684
  11.3 0.7 %copy-start.4 = (f32[5,2,17]{2,1,0:T(2,128)S(1)}, f32[5,2,17]{2,1,0:T(2,128)}, u32[]{:S(2)}) copy-start(f32[5,2,17]{2,1,0:T(2,128)} %across_ref.1) | copy-start | bytes 2044
  12.0 0.7 %copy-start.5 = (f32[5,2,17]{2,1,0:T(2,128)S(1)}, f32[5,2,17]{2,1,0:T(2,128)}, u32[]{:S(2)}) copy-start(f32[5,2,17]{2,1,0:T(2,128)} %along_ref.1) | copy-start | bytes 2044
  19.9 4.3 %copy-start.2 = (f32[5,2,8,8]{3,2,1,0:T(8,128)S(1)}, f32[5,2,8,8]{3,2,1,0:T(8,128)}, u32[]{:S(2)}) copy-start(f32[5,2,8,8]{3,2,1,0:T(8,128)} %mix_ref.3) | copy-start | bytes 7684
  23.2 9.3 %collective-permute-start.3 = (f32[384,128]{1,0:T(8,128)S(1)}, f32[384,128]{1,0:T(8,128)S(1)}, u32[]{:S(2)}, u32[]{:S(2)}) collective-permute-start(f32[384,128]{1,0:T(8,128)S(1)} %get-tuple-element.54), channel_id=1, source_target_pairs={{0,1},{1,0},{2,3},{3,2},{4,5},{5,4},{6,7},{7,6},{8,9},{9,8},{10,11... | collective-permute-start | bytes 589832 | tf_op jit(solution)/shard_map/ppermute | solution.py:543
  23.3 9.1 %collective-permute-start.4 = (f32[384,128]{1,0:T(8,128)S(1)}, f32[384,128]{1,0:T(8,128)S(1)}, u32[]{:S(2)}, u32[]{:S(2)}) collective-permute-start(f32[384,128]{1,0:T(8,128)S(1)} %get-tuple-element.55), channel_id=1, source_target_pairs={{1,2},{2,1},{3,4},{4,3},{5,6},{6,5},{7,8},{8,7},{9,10},{10,9},{11,... | collective-permute-start | bytes 589832 | tf_op jit(solution)/shard_map/ppermute | solution.py:544
  38.1 4.5 %collective-permute-start.5 = (f32[8,128]{1,0:T(8,128)S(1)}, f32[8,128]{1,0:T(8,128)S(1)}, u32[]{:S(2)}, u32[]{:S(2)}) collective-permute-start(f32[8,128]{1,0:T(8,128)S(1)} %get-tuple-element.71), channel_id=1, source_target_pairs={{0,1},{1,0},{2,3},{3,2},{4,5},{5,4},{6,7},{7,6},{8,9},{9,8},{10,11... | collective-permute-start | bytes 12296 | tf_op jit(solution)/shard_map/ppermute | solution.py:568
  41.2 3.6 %collective-permute-start.6 = (f32[8,128]{1,0:T(8,128)S(1)}, f32[8,128]{1,0:T(8,128)S(1)}, u32[]{:S(2)}, u32[]{:S(2)}) collective-permute-start(f32[8,128]{1,0:T(8,128)S(1)} %get-tuple-element.72), channel_id=1, source_target_pairs={{0,2},{1,3},{2,0},{3,1},{4,6},{5,7},{6,4},{7,5},{8,10},{9,11},{10,... | collective-permute-start | bytes 12296 | tf_op jit(solution)/shard_map/ppermute | solution.py:568
  42.6 3.0 %collective-permute-start.7 = (f32[8,128]{1,0:T(8,128)S(1)}, f32[8,128]{1,0:T(8,128)S(1)}, u32[]{:S(2)}, u32[]{:S(2)}) collective-permute-start(f32[8,128]{1,0:T(8,128)S(1)} %get-tuple-element.73), channel_id=1, source_target_pairs={{0,3},{1,2},{2,1},{3,0},{4,7},{5,6},{6,5},{7,4},{8,11},{9,10},{10,... | collective-permute-start | bytes 12296 | tf_op jit(solution)/shard_map/ppermute | solution.py:568

commit v5 on v4

--- a/solution.py
+++ b/solution.py
@@ -489,6 +489,7 @@
             pltpu.VMEM((1, BRICKS), jnp.int32),
             pltpu.SemaphoreType.DMA((5,)),
         ],
+        megabytes=63,
     )(
         brick_count,
         currents.reshape(1, SEGS),

time: 47.1 us -> 44.9 us (0.953)
  local copies, waits for them, and re-layouts: 5.99 us -> 3.09 us
  Pallas kernels: 25.2 us -> 26.8 us
  waiting for transfers between devices: 5.32 us -> 4.59 us
    unnamed x18 -> x12, local copies, waits for them, and re-layouts: 5.99 us -> 3.09 us
    pallas_call x1, Pallas kernels: 1.19 us -> 2.76 us  [body(): call(route_kernel, [SMEM] + [HBM] * 5, [shape(ROWS, CX)] * PEERS + [shape...]
    ppermute x3, waiting for transfers between devices: 2.27 us -> 1.55 us  [body(): lax.ppermute(sends[k], 'sect', swaps[k])]
  transfers between devices with their start and end apart: 8 -> 8, of which waited for: 3 -> 3; matrix products, arithmetic and copies ran while one was open for 0% -> 0% of each run, Pallas kernels for 30% -> 32%
where the time goes in v5:
time: 44.9 us; the launch traced here: 44.6 us
  Pallas kernels  26.8 us (60%)
  starting transfers between devices  8.72 us (19%)
  waiting for transfers between devices  4.59 us (10%)
  local copies, waits for them, and re-layouts  3.09 us (7%)
  between operations  1.39 us (3%)
    pallas_call x1, Pallas kernels, body(): call(inner_kernel, [SMEM] + [VMEM] * 8, [shape(ALL_ROWS, HALF)], [pltpu.V...  8.23 us
    pallas_call x1, Pallas kernels, body(): call(outer_kernel, [VMEM] * (8 + 2 * PEERS), [shape(PLANES, NY, CX)] + [s...  5.68 us
    ppermute x3, starting transfers between devices, body(): lax.ppermute(samples[k], 'sect', swaps[k])  4.52 us
    pallas_call x1, Pallas kernels, body(): call(charge_kernel, [VMEM] * 3, kept + [shape(PLANES, size, CX) for size...  3.22 us
    ppermute x3, starting transfers between devices, body(): lax.ppermute(sends[k], 'sect', swaps[k])  3.18 us
    unnamed x12, local copies, waits for them, and re-layouts  3.09 us
    pallas_call x3, Pallas kernels, body(): call(brick_kernel, [VMEM] * (1 + len(total)), kept + [shape(TILES, HALF)]...  3.07 us
    ppermute x3, waiting for transfers between devices, body(): lax.ppermute(samples[k], 'sect', swaps[k])  3.03 us
  transfers between devices with their start and end apart: 8, of which 3 were waited for; matrix products, arithmetic and copies ran while one was open for 0% of the time, Pallas kernels for 32%

profile of v5, /device:TPU:0, one launch (start us, length us, event | category | flops | bytes accessed | tf_op | source)
XLA Modules:
  0.0 44.6 jit_solution(7499264493303078390)
XLA Ops:
  1.3 2.8 %shard_map.104 = (f32[432,128]{1,0:T(8,128)}, f32[432,128]{1,0:T(8,128)}, f32[432,128]{1,0:T(8,128)}, f32[432,128]{1,0:T(8,128)}, f32[8,256]{1,0:T(8,128)}) custom-call(s32[1]{0:T(128)S(6)} %copy.11.count_ref, f32[1,1024]{1,0:T(1,128)} %bitcast.4, f32[8,1024]{1,0:T(8,128)} %planes_hbm.1, f32[1024,128]{1,0:T(8,128)} %cells_hbm.1, s32[1,256]{1,0:T(1,128)} %bitcast.6, ...), custom_call_target="tpu_custom_call" | custom-call | tf_op jit(solution)/shard_map/pallas_call | solution.py:479
  4.0 0.5 %collective-permute-start.2 = (f32[432,128]{1,0:T(8,128)}, f32[432,128]{1,0:T(8,128)S(1)}, u32[]{:S(2)}, u32[]{:S(2)}) collective-permute-start(f32[432,128]{1,0:T(8,128)} %get-tuple-element.40), channel_id=1, source_target_pairs={{0,1},{1,0},{2,3},{3,2},{4,5},{5,4},{6,7},{7,6},{8,9},{9,8},{10,11... | collective-permute-start | bytes 663560 | tf_op jit(solution)/shard_map/ppermute | solution.py:502
  4.6 2.6 %collective-permute-start.1 = (f32[432,128]{1,0:T(8,128)}, f32[432,128]{1,0:T(8,128)S(1)}, u32[]{:S(2)}, u32[]{:S(2)}) collective-permute-start(f32[432,128]{1,0:T(8,128)} %get-tuple-element.39), channel_id=1, source_target_pairs={{0,2},{1,3},{2,0},{3,1},{4,6},{5,7},{6,4},{7,5},{8,10},{9,11},{10,... | collective-permute-start | bytes 663560 | tf_op jit(solution)/shard_map/ppermute | solution.py:502
  7.2 0.1 collective-permute-start
  7.2 0.0 copy-start
  7.2 0.9 %copy-done = f32[432,128]{1,0:T(8,128)S(1)} copy-done((f32[432,128]{1,0:T(8,128)S(1)}, f32[432,128]{1,0:T(8,128)}, u32[]{:S(2)}) %copy-start) | copy-done | bytes 221208
  8.2 1.0 %shard_map.105 = (bf16[96,384]{1,0:T(8,128)(2,1)S(1)}, f32[32,96,128]{2,1,0:T(8,128)S(1)}, f32[384,1024]{1,0:T(8,128)S(1)}) custom-call(f32[432,128]{1,0:T(8,128)S(1)} %copy-done), custom_call_target="tpu_custom_call" | custom-call | tf_op jit(solution)/shard_map/pallas_call | solution.py:523
  9.2 0.0 copy-start.1
  9.2 0.8 %copy-done.1 = f32[5,2,8,8]{3,2,1,0:T(8,128)S(1)} copy-done((f32[5,2,8,8]{3,2,1,0:T(8,128)S(1)}, f32[5,2,8,8]{3,2,1,0:T(8,128)}, u32[]{:S(2)}) %copy-start.1) | copy-done | bytes 2584
  10.0 0.0 copy-start.4
  10.0 0.7 %copy-done.4 = f32[5,2,17]{2,1,0:T(2,128)S(1)} copy-done((f32[5,2,17]{2,1,0:T(2,128)S(1)}, f32[5,2,17]{2,1,0:T(2,128)}, u32[]{:S(2)}) %copy-start.4) | copy-done | bytes 704
  10.7 0.0 copy-start.5
  10.7 0.7 %copy-done.5 = f32[5,2,17]{2,1,0:T(2,128)S(1)} copy-done((f32[5,2,17]{2,1,0:T(2,128)S(1)}, f32[5,2,17]{2,1,0:T(2,128)}, u32[]{:S(2)}) %copy-start.5) | copy-done | bytes 704
  11.3 2.9 %shard_map.108 = (bf16[5,256,256]{2,1,0:T(8,128)(2,1)S(1)}, bf16[5,128,256]{2,1,0:T(8,128)(2,1)S(1)}, bf16[1504,768]{1,0:T(8,128)(2,1)S(1)}, bf16[5,128,256]{2,1...) custom-call(f32[5,2,17]{2,1,0:T(2,128)S(1)} %copy-done.4, ...), custom_call_target="tpu_custom_call" | custom-call | tf_op jit(solution)/shard_map/pallas_call | solution.py:503
  14.2 0.0 collective-permute-done.2.ref
  14.2 1.0 %shard_map.106 = (bf16[96,384]{1,0:T(8,128)(2,1)S(1)}, f32[32,96,128]{2,1,0:T(8,128)S(1)}, f32[384,1024]{1,0:T(8,128)S(1)}) custom-call(f32[432,128]{1,0:T(8,128)S(1)} %collective-permute-done.2.ref, f32[384,1024]{1,0:T(8,128)S(1)} %get-tuple-element.42.refs_0_), custom_call_target="tpu_custom_call" | custom-call | tf_op jit(solution)/shard_map/pallas_call | solution.py:523
  15.3 0.0 collective-permute-done.1.ref
  15.3 1.0 %shard_map.107 = (bf16[96,384]{1,0:T(8,128)(2,1)S(1)}, f32[32,96,128]{2,1,0:T(8,128)S(1)}, f32[384,1024]{1,0:T(8,128)S(1)}) custom-call(f32[432,128]{1,0:T(8,128)S(1)} %collective-permute-done.1.ref, f32[384,1024]{1,0:T(8,128)S(1)} %get-tuple-element.43.refs_0_), custom_call_target="tpu_custom_call" | custom-call | tf_op jit(solution)/shard_map/pallas_call | solution.py:523
  16.3 1.5 %collective-permute-done.ref = f32[432,128]{1,0:T(8,128)S(1)} collective-permute-done((f32[432,128]{1,0:T(8,128)}, f32[432,128]{1,0:T(8,128)S(1)}, u32[]{:S(2)}, u32[]{:S(2)}) %collective-permute-start) | collective-permute-done | bytes 221216 | tf_op jit(solution)/shard_map/ppermute | solution.py:502
  17.9 0.0 copy-start.2
  17.9 3.2 %shard_map.109 = (bf16[96,384]{1,0:T(8,128)(2,1)S(1)}, f32[32,96,128]{2,1,0:T(8,128)S(1)}, f32[8,384,128]{2,1,0:T(8,128)S(1)}, f32[8,192,128]{2,1,0:T(8,128)S(1)...) custom-call(f32[432,128]{1,0:T(8,128)S(1)} %collective-permute-done., ...), custom_call_target="tpu_custom_call" | custom-call | tf_op jit(solution)/shard_map/pallas_call | solution.py:532
  21.1 0.2 collective-permute-start.3
  21.3 0.8 %collective-permute-start.4 = (f32[384,128]{1,0:T(8,128)S(1)}, f32[384,128]{1,0:T(8,128)S(1)}, u32[]{:S(2)}, u32[]{:S(2)}) collective-permute-start(f32[384,128]{1,0:T(8,128)S(1)} %get-tuple-element.55), channel_id=1, source_target_pairs={{1,2},{2,1},{3,4},{4,3},{5,6},{6,5},{7,8},{8,7},{9,10},{10,9},{11,... | collective-permute-start | bytes 589832 | tf_op jit(solution)/shard_map/ppermute | solution.py:545
  22.1 0.0 copy-done.2
  22.1 8.2 %shard_map.110.refs_0_ = f32[752,1024]{1,0:T(8,128)S(1)} custom-call(f32[5,2,8,8]{3,2,1,0:T(8,128)S(1)} %copy-done.2, f32[8,384,128]{2,1,0:T(8,128)S(1)} %get-tuple-element.46.q0, f32[8,192,128]{2,1,0:T(8,128)S(1)} %get-tuple-element.47.s1, f32[8,96,128]{2,1,0:T(8,128)S(1)} %get-tuple-element.48.s2, f32[8,48,128]{2,1,0:T(8,128)S(1)} %get-tuple-element.49.s3, ...), custom_call_target="tpu_custom_call" | custom-call | tf_op jit(solution)/shard_map/pallas_call | solution.py:546
  30.4 0.0 collective-permute-done.3.refs_1_
  30.4 0.0 collective-permute-done.4.refs_2_
  30.4 0.0 copy-start.3
  30.4 5.7 %shard_map.111 = (f32[8,384,128]{2,1,0:T(8,128)}, f32[8,128]{1,0:T(8,128)S(1)}, f32[8,128]{1,0:T(8,128)S(1)}, f32[8,128]{1,0:T(8,128)S(1)}, f32[8,128]{1,0:T(8,128)S(1)}) custom-call(f32[752,1024]{1,0:T(8,128)S(1)} %shard_map.110.refs_0_, f32[384,128]{1,0:T(8,128)S(1)} %collective-permute-done.3.refs_1_, f32[384,128]{1,0:T(8,128)S(1)} %collective-permute-done.4.refs_2_, ...), custom_call_target="tpu_custom_call" | custom-call | tf_op jit(solution)/shard_map/pallas_call | solution.py:557
  36.1 3.1 %collective-permute-start.5 = (f32[8,128]{1,0:T(8,128)S(1)}, f32[8,128]{1,0:T(8,128)S(1)}, u32[]{:S(2)}, u32[]{:S(2)}) collective-permute-start(f32[8,128]{1,0:T(8,128)S(1)} %get-tuple-element.71), channel_id=1, source_target_pairs={{0,1},{1,0},{2,3},{3,2},{4,5},{5,4},{6,7},{7,6},{8,9},{9,8},{10,11... | collective-permute-start | bytes 12296 | tf_op jit(solution)/shard_map/ppermute | solution.py:569
  39.2 1.4 %collective-permute-start.6 = (f32[8,128]{1,0:T(8,128)S(1)}, f32[8,128]{1,0:T(8,128)S(1)}, u32[]{:S(2)}, u32[]{:S(2)}) collective-permute-start(f32[8,128]{1,0:T(8,128)S(1)} %get-tuple-element.72), channel_id=1, source_target_pairs={{0,2},{1,3},{2,0},{3,1},{4,6},{5,7},{6,4},{7,5},{8,10},{9,11},{10,... | collective-permute-start | bytes 12296 | tf_op jit(solution)/shard_map/ppermute | solution.py:569
  40.6 0.0 collective-permute-start.7
  40.6 0.0 collective-permute-done.5.b1
  40.6 2.2 %collective-permute-done.6.b2 = f32[8,128]{1,0:T(8,128)S(1)} collective-permute-done((f32[8,128]{1,0:T(8,128)S(1)}, f32[8,128]{1,0:T(8,128)S(1)}, u32[]{:S(2)}, u32[]{:S(2)}) %collective-permute-start.6) | collective-permute-done | bytes 4128 | tf_op jit(solution)/shard_map/ppermute | solution.py:569
  42.8 0.9 %collective-permute-done.7.b3 = f32[8,128]{1,0:T(8,128)S(1)} collective-permute-done((f32[8,128]{1,0:T(8,128)S(1)}, f32[8,128]{1,0:T(8,128)S(1)}, u32[]{:S(2)}, u32[]{:S(2)}) %collective-permute-start.7) | collective-permute-done | bytes 4128 | tf_op jit(solution)/shard_map/ppermute | solution.py:569
  43.6 0.0 copy-done.3
  43.6 1.0 %shard_map.112 = f32[1,1024]{1,0:T(1,128)} custom-call(s32[1]{0:T(128)S(6)} %copy.11.count_ref, f32[8,256]{1,0:T(8,128)S(1)} %copy-done.3, f32[8,128]{1,0:T(8,128)S(1)} %get-tuple-element.70.b0, f32[8,128]{1,0:T(8,128)S(1)} %collective-permute-done.5.b1, f32[8,128]{1,0:T(8,128)S(1)} %collective-permute-done.6.b2, f32[8,128]{1,0:T(8,128)S(1)} %collective-permute-done.7.b3), custom_call_target="tpu_custom_call" | custom-call | tf_op jit(solution)/shard_map/pallas_call | solution.py:570
Async XLA Ops:
  4.0 10.2 %collective-permute-start.2 = (f32[432,128]{1,0:T(8,128)}, f32[432,128]{1,0:T(8,128)S(1)}, u32[]{:S(2)}, u32[]{:S(2)}) collective-permute-start(f32[432,128]{1,0:T(8,128)} %get-tuple-element.40), channel_id=1, source_target_pairs={{0,1},{1,0},{2,3},{3,2},{4,5},{5,4},{6,7},{7,6},{8,9},{9,8},{10,11... | collective-permute-start | bytes 663560 | tf_op jit(solution)/shard_map/ppermute | solution.py:502
  4.6 10.7 %collective-permute-start.1 = (f32[432,128]{1,0:T(8,128)}, f32[432,128]{1,0:T(8,128)S(1)}, u32[]{:S(2)}, u32[]{:S(2)}) collective-permute-start(f32[432,128]{1,0:T(8,128)} %get-tuple-element.39), channel_id=1, source_target_pairs={{0,2},{1,3},{2,0},{3,1},{4,6},{5,7},{6,4},{7,5},{8,10},{9,11},{10,... | collective-permute-start | bytes 663560 | tf_op jit(solution)/shard_map/ppermute | solution.py:502
  7.2 10.7 %collective-permute-start = (f32[432,128]{1,0:T(8,128)}, f32[432,128]{1,0:T(8,128)S(1)}, u32[]{:S(2)}, u32[]{:S(2)}) collective-permute-start(f32[432,128]{1,0:T(8,128)} %get-tuple-element.38), channel_id=1, source_target_pairs={{0,3},{1,2},{2,1},{3,0},{4,7},{5,6},{6,5},{7,4},{8,11},{9,10},{10,... | collective-permute-start | bytes 663560 | tf_op jit(solution)/shard_map/ppermute | solution.py:502
  7.2 0.9 %copy-start = (f32[432,128]{1,0:T(8,128)S(1)}, f32[432,128]{1,0:T(8,128)}, u32[]{:S(2)}) copy-start(f32[432,128]{1,0:T(8,128)} %get-tuple-element.41.ref) | copy-start | bytes 663556
  9.2 0.8 %copy-start.1 = (f32[5,2,8,8]{3,2,1,0:T(8,128)S(1)}, f32[5,2,8,8]{3,2,1,0:T(8,128)}, u32[]{:S(2)}) copy-start(f32[5,2,8,8]{3,2,1,0:T(8,128)} %mix_ref.3) | copy-start | bytes 7684
  10.0 0.7 %copy-start.4 = (f32[5,2,17]{2,1,0:T(2,128)S(1)}, f32[5,2,17]{2,1,0:T(2,128)}, u32[]{:S(2)}) copy-start(f32[5,2,17]{2,1,0:T(2,128)} %across_ref.1) | copy-start | bytes 2044
  10.7 0.7 %copy-start.5 = (f32[5,2,17]{2,1,0:T(2,128)S(1)}, f32[5,2,17]{2,1,0:T(2,128)}, u32[]{:S(2)}) copy-start(f32[5,2,17]{2,1,0:T(2,128)} %along_ref.1) | copy-start | bytes 2044
  17.9 4.3 %copy-start.2 = (f32[5,2,8,8]{3,2,1,0:T(8,128)S(1)}, f32[5,2,8,8]{3,2,1,0:T(8,128)}, u32[]{:S(2)}) copy-start(f32[5,2,8,8]{3,2,1,0:T(8,128)} %mix_ref.3) | copy-start | bytes 7684
  21.1 9.3 %collective-permute-start.3 = (f32[384,128]{1,0:T(8,128)S(1)}, f32[384,128]{1,0:T(8,128)S(1)}, u32[]{:S(2)}, u32[]{:S(2)}) collective-permute-start(f32[384,128]{1,0:T(8,128)S(1)} %get-tuple-element.54), channel_id=1, source_target_pairs={{0,1},{1,0},{2,3},{3,2},{4,5},{5,4},{6,7},{7,6},{8,9},{9,8},{10,11... | collective-permute-start | bytes 589832 | tf_op jit(solution)/shard_map/ppermute | solution.py:544
  21.3 9.1 %collective-permute-start.4 = (f32[384,128]{1,0:T(8,128)S(1)}, f32[384,128]{1,0:T(8,128)S(1)}, u32[]{:S(2)}, u32[]{:S(2)}) collective-permute-start(f32[384,128]{1,0:T(8,128)S(1)} %get-tuple-element.55), channel_id=1, source_target_pairs={{1,2},{2,1},{3,4},{4,3},{5,6},{6,5},{7,8},{8,7},{9,10},{10,9},{11,... | collective-permute-start | bytes 589832 | tf_op jit(solution)/shard_map/ppermute | solution.py:545
  30.4 13.2 %copy-start.3 = (f32[8,256]{1,0:T(8,128)S(1)}, f32[8,256]{1,0:T(8,128)}, u32[]{:S(2)}) copy-start(f32[8,256]{1,0:T(8,128)} %get-tuple-element.69.slot_ref) | copy-start | bytes 24580
  36.1 4.5 %collective-permute-start.5 = (f32[8,128]{1,0:T(8,128)S(1)}, f32[8,128]{1,0:T(8,128)S(1)}, u32[]{:S(2)}, u32[]{:S(2)}) collective-permute-start(f32[8,128]{1,0:T(8,128)S(1)} %get-tuple-element.71), channel_id=1, source_target_pairs={{0,1},{1,0},{2,3},{3,2},{4,5},{5,4},{6,7},{7,6},{8,9},{9,8},{10,11... | collective-permute-start | bytes 12296 | tf_op jit(solution)/shard_map/ppermute | solution.py:569
  39.2 3.6 %collective-permute-start.6 = (f32[8,128]{1,0:T(8,128)S(1)}, f32[8,128]{1,0:T(8,128)S(1)}, u32[]{:S(2)}, u32[]{:S(2)}) collective-permute-start(f32[8,128]{1,0:T(8,128)S(1)} %get-tuple-element.72), channel_id=1, source_target_pairs={{0,2},{1,3},{2,0},{3,1},{4,6},{5,7},{6,4},{7,5},{8,10},{9,11},{10,... | collective-permute-start | bytes 12296 | tf_op jit(solution)/shard_map/ppermute | solution.py:569
  40.6 3.0 %collective-permute-start.7 = (f32[8,128]{1,0:T(8,128)S(1)}, f32[8,128]{1,0:T(8,128)S(1)}, u32[]{:S(2)}, u32[]{:S(2)}) collective-permute-start(f32[8,128]{1,0:T(8,128)S(1)} %get-tuple-element.73), channel_id=1, source_target_pairs={{0,3},{1,2},{2,1},{3,0},{4,7},{5,6},{6,5},{7,4},{8,11},{9,10},{10,... | collective-permute-start | bytes 12296 | tf_op jit(solution)/shard_map/ppermute | solution.py:569

commit v6 on v5

--- a/solution.py
+++ b/solution.py
@@ -17,7 +17,9 @@
 CAP = 96
 PEERS = 4
 CELLS = SLOTS * CAP
-PACK = CAP // 2
+PACK = CAP // 3
+SPAN = 10
+WIDE = SPAN * SLOTS
 ROWS = CELLS + PACK
 SEGS = BRICKS * SLOTS
 BAND = NY // 8
@@ -100,7 +102,7 @@
         feature[part * CX : (part + 1) * CX, :] = lines[:, part * CX : (part + 1) * CX].T
     meta = jnp.zeros((BRICKS, CX), F32)
     for s in range(SLOTS):
-        meta = meta + turn(feature[pl.ds(s, BRICKS, stride=SLOTS), :], 16 * s)
+        meta = meta + turn(feature[pl.ds(s, BRICKS, stride=SLOTS), :], SPAN * s)
     tile = tile_ref[...]
     tile = (tile & 7) * BAND + (tile >> 3)
     tiles = jnp.concatenate([tile.astype(F32), jnp.zeros((CX - 1, BRICKS), F32)], axis=0)
@@ -109,9 +111,11 @@
     both = dot(choose, jnp.concatenate(split(meta), axis=1))
     both = both[:, :CX] + both[:, CX:]
     for k in range(PEERS):
-        lower = both[k * CAP : k * CAP + PACK]
-        upper = both[k * CAP + PACK : (k + 1) * CAP]
-        outs[k][CELLS:, :] = lower + turn(upper, CX // 2)
+        packed = both[k * CAP : k * CAP + PACK]
+        for i in range(1, 3):
+            start = k * CAP + i * PACK
+            packed = packed + turn(both[start : start + PACK], WIDE * i)
+        outs[k][CELLS:, :] = packed
     copies[4].wait()
     for s in range(SLOTS):
         high, low = split(cells_ref[pl.ds(s, BRICKS, stride=SLOTS), :])
@@ -214,13 +218,13 @@
 
 def brick_products(ref, match, weights, bricks):
     packed = ref[CELLS:, :]
-    meta = jnp.concatenate([packed, turn(packed, CX // 2)], axis=0)
+    meta = jnp.concatenate([packed, turn(packed, -WIDE), turn(packed, -2 * WIDE)], axis=0)
     cells = [ref[s * CAP : (s + 1) * CAP, :] for s in range(SLOTS)]
     totals = [None] * PLANES
     for s in range(SLOTS):
-        current = meta[:, 16 * s + 8 : 16 * s + 9]
+        current = meta[:, SPAN * s + 8 : SPAN * s + 9]
         for z in range(PLANES):
-            piece = cells[s] * meta[:, 16 * s + z : 16 * s + z + 1]
+            piece = cells[s] * meta[:, SPAN * s + z : SPAN * s + z + 1]
             weights[s * PLANES + z] = piece
             piece = piece * current
             totals[z] = piece if s == 0 else totals[z] + piece
@@ -415,12 +419,13 @@
                 high, low = split(band)
                 rows = slice(b * BAND, (b + 1) * BAND)
                 tiles[rows, z * CX : (z + 1) * CX] = high
-                tiles[rows, HALF + z * CX : HALF + (z + 1) * CX] = low
+                rows = slice(TILES + b * BAND, TILES + (b + 1) * BAND)
+                tiles[rows, z * CX : (z + 1) * CX] = low
     match = jnp.concatenate([ref[...] for ref in matches], axis=0)
+    match = jnp.concatenate([match, match], axis=1)
     for pair in range(PLANES // 2):
         part = slice(pair * 2 * CX, (pair + 1) * 2 * CX)
-        lower = slice(HALF + pair * 2 * CX, HALF + (pair + 1) * 2 * CX)
-        picked[:, part] = dot(match, tiles[:, part]) + dot(match, tiles[:, lower])
+        picked[:, part] = dot(match, tiles[:, part])
     for j in range(PEERS):
         mine = slice(j * CAP, (j + 1) * CAP)
         values = jnp.zeros((CAP, CX), F32)
@@ -433,18 +438,21 @@
         outs[j][...] = values.T[:8, :]
 
 
-def pick_kernel(count_ref, slot_ref, b0, b1, b2, b3, out_ref):
+def spread_kernel(slot_ref, match_ref):
     slot = slot_ref[0:1, :]
     away = jnp.floor((slot + 0.5) * (1.0 / CAP))
-    place = slot + away * (CX - CAP)
-    match = (iota((PEERS * CX, BRICKS), 0).astype(F32) == place).astype(F32).astype(BF16)
+    pieces = jnp.concatenate(
+        [away, slot - away * CAP, jnp.zeros((14, BRICKS), F32)], axis=0
+    )
+    spread = flags(iota((BRICKS, SEGS), 1) // SLOTS == iota((BRICKS, SEGS), 0))
+    pieces = dot(pieces.astype(BF16), spread)
+    place = pieces[0:1] * CX + pieces[1:2]
+    match_ref[...] = flags(iota((PEERS * CX, SEGS), 0).astype(F32) == place)
+
+
+def pick_kernel(count_ref, match_ref, b0, b1, b2, b3, out_ref):
     held = jnp.concatenate([b0[...], b1[...], b2[...], b3[...]], axis=1)
-    high, low = split(held)
-    value = dot(jnp.concatenate([high, low], axis=0), match)
-    value = value[:8] + value[8:]
-    spread = (iota((BRICKS, SEGS), 1) // SLOTS == iota((BRICKS, SEGS), 0)).astype(F32).astype(BF16)
-    high, low = split(value)
-    value = dot(jnp.concatenate([high, low], axis=0), spread)
+    value = dot(jnp.concatenate(split(held), axis=0), match_ref[...])
     value = value[:8] + value[8:]
     lane = iota((8, SEGS), 1)
     mine = (lane % SLOTS == iota((8, SEGS), 0)) & (lane // SLOTS < count_ref[0])
@@ -468,7 +476,7 @@
         out_specs=[VMEM] * len(outputs),
         out_shape=list(outputs),
         scratch_shapes=list(scratch),
-        compiler_params=pltpu.CompilerParams(vmem_limit_bytes=megabytes << 20),
+        compiler_params=pltpu.CompilerParams(vmem_limit_bytes=int(megabytes * (1 << 20))),
     )
 
 
@@ -561,15 +569,16 @@
         [
             pltpu.VMEM((ALL_K, 2 * CX), BF16),
             pltpu.VMEM((ALL_K, 2 * CX), BF16),
-            pltpu.VMEM((TILES, 2 * HALF), BF16),
+            pltpu.VMEM((2 * TILES, HALF), BF16),
             pltpu.VMEM((PEERS * CAP, HALF), F32),
             pltpu.VMEM((2 * BAND, CX), F32),
         ],
     )(inner, by_pair, by_next, across, *outer, *matches, *weights)
     back = [samples[0]] + [lax.ppermute(samples[k], "sect", swaps[k]) for k in range(1, PEERS)]
+    (match,) = call(spread_kernel, [VMEM], [shape(PEERS * CX, SEGS, kind=BF16)])(slots)
     (segments,) = call(
         pick_kernel, [SMEM] + [VMEM] * 5, [shape(1, SEGS)]
-    )(brick_count, slots, *back)
+    )(brick_count, match, *back)
     return grid, segments.reshape(SEGS)
 
 

time: 44.9 us -> 44.5 us (level)
  waiting for transfers between devices: 4.59 us -> 3.76 us
    ppermute x3, waiting for transfers between devices: 3.03 us -> 2.58 us  [body(): lax.ppermute(samples[k], 'sect', swaps[k])]
  transfers between devices with their start and end apart: 8 -> 8, of which waited for: 3 -> 3; matrix products, arithmetic and copies ran while one was open for 0% -> 0% of each run, Pallas kernels for 32% -> 33%
where the time goes in v6:
time: 44.5 us; the launch traced here: 44.2 us
  Pallas kernels  27.2 us (61%)
  starting transfers between devices  8.72 us (20%)
  waiting for transfers between devices  3.76 us (8%)
  local copies, waits for them, and re-layouts  3.09 us (7%)
  between operations  1.41 us (3%)
    pallas_call x1, Pallas kernels, body(): call(inner_kernel, [SMEM] + [VMEM] * 8, [shape(ALL_ROWS, HALF)], [pltpu.V...  8.23 us
    pallas_call x1, Pallas kernels, body(): call(outer_kernel, [VMEM] * (8 + 2 * PEERS), [shape(PLANES, NY, CX)] + [s...  5.68 us
    ppermute x3, starting transfers between devices, body(): lax.ppermute(samples[k], 'sect', swaps[k])  4.52 us
    pallas_call x1, Pallas kernels, body(): call(charge_kernel, [VMEM] * 3, kept + [shape(PLANES, size, CX) for size...  3.25 us
    ppermute x3, starting transfers between devices, body(): lax.ppermute(sends[k], 'sect', swaps[k])  3.18 us
    pallas_call x3, Pallas kernels, body(): call(brick_kernel, [VMEM] * (1 + len(total)), kept + [shape(TILES, HALF)]...  3.12 us
    unnamed x12, local copies, waits for them, and re-layouts  3.09 us
    pallas_call x1, Pallas kernels, body(): call(prep_kernel, [VMEM, VMEM, VMEM], [shape(LEVELS + 1, 2 * CX, 2 * CX,...  2.86 us
  transfers between devices with their start and end apart: 8, of which 3 were waited for; matrix products, arithmetic and copies ran while one was open for 0% of the time, Pallas kernels for 33%

profile of v6, /device:TPU:0, one launch (start us, length us, event | category | flops | bytes accessed | tf_op | source)
XLA Modules:
  0.0 44.2 jit_solution(6907815132189159648)
XLA Ops:
  1.3 2.7 %shard_map.104 = (f32[416,128]{1,0:T(8,128)}, f32[416,128]{1,0:T(8,128)}, f32[416,128]{1,0:T(8,128)}, f32[416,128]{1,0:T(8,128)}, f32[8,256]{1,0:T(8,128)}) custom-call(s32[1]{0:T(128)S(6)} %copy.11.count_ref, f32[1,1024]{1,0:T(1,128)} %bitcast.4, f32[8,1024]{1,0:T(8,128)} %planes_hbm.1, f32[1024,128]{1,0:T(8,128)} %cells_hbm.1, s32[1,256]{1,0:T(1,128)} %bitcast.6, ...), custom_call_target="tpu_custom_call" | custom-call | tf_op jit(solution)/shard_map/pallas_call | solution.py:487
  4.0 0.5 %collective-permute-start.2 = (f32[416,128]{1,0:T(8,128)}, f32[416,128]{1,0:T(8,128)S(1)}, u32[]{:S(2)}, u32[]{:S(2)}) collective-permute-start(f32[416,128]{1,0:T(8,128)} %get-tuple-element.40), channel_id=1, source_target_pairs={{0,1},{1,0},{2,3},{3,2},{4,5},{5,4},{6,7},{7,6},{8,9},{9,8},{10,11... | collective-permute-start | bytes 638984 | tf_op jit(solution)/shard_map/ppermute | solution.py:510
  4.5 2.6 %collective-permute-start.1 = (f32[416,128]{1,0:T(8,128)}, f32[416,128]{1,0:T(8,128)S(1)}, u32[]{:S(2)}, u32[]{:S(2)}) collective-permute-start(f32[416,128]{1,0:T(8,128)} %get-tuple-element.39), channel_id=1, source_target_pairs={{0,2},{1,3},{2,0},{3,1},{4,6},{5,7},{6,4},{7,5},{8,10},{9,11},{10,... | collective-permute-start | bytes 638984 | tf_op jit(solution)/shard_map/ppermute | solution.py:510
  7.1 0.1 collective-permute-start
  7.2 0.0 copy-start
  7.2 0.9 %copy-done = f32[416,128]{1,0:T(8,128)S(1)} copy-done((f32[416,128]{1,0:T(8,128)S(1)}, f32[416,128]{1,0:T(8,128)}, u32[]{:S(2)}) %copy-start) | copy-done | bytes 213016
  8.1 1.0 %shard_map.105 = (bf16[96,384]{1,0:T(8,128)(2,1)S(1)}, f32[32,96,128]{2,1,0:T(8,128)S(1)}, f32[384,1024]{1,0:T(8,128)S(1)}) custom-call(f32[416,128]{1,0:T(8,128)S(1)} %copy-done), custom_call_target="tpu_custom_call" | custom-call | tf_op jit(solution)/shard_map/pallas_call | solution.py:531
  9.2 0.0 copy-start.1
  9.2 0.8 %copy-done.1 = f32[5,2,8,8]{3,2,1,0:T(8,128)S(1)} copy-done((f32[5,2,8,8]{3,2,1,0:T(8,128)S(1)}, f32[5,2,8,8]{3,2,1,0:T(8,128)}, u32[]{:S(2)}) %copy-start.1) | copy-done | bytes 2584
  10.0 0.0 copy-start.4
  10.0 0.7 %copy-done.4 = f32[5,2,17]{2,1,0:T(2,128)S(1)} copy-done((f32[5,2,17]{2,1,0:T(2,128)S(1)}, f32[5,2,17]{2,1,0:T(2,128)}, u32[]{:S(2)}) %copy-start.4) | copy-done | bytes 704
  10.7 0.0 copy-start.5
  10.7 0.7 %copy-done.5 = f32[5,2,17]{2,1,0:T(2,128)S(1)} copy-done((f32[5,2,17]{2,1,0:T(2,128)S(1)}, f32[5,2,17]{2,1,0:T(2,128)}, u32[]{:S(2)}) %copy-start.5) | copy-done | bytes 704
  11.3 2.9 %shard_map.108 = (bf16[5,256,256]{2,1,0:T(8,128)(2,1)S(1)}, bf16[5,128,256]{2,1,0:T(8,128)(2,1)S(1)}, bf16[1504,768]{1,0:T(8,128)(2,1)S(1)}, bf16[5,128,256]{2,1...) custom-call(f32[5,2,17]{2,1,0:T(2,128)S(1)} %copy-done.4, ...), custom_call_target="tpu_custom_call" | custom-call | tf_op jit(solution)/shard_map/pallas_call | solution.py:511
  14.2 0.0 collective-permute-done.2.ref
  14.2 1.0 %shard_map.106 = (bf16[96,384]{1,0:T(8,128)(2,1)S(1)}, f32[32,96,128]{2,1,0:T(8,128)S(1)}, f32[384,1024]{1,0:T(8,128)S(1)}) custom-call(f32[416,128]{1,0:T(8,128)S(1)} %collective-permute-done.2.ref, f32[384,1024]{1,0:T(8,128)S(1)} %get-tuple-element.42.refs_0_), custom_call_target="tpu_custom_call" | custom-call | tf_op jit(solution)/shard_map/pallas_call | solution.py:531
  15.3 0.0 collective-permute-done.1.ref
  15.3 1.0 %shard_map.107 = (bf16[96,384]{1,0:T(8,128)(2,1)S(1)}, f32[32,96,128]{2,1,0:T(8,128)S(1)}, f32[384,1024]{1,0:T(8,128)S(1)}) custom-call(f32[416,128]{1,0:T(8,128)S(1)} %collective-permute-done.1.ref, f32[384,1024]{1,0:T(8,128)S(1)} %get-tuple-element.43.refs_0_), custom_call_target="tpu_custom_call" | custom-call | tf_op jit(solution)/shard_map/pallas_call | solution.py:531
  16.3 1.2 %collective-permute-done.ref = f32[416,128]{1,0:T(8,128)S(1)} collective-permute-done((f32[416,128]{1,0:T(8,128)}, f32[416,128]{1,0:T(8,128)S(1)}, u32[]{:S(2)}, u32[]{:S(2)}) %collective-permute-start) | collective-permute-done | bytes 213024 | tf_op jit(solution)/shard_map/ppermute | solution.py:510
  17.5 0.0 copy-start.2
  17.5 3.3 %shard_map.109 = (bf16[96,384]{1,0:T(8,128)(2,1)S(1)}, f32[32,96,128]{2,1,0:T(8,128)S(1)}, f32[8,384,128]{2,1,0:T(8,128)S(1)}, f32[8,192,128]{2,1,0:T(8,128)S(1)...) custom-call(f32[416,128]{1,0:T(8,128)S(1)} %collective-permute-done., ...), custom_call_target="tpu_custom_call" | custom-call | tf_op jit(solution)/shard_map/pallas_call | solution.py:540
  20.8 0.2 collective-permute-start.3
  20.9 0.8 %collective-permute-start.4 = (f32[384,128]{1,0:T(8,128)S(1)}, f32[384,128]{1,0:T(8,128)S(1)}, u32[]{:S(2)}, u32[]{:S(2)}) collective-permute-start(f32[384,128]{1,0:T(8,128)S(1)} %get-tuple-element.55), channel_id=1, source_target_pairs={{1,2},{2,1},{3,4},{4,3},{5,6},{6,5},{7,8},{8,7},{9,10},{10,9},{11,... | collective-permute-start | bytes 589832 | tf_op jit(solution)/shard_map/ppermute | solution.py:553
  21.8 0.0 copy-done.2
  21.8 8.2 %shard_map.110.refs_0_ = f32[752,1024]{1,0:T(8,128)S(1)} custom-call(f32[5,2,8,8]{3,2,1,0:T(8,128)S(1)} %copy-done.2, f32[8,384,128]{2,1,0:T(8,128)S(1)} %get-tuple-element.46.q0, f32[8,192,128]{2,1,0:T(8,128)S(1)} %get-tuple-element.47.s1, f32[8,96,128]{2,1,0:T(8,128)S(1)} %get-tuple-element.48.s2, f32[8,48,128]{2,1,0:T(8,128)S(1)} %get-tuple-element.49.s3, ...), custom_call_target="tpu_custom_call" | custom-call | tf_op jit(solution)/shard_map/pallas_call | solution.py:554
  30.0 0.0 collective-permute-done.3.refs_1_
  30.0 0.0 collective-permute-done.4.refs_2_
  30.1 0.0 copy-start.3
  30.1 5.7 %shard_map.111 = (f32[8,384,128]{2,1,0:T(8,128)}, f32[8,128]{1,0:T(8,128)S(1)}, f32[8,128]{1,0:T(8,128)S(1)}, f32[8,128]{1,0:T(8,128)S(1)}, f32[8,128]{1,0:T(8,128)S(1)}) custom-call(f32[752,1024]{1,0:T(8,128)S(1)} %shard_map.110.refs_0_, f32[384,128]{1,0:T(8,128)S(1)} %collective-permute-done.3.refs_1_, f32[384,128]{1,0:T(8,128)S(1)} %collective-permute-done.4.refs_2_, ...), custom_call_target="tpu_custom_call" | custom-call | tf_op jit(solution)/shard_map/pallas_call | solution.py:565
  35.7 3.1 %collective-permute-start.5 = (f32[8,128]{1,0:T(8,128)S(1)}, f32[8,128]{1,0:T(8,128)S(1)}, u32[]{:S(2)}, u32[]{:S(2)}) collective-permute-start(f32[8,128]{1,0:T(8,128)S(1)} %get-tuple-element.71), channel_id=1, source_target_pairs={{0,1},{1,0},{2,3},{3,2},{4,5},{5,4},{6,7},{7,6},{8,9},{9,8},{10,11... | collective-permute-start | bytes 12296 | tf_op jit(solution)/shard_map/ppermute | solution.py:577
  38.8 1.4 %collective-permute-start.6 = (f32[8,128]{1,0:T(8,128)S(1)}, f32[8,128]{1,0:T(8,128)S(1)}, u32[]{:S(2)}, u32[]{:S(2)}) collective-permute-start(f32[8,128]{1,0:T(8,128)S(1)} %get-tuple-element.72), channel_id=1, source_target_pairs={{0,2},{1,3},{2,0},{3,1},{4,6},{5,7},{6,4},{7,5},{8,10},{9,11},{10,... | collective-permute-start | bytes 12296 | tf_op jit(solution)/shard_map/ppermute | solution.py:577
  40.3 0.0 collective-permute-start.7
  40.3 0.0 copy-done.3
  40.3 0.4 shard_map.112.match_ref
  40.7 0.0 collective-permute-done.5.b1
  40.7 1.7 %collective-permute-done.6.b2 = f32[8,128]{1,0:T(8,128)S(1)} collective-permute-done((f32[8,128]{1,0:T(8,128)S(1)}, f32[8,128]{1,0:T(8,128)S(1)}, u32[]{:S(2)}, u32[]{:S(2)}) %collective-permute-start.6) | collective-permute-done | bytes 4128 | tf_op jit(solution)/shard_map/ppermute | solution.py:577
  42.4 0.9 %collective-permute-done.7.b3 = f32[8,128]{1,0:T(8,128)S(1)} collective-permute-done((f32[8,128]{1,0:T(8,128)S(1)}, f32[8,128]{1,0:T(8,128)S(1)}, u32[]{:S(2)}, u32[]{:S(2)}) %collective-permute-start.7) | collective-permute-done | bytes 4128 | tf_op jit(solution)/shard_map/ppermute | solution.py:577
  43.3 0.9 %shard_map.113 = f32[1,1024]{1,0:T(1,128)} custom-call(s32[1]{0:T(128)S(6)} %copy.11.count_ref, bf16[512,1024]{1,0:T(8,128)(2,1)S(1)} %shard_map.112.match_ref, f32[8,128]{1,0:T(8,128)S(1)} %get-tuple-element.70.b0, f32[8,128]{1,0:T(8,128)S(1)} %collective-permute-done.5.b1, f32[8,128]{1,0:T(8,128)S(1)} %collective-permute-done.6.b2, ...), custom_call_target="tpu_custom_call" | custom-call | tf_op jit(solution)/shard_map/pallas_call | solution.py:579
Async XLA Ops:
  4.0 10.2 %collective-permute-start.2 = (f32[416,128]{1,0:T(8,128)}, f32[416,128]{1,0:T(8,128)S(1)}, u32[]{:S(2)}, u32[]{:S(2)}) collective-permute-start(f32[416,128]{1,0:T(8,128)} %get-tuple-element.40), channel_id=1, source_target_pairs={{0,1},{1,0},{2,3},{3,2},{4,5},{5,4},{6,7},{7,6},{8,9},{9,8},{10,11... | collective-permute-start | bytes 638984 | tf_op jit(solution)/shard_map/ppermute | solution.py:510
  4.5 10.7 %collective-permute-start.1 = (f32[416,128]{1,0:T(8,128)}, f32[416,128]{1,0:T(8,128)S(1)}, u32[]{:S(2)}, u32[]{:S(2)}) collective-permute-start(f32[416,128]{1,0:T(8,128)} %get-tuple-element.39), channel_id=1, source_target_pairs={{0,2},{1,3},{2,0},{3,1},{4,6},{5,7},{6,4},{7,5},{8,10},{9,11},{10,... | collective-permute-start | bytes 638984 | tf_op jit(solution)/shard_map/ppermute | solution.py:510
  7.1 10.4 %collective-permute-start = (f32[416,128]{1,0:T(8,128)}, f32[416,128]{1,0:T(8,128)S(1)}, u32[]{:S(2)}, u32[]{:S(2)}) collective-permute-start(f32[416,128]{1,0:T(8,128)} %get-tuple-element.38), channel_id=1, source_target_pairs={{0,3},{1,2},{2,1},{3,0},{4,7},{5,6},{6,5},{7,4},{8,11},{9,10},{10,... | collective-permute-start | bytes 638984 | tf_op jit(solution)/shard_map/ppermute | solution.py:510
  7.2 0.9 %copy-start = (f32[416,128]{1,0:T(8,128)S(1)}, f32[416,128]{1,0:T(8,128)}, u32[]{:S(2)}) copy-start(f32[416,128]{1,0:T(8,128)} %get-tuple-element.41.ref) | copy-start | bytes 638980
  9.2 0.8 %copy-start.1 = (f32[5,2,8,8]{3,2,1,0:T(8,128)S(1)}, f32[5,2,8,8]{3,2,1,0:T(8,128)}, u32[]{:S(2)}) copy-start(f32[5,2,8,8]{3,2,1,0:T(8,128)} %mix_ref.3) | copy-start | bytes 7684
  10.0 0.7 %copy-start.4 = (f32[5,2,17]{2,1,0:T(2,128)S(1)}, f32[5,2,17]{2,1,0:T(2,128)}, u32[]{:S(2)}) copy-start(f32[5,2,17]{2,1,0:T(2,128)} %across_ref.1) | copy-start | bytes 2044
  10.7 0.7 %copy-start.5 = (f32[5,2,17]{2,1,0:T(2,128)S(1)}, f32[5,2,17]{2,1,0:T(2,128)}, u32[]{:S(2)}) copy-start(f32[5,2,17]{2,1,0:T(2,128)} %along_ref.1) | copy-start | bytes 2044
  17.5 4.3 %copy-start.2 = (f32[5,2,8,8]{3,2,1,0:T(8,128)S(1)}, f32[5,2,8,8]{3,2,1,0:T(8,128)}, u32[]{:S(2)}) copy-start(f32[5,2,8,8]{3,2,1,0:T(8,128)} %mix_ref.3) | copy-start | bytes 7684
  20.8 9.3 %collective-permute-start.3 = (f32[384,128]{1,0:T(8,128)S(1)}, f32[384,128]{1,0:T(8,128)S(1)}, u32[]{:S(2)}, u32[]{:S(2)}) collective-permute-start(f32[384,128]{1,0:T(8,128)S(1)} %get-tuple-element.54), channel_id=1, source_target_pairs={{0,1},{1,0},{2,3},{3,2},{4,5},{5,4},{6,7},{7,6},{8,9},{9,8},{10,11... | collective-permute-start | bytes 589832 | tf_op jit(solution)/shard_map/ppermute | solution.py:552
  20.9 9.1 %collective-permute-start.4 = (f32[384,128]{1,0:T(8,128)S(1)}, f32[384,128]{1,0:T(8,128)S(1)}, u32[]{:S(2)}, u32[]{:S(2)}) collective-permute-start(f32[384,128]{1,0:T(8,128)S(1)} %get-tuple-element.55), channel_id=1, source_target_pairs={{1,2},{2,1},{3,4},{4,3},{5,6},{6,5},{7,8},{8,7},{9,10},{10,9},{11,... | collective-permute-start | bytes 589832 | tf_op jit(solution)/shard_map/ppermute | solution.py:553
  30.1 10.2 %copy-start.3 = (f32[8,256]{1,0:T(8,128)S(1)}, f32[8,256]{1,0:T(8,128)}, u32[]{:S(2)}) copy-start(f32[8,256]{1,0:T(8,128)} %get-tuple-element.69.slot_ref) | copy-start | bytes 24580
  35.7 5.0 %collective-permute-start.5 = (f32[8,128]{1,0:T(8,128)S(1)}, f32[8,128]{1,0:T(8,128)S(1)}, u32[]{:S(2)}, u32[]{:S(2)}) collective-permute-start(f32[8,128]{1,0:T(8,128)S(1)} %get-tuple-element.71), channel_id=1, source_target_pairs={{0,1},{1,0},{2,3},{3,2},{4,5},{5,4},{6,7},{7,6},{8,9},{9,8},{10,11... | collective-permute-start | bytes 12296 | tf_op jit(solution)/shard_map/ppermute | solution.py:577
  38.8 3.6 %collective-permute-start.6 = (f32[8,128]{1,0:T(8,128)S(1)}, f32[8,128]{1,0:T(8,128)S(1)}, u32[]{:S(2)}, u32[]{:S(2)}) collective-permute-start(f32[8,128]{1,0:T(8,128)S(1)} %get-tuple-element.72), channel_id=1, source_target_pairs={{0,2},{1,3},{2,0},{3,1},{4,6},{5,7},{6,4},{7,5},{8,10},{9,11},{10,... | collective-permute-start | bytes 12296 | tf_op jit(solution)/shard_map/ppermute | solution.py:577
  40.3 3.0 %collective-permute-start.7 = (f32[8,128]{1,0:T(8,128)S(1)}, f32[8,128]{1,0:T(8,128)S(1)}, u32[]{:S(2)}, u32[]{:S(2)}) collective-permute-start(f32[8,128]{1,0:T(8,128)S(1)} %get-tuple-element.73), channel_id=1, source_target_pairs={{0,3},{1,2},{2,1},{3,0},{4,7},{5,6},{6,5},{7,4},{8,11},{9,10},{10,... | collective-permute-start | bytes 12296 | tf_op jit(solution)/shard_map/ppermute | solution.py:577

commit v7 on v6

--- a/solution.py
+++ b/solution.py
@@ -318,9 +318,10 @@
                 line = MIX_ROW[level] + w * size + start
                 parts.append(ranked[line : line + chunk, r * CX : (r + 1) * CX])
             for z in range(PLANES):
-                total = parts[0] * mix_ref[level, r, z, 0]
-                for w in range(1, PLANES):
-                    total = total + parts[w] * mix_ref[level, r, z, w]
+                terms = [parts[w] * mix_ref[level, r, z, w] for w in range(PLANES)]
+                while len(terms) > 1:
+                    terms = [terms[i] + terms[i + 1] for i in range(0, len(terms), 2)]
+                total = terms[0]
                 if chunk == 24:
                     total = jnp.concatenate([total, jnp.zeros((8, CX), F32)], axis=0)
                 high, low = split(total)
@@ -335,20 +336,18 @@
         taps = across[lines, : 2 * step]
         for pair in range(PLANES // 2):
             part = slice(pair * 2 * CX, (pair + 1) * 2 * CX)
-            found = dot(taps, high_ref[lines, part])
-            found = found[:size] + found[step : step + size]
-            out_ref[rows, part] = found + dot(taps[:step], low_ref[lines, part])[:size]
-
-    along(0)
-    blend(0, 0)
-    blend(0, 1)
-    for level in range(1, LEVELS + 1):
+            high = high_ref[lines, part]
+            stack = jnp.concatenate([high, low_ref[lines, part]], axis=0)
+            double = jnp.concatenate([taps[:step], taps[:step]], axis=1)
+            found = dot(double, stack) + dot(taps[step:], high)
+            out_ref[rows, part] = found[:size]
+
+    for level in range(LEVELS + 1):
         along(level)
-    combine(0)
-    for level in range(1, LEVELS + 1):
+    for level in range(LEVELS + 1):
         blend(level, 0)
         blend(level, 1)
-    for level in range(1, LEVELS + 1):
+    for level in range(LEVELS + 1):
         combine(level)
 
 
@@ -384,6 +383,8 @@
             place = slice(K_OF[level] + r * step, K_OF[level] + (r + 1) * step)
             high_ref[place, part] = high[:, part]
             low_ref[place, part] = low[:, part]
+    for level in range(LEVELS + 1):
+        size, step = HEIGHTS[level], STEP[level]
         place = slice(K_OF[level], K_OF[level] + 2 * step)
         taps = across[TAP_ROW[level] : TAP_ROW[level] + 2 * step, : 2 * step]
         found = dot(taps, high_ref[place, :])

time: 44.5 us -> 44.2 us (level)
  no operation moved by 1% of the time
where the time goes in v7:
time: 44.2 us; the launch traced here: 43.9 us
  Pallas kernels  26.9 us (61%)
  starting transfers between devices  8.72 us (20%)
  waiting for transfers between devices  3.75 us (8%)
  local copies, waits for them, and re-layouts  3.09 us (7%)
  between operations  1.41 us (3%)
    pallas_call x1, Pallas kernels, body(): call(inner_kernel, [SMEM] + [VMEM] * 8, [shape(ALL_ROWS, HALF)], [pltpu.V...  8.2 us
    pallas_call x1, Pallas kernels, body(): call(outer_kernel, [VMEM] * (8 + 2 * PEERS), [shape(PLANES, NY, CX)] + [s...  5.48 us
    ppermute x3, starting transfers between devices, body(): lax.ppermute(samples[k], 'sect', swaps[k])  4.52 us
    pallas_call x1, Pallas kernels, body(): call(charge_kernel, [VMEM] * 3, kept + [shape(PLANES, size, CX) for size...  3.25 us
    ppermute x3, starting transfers between devices, body(): lax.ppermute(sends[k], 'sect', swaps[k])  3.18 us
    pallas_call x3, Pallas kernels, body(): call(brick_kernel, [VMEM] * (1 + len(total)), kept + [shape(TILES, HALF)]...  3.12 us
    unnamed x12, local copies, waits for them, and re-layouts  3.09 us
    pallas_call x1, Pallas kernels, body(): call(prep_kernel, [VMEM, VMEM, VMEM], [shape(LEVELS + 1, 2 * CX, 2 * CX,...  2.86 us
  transfers between devices with their start and end apart: 8, of which 3 were waited for; matrix products, arithmetic and copies ran while one was open for 0% of the time, Pallas kernels for 33%

profile of v7, /device:TPU:0, one launch (start us, length us, event | category | flops | bytes accessed | tf_op | source)
XLA Modules:
  0.0 43.9 jit_solution(10058719503727916732)
XLA Ops:
  1.3 2.7 %shard_map.104 = (f32[416,128]{1,0:T(8,128)}, f32[416,128]{1,0:T(8,128)}, f32[416,128]{1,0:T(8,128)}, f32[416,128]{1,0:T(8,128)}, f32[8,256]{1,0:T(8,128)}) custom-call(s32[1]{0:T(128)S(6)} %copy.11.count_ref, f32[1,1024]{1,0:T(1,128)} %bitcast.4, f32[8,1024]{1,0:T(8,128)} %planes_hbm.1, f32[1024,128]{1,0:T(8,128)} %cells_hbm.1, s32[1,256]{1,0:T(1,128)} %bitcast.6, ...), custom_call_target="tpu_custom_call" | custom-call | tf_op jit(solution)/shard_map/pallas_call | solution.py:488
  4.0 0.5 %collective-permute-start.2 = (f32[416,128]{1,0:T(8,128)}, f32[416,128]{1,0:T(8,128)S(1)}, u32[]{:S(2)}, u32[]{:S(2)}) collective-permute-start(f32[416,128]{1,0:T(8,128)} %get-tuple-element.40), channel_id=1, source_target_pairs={{0,1},{1,0},{2,3},{3,2},{4,5},{5,4},{6,7},{7,6},{8,9},{9,8},{10,11... | collective-permute-start | bytes 638984 | tf_op jit(solution)/shard_map/ppermute | solution.py:511
  4.5 2.6 %collective-permute-start.1 = (f32[416,128]{1,0:T(8,128)}, f32[416,128]{1,0:T(8,128)S(1)}, u32[]{:S(2)}, u32[]{:S(2)}) collective-permute-start(f32[416,128]{1,0:T(8,128)} %get-tuple-element.39), channel_id=1, source_target_pairs={{0,2},{1,3},{2,0},{3,1},{4,6},{5,7},{6,4},{7,5},{8,10},{9,11},{10,... | collective-permute-start | bytes 638984 | tf_op jit(solution)/shard_map/ppermute | solution.py:511
  7.1 0.1 collective-permute-start
  7.2 0.0 copy-start
  7.2 0.9 %copy-done = f32[416,128]{1,0:T(8,128)S(1)} copy-done((f32[416,128]{1,0:T(8,128)S(1)}, f32[416,128]{1,0:T(8,128)}, u32[]{:S(2)}) %copy-start) | copy-done | bytes 213016
  8.1 1.0 %shard_map.105 = (bf16[96,384]{1,0:T(8,128)(2,1)S(1)}, f32[32,96,128]{2,1,0:T(8,128)S(1)}, f32[384,1024]{1,0:T(8,128)S(1)}) custom-call(f32[416,128]{1,0:T(8,128)S(1)} %copy-done), custom_call_target="tpu_custom_call" | custom-call | tf_op jit(solution)/shard_map/pallas_call | solution.py:532
  9.2 0.0 copy-start.1
  9.2 0.8 %copy-done.1 = f32[5,2,8,8]{3,2,1,0:T(8,128)S(1)} copy-done((f32[5,2,8,8]{3,2,1,0:T(8,128)S(1)}, f32[5,2,8,8]{3,2,1,0:T(8,128)}, u32[]{:S(2)}) %copy-start.1) | copy-done | bytes 2584
  10.0 0.0 copy-start.4
  10.0 0.7 %copy-done.4 = f32[5,2,17]{2,1,0:T(2,128)S(1)} copy-done((f32[5,2,17]{2,1,0:T(2,128)S(1)}, f32[5,2,17]{2,1,0:T(2,128)}, u32[]{:S(2)}) %copy-start.4) | copy-done | bytes 704
  10.7 0.0 copy-start.5
  10.7 0.7 %copy-done.5 = f32[5,2,17]{2,1,0:T(2,128)S(1)} copy-done((f32[5,2,17]{2,1,0:T(2,128)S(1)}, f32[5,2,17]{2,1,0:T(2,128)}, u32[]{:S(2)}) %copy-start.5) | copy-done | bytes 704
  11.3 2.9 %shard_map.108 = (bf16[5,256,256]{2,1,0:T(8,128)(2,1)S(1)}, bf16[5,128,256]{2,1,0:T(8,128)(2,1)S(1)}, bf16[1504,768]{1,0:T(8,128)(2,1)S(1)}, bf16[5,128,256]{2,1...) custom-call(f32[5,2,17]{2,1,0:T(2,128)S(1)} %copy-done.4, ...), custom_call_target="tpu_custom_call" | custom-call | tf_op jit(solution)/shard_map/pallas_call | solution.py:512
  14.2 0.0 collective-permute-done.2.ref
  14.2 1.0 %shard_map.106 = (bf16[96,384]{1,0:T(8,128)(2,1)S(1)}, f32[32,96,128]{2,1,0:T(8,128)S(1)}, f32[384,1024]{1,0:T(8,128)S(1)}) custom-call(f32[416,128]{1,0:T(8,128)S(1)} %collective-permute-done.2.ref, f32[384,1024]{1,0:T(8,128)S(1)} %get-tuple-element.42.refs_0_), custom_call_target="tpu_custom_call" | custom-call | tf_op jit(solution)/shard_map/pallas_call | solution.py:532
  15.3 0.0 collective-permute-done.1.ref
  15.3 1.0 %shard_map.107 = (bf16[96,384]{1,0:T(8,128)(2,1)S(1)}, f32[32,96,128]{2,1,0:T(8,128)S(1)}, f32[384,1024]{1,0:T(8,128)S(1)}) custom-call(f32[416,128]{1,0:T(8,128)S(1)} %collective-permute-done.1.ref, f32[384,1024]{1,0:T(8,128)S(1)} %get-tuple-element.43.refs_0_), custom_call_target="tpu_custom_call" | custom-call | tf_op jit(solution)/shard_map/pallas_call | solution.py:532
  16.3 1.2 %collective-permute-done.ref = f32[416,128]{1,0:T(8,128)S(1)} collective-permute-done((f32[416,128]{1,0:T(8,128)}, f32[416,128]{1,0:T(8,128)S(1)}, u32[]{:S(2)}, u32[]{:S(2)}) %collective-permute-start) | collective-permute-done | bytes 213024 | tf_op jit(solution)/shard_map/ppermute | solution.py:511
  17.5 0.0 copy-start.2
  17.5 3.3 %shard_map.109 = (bf16[96,384]{1,0:T(8,128)(2,1)S(1)}, f32[32,96,128]{2,1,0:T(8,128)S(1)}, f32[8,384,128]{2,1,0:T(8,128)S(1)}, f32[8,192,128]{2,1,0:T(8,128)S(1)...) custom-call(f32[416,128]{1,0:T(8,128)S(1)} %collective-permute-done., ...), custom_call_target="tpu_custom_call" | custom-call | tf_op jit(solution)/shard_map/pallas_call | solution.py:541
  20.8 0.2 collective-permute-start.3
  20.9 0.8 %collective-permute-start.4 = (f32[384,128]{1,0:T(8,128)S(1)}, f32[384,128]{1,0:T(8,128)S(1)}, u32[]{:S(2)}, u32[]{:S(2)}) collective-permute-start(f32[384,128]{1,0:T(8,128)S(1)} %get-tuple-element.55), channel_id=1, source_target_pairs={{1,2},{2,1},{3,4},{4,3},{5,6},{6,5},{7,8},{8,7},{9,10},{10,9},{11,... | collective-permute-start | bytes 589832 | tf_op jit(solution)/shard_map/ppermute | solution.py:554
  21.8 0.0 copy-done.2
  21.8 8.2 %shard_map.110.refs_0_ = f32[752,1024]{1,0:T(8,128)S(1)} custom-call(f32[5,2,8,8]{3,2,1,0:T(8,128)S(1)} %copy-done.2, f32[8,384,128]{2,1,0:T(8,128)S(1)} %get-tuple-element.46.q0, f32[8,192,128]{2,1,0:T(8,128)S(1)} %get-tuple-element.47.s1, f32[8,96,128]{2,1,0:T(8,128)S(1)} %get-tuple-element.48.s2, f32[8,48,128]{2,1,0:T(8,128)S(1)} %get-tuple-element.49.s3, ...), custom_call_target="tpu_custom_call" | custom-call | tf_op jit(solution)/shard_map/pallas_call | solution.py:555
  30.0 0.0 collective-permute-done.3.refs_1_
  30.0 0.0 collective-permute-done.4.refs_2_
  30.0 0.0 copy-start.3
  30.0 5.5 %shard_map.111 = (f32[8,384,128]{2,1,0:T(8,128)}, f32[8,128]{1,0:T(8,128)S(1)}, f32[8,128]{1,0:T(8,128)S(1)}, f32[8,128]{1,0:T(8,128)S(1)}, f32[8,128]{1,0:T(8,128)S(1)}) custom-call(f32[752,1024]{1,0:T(8,128)S(1)} %shard_map.110.refs_0_, f32[384,128]{1,0:T(8,128)S(1)} %collective-permute-done.3.refs_1_, f32[384,128]{1,0:T(8,128)S(1)} %collective-permute-done.4.refs_2_, ...), custom_call_target="tpu_custom_call" | custom-call | tf_op jit(solution)/shard_map/pallas_call | solution.py:566
  35.5 3.1 %collective-permute-start.5 = (f32[8,128]{1,0:T(8,128)S(1)}, f32[8,128]{1,0:T(8,128)S(1)}, u32[]{:S(2)}, u32[]{:S(2)}) collective-permute-start(f32[8,128]{1,0:T(8,128)S(1)} %get-tuple-element.71), channel_id=1, source_target_pairs={{0,1},{1,0},{2,3},{3,2},{4,5},{5,4},{6,7},{7,6},{8,9},{9,8},{10,11... | collective-permute-start | bytes 12296 | tf_op jit(solution)/shard_map/ppermute | solution.py:578
  38.6 1.4 %collective-permute-start.6 = (f32[8,128]{1,0:T(8,128)S(1)}, f32[8,128]{1,0:T(8,128)S(1)}, u32[]{:S(2)}, u32[]{:S(2)}) collective-permute-start(f32[8,128]{1,0:T(8,128)S(1)} %get-tuple-element.72), channel_id=1, source_target_pairs={{0,2},{1,3},{2,0},{3,1},{4,6},{5,7},{6,4},{7,5},{8,10},{9,11},{10,... | collective-permute-start | bytes 12296 | tf_op jit(solution)/shard_map/ppermute | solution.py:578
  40.0 0.0 collective-permute-start.7
  40.0 0.0 copy-done.3
  40.0 0.4 shard_map.112.match_ref
  40.5 0.0 collective-permute-done.5.b1
  40.5 1.7 %collective-permute-done.6.b2 = f32[8,128]{1,0:T(8,128)S(1)} collective-permute-done((f32[8,128]{1,0:T(8,128)S(1)}, f32[8,128]{1,0:T(8,128)S(1)}, u32[]{:S(2)}, u32[]{:S(2)}) %collective-permute-start.6) | collective-permute-done | bytes 4128 | tf_op jit(solution)/shard_map/ppermute | solution.py:578
  42.2 0.9 %collective-permute-done.7.b3 = f32[8,128]{1,0:T(8,128)S(1)} collective-permute-done((f32[8,128]{1,0:T(8,128)S(1)}, f32[8,128]{1,0:T(8,128)S(1)}, u32[]{:S(2)}, u32[]{:S(2)}) %collective-permute-start.7) | collective-permute-done | bytes 4128 | tf_op jit(solution)/shard_map/ppermute | solution.py:578
  43.1 0.9 %shard_map.113 = f32[1,1024]{1,0:T(1,128)} custom-call(s32[1]{0:T(128)S(6)} %copy.11.count_ref, bf16[512,1024]{1,0:T(8,128)(2,1)S(1)} %shard_map.112.match_ref, f32[8,128]{1,0:T(8,128)S(1)} %get-tuple-element.70.b0, f32[8,128]{1,0:T(8,128)S(1)} %collective-permute-done.5.b1, f32[8,128]{1,0:T(8,128)S(1)} %collective-permute-done.6.b2, ...), custom_call_target="tpu_custom_call" | custom-call | tf_op jit(solution)/shard_map/pallas_call | solution.py:580
Async XLA Ops:
  4.0 10.2 %collective-permute-start.2 = (f32[416,128]{1,0:T(8,128)}, f32[416,128]{1,0:T(8,128)S(1)}, u32[]{:S(2)}, u32[]{:S(2)}) collective-permute-start(f32[416,128]{1,0:T(8,128)} %get-tuple-element.40), channel_id=1, source_target_pairs={{0,1},{1,0},{2,3},{3,2},{4,5},{5,4},{6,7},{7,6},{8,9},{9,8},{10,11... | collective-permute-start | bytes 638984 | tf_op jit(solution)/shard_map/ppermute | solution.py:511
  4.5 10.7 %collective-permute-start.1 = (f32[416,128]{1,0:T(8,128)}, f32[416,128]{1,0:T(8,128)S(1)}, u32[]{:S(2)}, u32[]{:S(2)}) collective-permute-start(f32[416,128]{1,0:T(8,128)} %get-tuple-element.39), channel_id=1, source_target_pairs={{0,2},{1,3},{2,0},{3,1},{4,6},{5,7},{6,4},{7,5},{8,10},{9,11},{10,... | collective-permute-start | bytes 638984 | tf_op jit(solution)/shard_map/ppermute | solution.py:511
  7.1 10.4 %collective-permute-start = (f32[416,128]{1,0:T(8,128)}, f32[416,128]{1,0:T(8,128)S(1)}, u32[]{:S(2)}, u32[]{:S(2)}) collective-permute-start(f32[416,128]{1,0:T(8,128)} %get-tuple-element.38), channel_id=1, source_target_pairs={{0,3},{1,2},{2,1},{3,0},{4,7},{5,6},{6,5},{7,4},{8,11},{9,10},{10,... | collective-permute-start | bytes 638984 | tf_op jit(solution)/shard_map/ppermute | solution.py:511
  7.2 0.9 %copy-start = (f32[416,128]{1,0:T(8,128)S(1)}, f32[416,128]{1,0:T(8,128)}, u32[]{:S(2)}) copy-start(f32[416,128]{1,0:T(8,128)} %get-tuple-element.41.ref) | copy-start | bytes 638980
  9.2 0.8 %copy-start.1 = (f32[5,2,8,8]{3,2,1,0:T(8,128)S(1)}, f32[5,2,8,8]{3,2,1,0:T(8,128)}, u32[]{:S(2)}) copy-start(f32[5,2,8,8]{3,2,1,0:T(8,128)} %mix_ref.3) | copy-start | bytes 7684
  10.0 0.7 %copy-start.4 = (f32[5,2,17]{2,1,0:T(2,128)S(1)}, f32[5,2,17]{2,1,0:T(2,128)}, u32[]{:S(2)}) copy-start(f32[5,2,17]{2,1,0:T(2,128)} %across_ref.1) | copy-start | bytes 2044
  10.7 0.7 %copy-start.5 = (f32[5,2,17]{2,1,0:T(2,128)S(1)}, f32[5,2,17]{2,1,0:T(2,128)}, u32[]{:S(2)}) copy-start(f32[5,2,17]{2,1,0:T(2,128)} %along_ref.1) | copy-start | bytes 2044
  17.5 4.3 %copy-start.2 = (f32[5,2,8,8]{3,2,1,0:T(8,128)S(1)}, f32[5,2,8,8]{3,2,1,0:T(8,128)}, u32[]{:S(2)}) copy-start(f32[5,2,8,8]{3,2,1,0:T(8,128)} %mix_ref.3) | copy-start | bytes 7684
  20.8 9.2 %collective-permute-start.3 = (f32[384,128]{1,0:T(8,128)S(1)}, f32[384,128]{1,0:T(8,128)S(1)}, u32[]{:S(2)}, u32[]{:S(2)}) collective-permute-start(f32[384,128]{1,0:T(8,128)S(1)} %get-tuple-element.54), channel_id=1, source_target_pairs={{0,1},{1,0},{2,3},{3,2},{4,5},{5,4},{6,7},{7,6},{8,9},{9,8},{10,11... | collective-permute-start | bytes 589832 | tf_op jit(solution)/shard_map/ppermute | solution.py:553
  20.9 9.1 %collective-permute-start.4 = (f32[384,128]{1,0:T(8,128)S(1)}, f32[384,128]{1,0:T(8,128)S(1)}, u32[]{:S(2)}, u32[]{:S(2)}) collective-permute-start(f32[384,128]{1,0:T(8,128)S(1)} %get-tuple-element.55), channel_id=1, source_target_pairs={{1,2},{2,1},{3,4},{4,3},{5,6},{6,5},{7,8},{8,7},{9,10},{10,9},{11,... | collective-permute-start | bytes 589832 | tf_op jit(solution)/shard_map/ppermute | solution.py:554
  30.0 10.0 %copy-start.3 = (f32[8,256]{1,0:T(8,128)S(1)}, f32[8,256]{1,0:T(8,128)}, u32[]{:S(2)}) copy-start(f32[8,256]{1,0:T(8,128)} %get-tuple-element.69.slot_ref) | copy-start | bytes 24580
  35.5 5.0 %collective-permute-start.5 = (f32[8,128]{1,0:T(8,128)S(1)}, f32[8,128]{1,0:T(8,128)S(1)}, u32[]{:S(2)}, u32[]{:S(2)}) collective-permute-start(f32[8,128]{1,0:T(8,128)S(1)} %get-tuple-element.71), channel_id=1, source_target_pairs={{0,1},{1,0},{2,3},{3,2},{4,5},{5,4},{6,7},{7,6},{8,9},{9,8},{10,11... | collective-permute-start | bytes 12296 | tf_op jit(solution)/shard_map/ppermute | solution.py:578
  38.6 3.6 %collective-permute-start.6 = (f32[8,128]{1,0:T(8,128)S(1)}, f32[8,128]{1,0:T(8,128)S(1)}, u32[]{:S(2)}, u32[]{:S(2)}) collective-permute-start(f32[8,128]{1,0:T(8,128)S(1)} %get-tuple-element.72), channel_id=1, source_target_pairs={{0,2},{1,3},{2,0},{3,1},{4,6},{5,7},{6,4},{7,5},{8,10},{9,11},{10,... | collective-permute-start | bytes 12296 | tf_op jit(solution)/shard_map/ppermute | solution.py:578
  40.0 3.0 %collective-permute-start.7 = (f32[8,128]{1,0:T(8,128)S(1)}, f32[8,128]{1,0:T(8,128)S(1)}, u32[]{:S(2)}, u32[]{:S(2)}) collective-permute-start(f32[8,128]{1,0:T(8,128)S(1)} %get-tuple-element.73), channel_id=1, source_target_pairs={{0,3},{1,2},{2,1},{3,0},{4,7},{5,6},{6,5},{7,4},{8,11},{9,10},{10,... | collective-permute-start | bytes 12296 | tf_op jit(solution)/shard_map/ppermute | solution.py:578

commit v8 on v6

--- a/solution.py
+++ b/solution.py
@@ -384,6 +384,8 @@
             place = slice(K_OF[level] + r * step, K_OF[level] + (r + 1) * step)
             high_ref[place, part] = high[:, part]
             low_ref[place, part] = low[:, part]
+    for level in range(LEVELS + 1):
+        size, step = HEIGHTS[level], STEP[level]
         place = slice(K_OF[level], K_OF[level] + 2 * step)
         taps = across[TAP_ROW[level] : TAP_ROW[level] + 2 * step, : 2 * step]
         found = dot(taps, high_ref[place, :])

time: 44.5 us -> 44.3 us (level)
  no operation moved by 1% of the time
where the time goes in v8:
time: 44.3 us; the launch traced here: 44 us
  Pallas kernels  27 us (61%)
  starting transfers between devices  8.72 us (20%)
  waiting for transfers between devices  3.76 us (8%)
  local copies, waits for them, and re-layouts  3.09 us (7%)
  between operations  1.41 us (3%)
    pallas_call x1, Pallas kernels, body(): call(inner_kernel, [SMEM] + [VMEM] * 8, [shape(ALL_ROWS, HALF)], [pltpu.V...  8.23 us
    pallas_call x1, Pallas kernels, body(): call(outer_kernel, [VMEM] * (8 + 2 * PEERS), [shape(PLANES, NY, CX)] + [s...  5.48 us
    ppermute x3, starting transfers between devices, body(): lax.ppermute(samples[k], 'sect', swaps[k])  4.52 us
    pallas_call x1, Pallas kernels, body(): call(charge_kernel, [VMEM] * 3, kept + [shape(PLANES, size, CX) for size...  3.25 us
    ppermute x3, starting transfers between devices, body(): lax.ppermute(sends[k], 'sect', swaps[k])  3.18 us
    pallas_call x3, Pallas kernels, body(): call(brick_kernel, [VMEM] * (1 + len(total)), kept + [shape(TILES, HALF)]...  3.12 us
    unnamed x12, local copies, waits for them, and re-layouts  3.09 us
    pallas_call x1, Pallas kernels, body(): call(prep_kernel, [VMEM, VMEM, VMEM], [shape(LEVELS + 1, 2 * CX, 2 * CX,...  2.86 us
  transfers between devices with their start and end apart: 8, of which 3 were waited for; matrix products, arithmetic and copies ran while one was open for 0% of the time, Pallas kernels for 33%

profile of v8, /device:TPU:0, one launch (start us, length us, event | category | flops | bytes accessed | tf_op | source)
XLA Modules:
  0.0 44.0 jit_solution(17992243667615790904)
XLA Ops:
  1.3 2.7 %shard_map.104 = (f32[416,128]{1,0:T(8,128)}, f32[416,128]{1,0:T(8,128)}, f32[416,128]{1,0:T(8,128)}, f32[416,128]{1,0:T(8,128)}, f32[8,256]{1,0:T(8,128)}) custom-call(s32[1]{0:T(128)S(6)} %copy.11.count_ref, f32[1,1024]{1,0:T(1,128)} %bitcast.4, f32[8,1024]{1,0:T(8,128)} %planes_hbm.1, f32[1024,128]{1,0:T(8,128)} %cells_hbm.1, s32[1,256]{1,0:T(1,128)} %bitcast.6, ...), custom_call_target="tpu_custom_call" | custom-call | tf_op jit(solution)/shard_map/pallas_call | solution.py:489
  4.0 0.5 %collective-permute-start.2 = (f32[416,128]{1,0:T(8,128)}, f32[416,128]{1,0:T(8,128)S(1)}, u32[]{:S(2)}, u32[]{:S(2)}) collective-permute-start(f32[416,128]{1,0:T(8,128)} %get-tuple-element.40), channel_id=1, source_target_pairs={{0,1},{1,0},{2,3},{3,2},{4,5},{5,4},{6,7},{7,6},{8,9},{9,8},{10,11... | collective-permute-start | bytes 638984 | tf_op jit(solution)/shard_map/ppermute | solution.py:512
  4.5 2.6 %collective-permute-start.1 = (f32[416,128]{1,0:T(8,128)}, f32[416,128]{1,0:T(8,128)S(1)}, u32[]{:S(2)}, u32[]{:S(2)}) collective-permute-start(f32[416,128]{1,0:T(8,128)} %get-tuple-element.39), channel_id=1, source_target_pairs={{0,2},{1,3},{2,0},{3,1},{4,6},{5,7},{6,4},{7,5},{8,10},{9,11},{10,... | collective-permute-start | bytes 638984 | tf_op jit(solution)/shard_map/ppermute | solution.py:512
  7.1 0.1 collective-permute-start
  7.2 0.0 copy-start
  7.2 0.9 %copy-done = f32[416,128]{1,0:T(8,128)S(1)} copy-done((f32[416,128]{1,0:T(8,128)S(1)}, f32[416,128]{1,0:T(8,128)}, u32[]{:S(2)}) %copy-start) | copy-done | bytes 213016
  8.1 1.0 %shard_map.105 = (bf16[96,384]{1,0:T(8,128)(2,1)S(1)}, f32[32,96,128]{2,1,0:T(8,128)S(1)}, f32[384,1024]{1,0:T(8,128)S(1)}) custom-call(f32[416,128]{1,0:T(8,128)S(1)} %copy-done), custom_call_target="tpu_custom_call" | custom-call | tf_op jit(solution)/shard_map/pallas_call | solution.py:533
  9.2 0.0 copy-start.1
  9.2 0.8 %copy-done.1 = f32[5,2,8,8]{3,2,1,0:T(8,128)S(1)} copy-done((f32[5,2,8,8]{3,2,1,0:T(8,128)S(1)}, f32[5,2,8,8]{3,2,1,0:T(8,128)}, u32[]{:S(2)}) %copy-start.1) | copy-done | bytes 2584
  10.0 0.0 copy-start.4
  10.0 0.7 %copy-done.4 = f32[5,2,17]{2,1,0:T(2,128)S(1)} copy-done((f32[5,2,17]{2,1,0:T(2,128)S(1)}, f32[5,2,17]{2,1,0:T(2,128)}, u32[]{:S(2)}) %copy-start.4) | copy-done | bytes 704
  10.7 0.0 copy-start.5
  10.7 0.7 %copy-done.5 = f32[5,2,17]{2,1,0:T(2,128)S(1)} copy-done((f32[5,2,17]{2,1,0:T(2,128)S(1)}, f32[5,2,17]{2,1,0:T(2,128)}, u32[]{:S(2)}) %copy-start.5) | copy-done | bytes 704
  11.3 2.9 %shard_map.108 = (bf16[5,256,256]{2,1,0:T(8,128)(2,1)S(1)}, bf16[5,128,256]{2,1,0:T(8,128)(2,1)S(1)}, bf16[1504,768]{1,0:T(8,128)(2,1)S(1)}, bf16[5,128,256]{2,1...) custom-call(f32[5,2,17]{2,1,0:T(2,128)S(1)} %copy-done.4, ...), custom_call_target="tpu_custom_call" | custom-call | tf_op jit(solution)/shard_map/pallas_call | solution.py:513
  14.2 0.0 collective-permute-done.2.ref
  14.2 1.0 %shard_map.106 = (bf16[96,384]{1,0:T(8,128)(2,1)S(1)}, f32[32,96,128]{2,1,0:T(8,128)S(1)}, f32[384,1024]{1,0:T(8,128)S(1)}) custom-call(f32[416,128]{1,0:T(8,128)S(1)} %collective-permute-done.2.ref, f32[384,1024]{1,0:T(8,128)S(1)} %get-tuple-element.42.refs_0_), custom_call_target="tpu_custom_call" | custom-call | tf_op jit(solution)/shard_map/pallas_call | solution.py:533
  15.3 0.0 collective-permute-done.1.ref
  15.3 1.0 %shard_map.107 = (bf16[96,384]{1,0:T(8,128)(2,1)S(1)}, f32[32,96,128]{2,1,0:T(8,128)S(1)}, f32[384,1024]{1,0:T(8,128)S(1)}) custom-call(f32[416,128]{1,0:T(8,128)S(1)} %collective-permute-done.1.ref, f32[384,1024]{1,0:T(8,128)S(1)} %get-tuple-element.43.refs_0_), custom_call_target="tpu_custom_call" | custom-call | tf_op jit(solution)/shard_map/pallas_call | solution.py:533
  16.3 1.2 %collective-permute-done.ref = f32[416,128]{1,0:T(8,128)S(1)} collective-permute-done((f32[416,128]{1,0:T(8,128)}, f32[416,128]{1,0:T(8,128)S(1)}, u32[]{:S(2)}, u32[]{:S(2)}) %collective-permute-start) | collective-permute-done | bytes 213024 | tf_op jit(solution)/shard_map/ppermute | solution.py:512
  17.5 0.0 copy-start.2
  17.5 3.3 %shard_map.109 = (bf16[96,384]{1,0:T(8,128)(2,1)S(1)}, f32[32,96,128]{2,1,0:T(8,128)S(1)}, f32[8,384,128]{2,1,0:T(8,128)S(1)}, f32[8,192,128]{2,1,0:T(8,128)S(1)...) custom-call(f32[416,128]{1,0:T(8,128)S(1)} %collective-permute-done., ...), custom_call_target="tpu_custom_call" | custom-call | tf_op jit(solution)/shard_map/pallas_call | solution.py:542
  20.8 0.2 collective-permute-start.3
  20.9 0.8 %collective-permute-start.4 = (f32[384,128]{1,0:T(8,128)S(1)}, f32[384,128]{1,0:T(8,128)S(1)}, u32[]{:S(2)}, u32[]{:S(2)}) collective-permute-start(f32[384,128]{1,0:T(8,128)S(1)} %get-tuple-element.55), channel_id=1, source_target_pairs={{1,2},{2,1},{3,4},{4,3},{5,6},{6,5},{7,8},{8,7},{9,10},{10,9},{11,... | collective-permute-start | bytes 589832 | tf_op jit(solution)/shard_map/ppermute | solution.py:555
  21.8 0.0 copy-done.2
  21.8 8.2 %shard_map.110.refs_0_ = f32[752,1024]{1,0:T(8,128)S(1)} custom-call(f32[5,2,8,8]{3,2,1,0:T(8,128)S(1)} %copy-done.2, f32[8,384,128]{2,1,0:T(8,128)S(1)} %get-tuple-element.46.q0, f32[8,192,128]{2,1,0:T(8,128)S(1)} %get-tuple-element.47.s1, f32[8,96,128]{2,1,0:T(8,128)S(1)} %get-tuple-element.48.s2, f32[8,48,128]{2,1,0:T(8,128)S(1)} %get-tuple-element.49.s3, ...), custom_call_target="tpu_custom_call" | custom-call | tf_op jit(solution)/shard_map/pallas_call | solution.py:556
  30.0 0.0 collective-permute-done.3.refs_1_
  30.0 0.0 collective-permute-done.4.refs_2_
  30.1 0.0 copy-start.3
  30.1 5.5 %shard_map.111 = (f32[8,384,128]{2,1,0:T(8,128)}, f32[8,128]{1,0:T(8,128)S(1)}, f32[8,128]{1,0:T(8,128)S(1)}, f32[8,128]{1,0:T(8,128)S(1)}, f32[8,128]{1,0:T(8,128)S(1)}) custom-call(f32[752,1024]{1,0:T(8,128)S(1)} %shard_map.110.refs_0_, f32[384,128]{1,0:T(8,128)S(1)} %collective-permute-done.3.refs_1_, f32[384,128]{1,0:T(8,128)S(1)} %collective-permute-done.4.refs_2_, ...), custom_call_target="tpu_custom_call" | custom-call | tf_op jit(solution)/shard_map/pallas_call | solution.py:567
  35.5 3.1 %collective-permute-start.5 = (f32[8,128]{1,0:T(8,128)S(1)}, f32[8,128]{1,0:T(8,128)S(1)}, u32[]{:S(2)}, u32[]{:S(2)}) collective-permute-start(f32[8,128]{1,0:T(8,128)S(1)} %get-tuple-element.71), channel_id=1, source_target_pairs={{0,1},{1,0},{2,3},{3,2},{4,5},{5,4},{6,7},{7,6},{8,9},{9,8},{10,11... | collective-permute-start | bytes 12296 | tf_op jit(solution)/shard_map/ppermute | solution.py:579
  38.6 1.4 %collective-permute-start.6 = (f32[8,128]{1,0:T(8,128)S(1)}, f32[8,128]{1,0:T(8,128)S(1)}, u32[]{:S(2)}, u32[]{:S(2)}) collective-permute-start(f32[8,128]{1,0:T(8,128)S(1)} %get-tuple-element.72), channel_id=1, source_target_pairs={{0,2},{1,3},{2,0},{3,1},{4,6},{5,7},{6,4},{7,5},{8,10},{9,11},{10,... | collective-permute-start | bytes 12296 | tf_op jit(solution)/shard_map/ppermute | solution.py:579
  40.1 0.0 collective-permute-start.7
  40.1 0.0 copy-done.3
  40.1 0.4 shard_map.112.match_ref
  40.5 0.0 collective-permute-done.5.b1
  40.5 1.7 %collective-permute-done.6.b2 = f32[8,128]{1,0:T(8,128)S(1)} collective-permute-done((f32[8,128]{1,0:T(8,128)S(1)}, f32[8,128]{1,0:T(8,128)S(1)}, u32[]{:S(2)}, u32[]{:S(2)}) %collective-permute-start.6) | collective-permute-done | bytes 4128 | tf_op jit(solution)/shard_map/ppermute | solution.py:579
  42.2 0.9 %collective-permute-done.7.b3 = f32[8,128]{1,0:T(8,128)S(1)} collective-permute-done((f32[8,128]{1,0:T(8,128)S(1)}, f32[8,128]{1,0:T(8,128)S(1)}, u32[]{:S(2)}, u32[]{:S(2)}) %collective-permute-start.7) | collective-permute-done | bytes 4128 | tf_op jit(solution)/shard_map/ppermute | solution.py:579
  43.1 0.9 %shard_map.113 = f32[1,1024]{1,0:T(1,128)} custom-call(s32[1]{0:T(128)S(6)} %copy.11.count_ref, bf16[512,1024]{1,0:T(8,128)(2,1)S(1)} %shard_map.112.match_ref, f32[8,128]{1,0:T(8,128)S(1)} %get-tuple-element.70.b0, f32[8,128]{1,0:T(8,128)S(1)} %collective-permute-done.5.b1, f32[8,128]{1,0:T(8,128)S(1)} %collective-permute-done.6.b2, ...), custom_call_target="tpu_custom_call" | custom-call | tf_op jit(solution)/shard_map/pallas_call | solution.py:581
Async XLA Ops:
  4.0 10.2 %collective-permute-start.2 = (f32[416,128]{1,0:T(8,128)}, f32[416,128]{1,0:T(8,128)S(1)}, u32[]{:S(2)}, u32[]{:S(2)}) collective-permute-start(f32[416,128]{1,0:T(8,128)} %get-tuple-element.40), channel_id=1, source_target_pairs={{0,1},{1,0},{2,3},{3,2},{4,5},{5,4},{6,7},{7,6},{8,9},{9,8},{10,11... | collective-permute-start | bytes 638984 | tf_op jit(solution)/shard_map/ppermute | solution.py:512
  4.5 10.7 %collective-permute-start.1 = (f32[416,128]{1,0:T(8,128)}, f32[416,128]{1,0:T(8,128)S(1)}, u32[]{:S(2)}, u32[]{:S(2)}) collective-permute-start(f32[416,128]{1,0:T(8,128)} %get-tuple-element.39), channel_id=1, source_target_pairs={{0,2},{1,3},{2,0},{3,1},{4,6},{5,7},{6,4},{7,5},{8,10},{9,11},{10,... | collective-permute-start | bytes 638984 | tf_op jit(solution)/shard_map/ppermute | solution.py:512
  7.1 10.4 %collective-permute-start = (f32[416,128]{1,0:T(8,128)}, f32[416,128]{1,0:T(8,128)S(1)}, u32[]{:S(2)}, u32[]{:S(2)}) collective-permute-start(f32[416,128]{1,0:T(8,128)} %get-tuple-element.38), channel_id=1, source_target_pairs={{0,3},{1,2},{2,1},{3,0},{4,7},{5,6},{6,5},{7,4},{8,11},{9,10},{10,... | collective-permute-start | bytes 638984 | tf_op jit(solution)/shard_map/ppermute | solution.py:512
  7.2 0.9 %copy-start = (f32[416,128]{1,0:T(8,128)S(1)}, f32[416,128]{1,0:T(8,128)}, u32[]{:S(2)}) copy-start(f32[416,128]{1,0:T(8,128)} %get-tuple-element.41.ref) | copy-start | bytes 638980
  9.2 0.8 %copy-start.1 = (f32[5,2,8,8]{3,2,1,0:T(8,128)S(1)}, f32[5,2,8,8]{3,2,1,0:T(8,128)}, u32[]{:S(2)}) copy-start(f32[5,2,8,8]{3,2,1,0:T(8,128)} %mix_ref.3) | copy-start | bytes 7684
  10.0 0.7 %copy-start.4 = (f32[5,2,17]{2,1,0:T(2,128)S(1)}, f32[5,2,17]{2,1,0:T(2,128)}, u32[]{:S(2)}) copy-start(f32[5,2,17]{2,1,0:T(2,128)} %across_ref.1) | copy-start | bytes 2044
  10.7 0.7 %copy-start.5 = (f32[5,2,17]{2,1,0:T(2,128)S(1)}, f32[5,2,17]{2,1,0:T(2,128)}, u32[]{:S(2)}) copy-start(f32[5,2,17]{2,1,0:T(2,128)} %along_ref.1) | copy-start | bytes 2044
  17.5 4.3 %copy-start.2 = (f32[5,2,8,8]{3,2,1,0:T(8,128)S(1)}, f32[5,2,8,8]{3,2,1,0:T(8,128)}, u32[]{:S(2)}) copy-start(f32[5,2,8,8]{3,2,1,0:T(8,128)} %mix_ref.3) | copy-start | bytes 7684
  20.8 9.3 %collective-permute-start.3 = (f32[384,128]{1,0:T(8,128)S(1)}, f32[384,128]{1,0:T(8,128)S(1)}, u32[]{:S(2)}, u32[]{:S(2)}) collective-permute-start(f32[384,128]{1,0:T(8,128)S(1)} %get-tuple-element.54), channel_id=1, source_target_pairs={{0,1},{1,0},{2,3},{3,2},{4,5},{5,4},{6,7},{7,6},{8,9},{9,8},{10,11... | collective-permute-start | bytes 589832 | tf_op jit(solution)/shard_map/ppermute | solution.py:554
  20.9 9.1 %collective-permute-start.4 = (f32[384,128]{1,0:T(8,128)S(1)}, f32[384,128]{1,0:T(8,128)S(1)}, u32[]{:S(2)}, u32[]{:S(2)}) collective-permute-start(f32[384,128]{1,0:T(8,128)S(1)} %get-tuple-element.55), channel_id=1, source_target_pairs={{1,2},{2,1},{3,4},{4,3},{5,6},{6,5},{7,8},{8,7},{9,10},{10,9},{11,... | collective-permute-start | bytes 589832 | tf_op jit(solution)/shard_map/ppermute | solution.py:555
  30.1 10.0 %copy-start.3 = (f32[8,256]{1,0:T(8,128)S(1)}, f32[8,256]{1,0:T(8,128)}, u32[]{:S(2)}) copy-start(f32[8,256]{1,0:T(8,128)} %get-tuple-element.69.slot_ref) | copy-start | bytes 24580
  35.5 5.0 %collective-permute-start.5 = (f32[8,128]{1,0:T(8,128)S(1)}, f32[8,128]{1,0:T(8,128)S(1)}, u32[]{:S(2)}, u32[]{:S(2)}) collective-permute-start(f32[8,128]{1,0:T(8,128)S(1)} %get-tuple-element.71), channel_id=1, source_target_pairs={{0,1},{1,0},{2,3},{3,2},{4,5},{5,4},{6,7},{7,6},{8,9},{9,8},{10,11... | collective-permute-start | bytes 12296 | tf_op jit(solution)/shard_map/ppermute | solution.py:579
  38.6 3.6 %collective-permute-start.6 = (f32[8,128]{1,0:T(8,128)S(1)}, f32[8,128]{1,0:T(8,128)S(1)}, u32[]{:S(2)}, u32[]{:S(2)}) collective-permute-start(f32[8,128]{1,0:T(8,128)S(1)} %get-tuple-element.72), channel_id=1, source_target_pairs={{0,2},{1,3},{2,0},{3,1},{4,6},{5,7},{6,4},{7,5},{8,10},{9,11},{10,... | collective-permute-start | bytes 12296 | tf_op jit(solution)/shard_map/ppermute | solution.py:579
  40.1 3.0 %collective-permute-start.7 = (f32[8,128]{1,0:T(8,128)S(1)}, f32[8,128]{1,0:T(8,128)S(1)}, u32[]{:S(2)}, u32[]{:S(2)}) collective-permute-start(f32[8,128]{1,0:T(8,128)S(1)} %get-tuple-element.73), channel_id=1, source_target_pairs={{0,3},{1,2},{2,1},{3,0},{4,7},{5,6},{6,5},{7,4},{8,11},{9,10},{10,... | collective-permute-start | bytes 12296 | tf_op jit(solution)/shard_map/ppermute | solution.py:579

commit v9 on v8

--- a/solution.py
+++ b/solution.py
@@ -374,8 +374,8 @@
         else:
             rims = jnp.where(lanes < CX // 2, from_right, from_left)
         high, low = split(rims)
-        mixed = dot(high, blend_high[level]) + dot(low, blend_high[level])
-        mixed = mixed + dot(high, blend_low[level])
+        heavy = jnp.concatenate([blend_high[level], blend_high[level]], axis=0)
+        mixed = dot(jnp.concatenate([high, low], axis=1), heavy) + dot(high, blend_low[level])
         if size < step:
             mixed = jnp.concatenate([mixed, jnp.zeros((step - size, 2 * CX), F32)], axis=0)
         high, low = split(mixed)

time: 44.3 us -> 44.2 us (level)
  no operation moved by 1% of the time
where the time goes in v9:
time: 44.2 us; the launch traced here: 43.9 us
  Pallas kernels  26.9 us (61%)
  starting transfers between devices  8.72 us (20%)
  waiting for transfers between devices  3.76 us (9%)
  local copies, waits for them, and re-layouts  3.09 us (7%)
  between operations  1.41 us (3%)
    pallas_call x1, Pallas kernels, body(): call(inner_kernel, [SMEM] + [VMEM] * 8, [shape(ALL_ROWS, HALF)], [pltpu.V...  8.23 us
    pallas_call x1, Pallas kernels, body(): call(outer_kernel, [VMEM] * (8 + 2 * PEERS), [shape(PLANES, NY, CX)] + [s...  5.38 us
    ppermute x3, starting transfers between devices, body(): lax.ppermute(samples[k], 'sect', swaps[k])  4.52 us
    pallas_call x1, Pallas kernels, body(): call(charge_kernel, [VMEM] * 3, kept + [shape(PLANES, size, CX) for size...  3.25 us
    ppermute x3, starting transfers between devices, body(): lax.ppermute(sends[k], 'sect', swaps[k])  3.18 us
    pallas_call x3, Pallas kernels, body(): call(brick_kernel, [VMEM] * (1 + len(total)), kept + [shape(TILES, HALF)]...  3.12 us
    unnamed x12, local copies, waits for them, and re-layouts  3.09 us
    pallas_call x1, Pallas kernels, body(): call(prep_kernel, [VMEM, VMEM, VMEM], [shape(LEVELS + 1, 2 * CX, 2 * CX,...  2.86 us
  transfers between devices with their start and end apart: 8, of which 3 were waited for; matrix products, arithmetic and copies ran while one was open for 0% of the time, Pallas kernels for 33%

profile of v9, /device:TPU:0, one launch (start us, length us, event | category | flops | bytes accessed | tf_op | source)
XLA Modules:
  0.0 43.9 jit_solution(10774195895549290926)
XLA Ops:
  1.3 2.7 %shard_map.104 = (f32[416,128]{1,0:T(8,128)}, f32[416,128]{1,0:T(8,128)}, f32[416,128]{1,0:T(8,128)}, f32[416,128]{1,0:T(8,128)}, f32[8,256]{1,0:T(8,128)}) custom-call(s32[1]{0:T(128)S(6)} %copy.11.count_ref, f32[1,1024]{1,0:T(1,128)} %bitcast.4, f32[8,1024]{1,0:T(8,128)} %planes_hbm.1, f32[1024,128]{1,0:T(8,128)} %cells_hbm.1, s32[1,256]{1,0:T(1,128)} %bitcast.6, ...), custom_call_target="tpu_custom_call" | custom-call | tf_op jit(solution)/shard_map/pallas_call | solution.py:489
  4.0 0.5 %collective-permute-start.2 = (f32[416,128]{1,0:T(8,128)}, f32[416,128]{1,0:T(8,128)S(1)}, u32[]{:S(2)}, u32[]{:S(2)}) collective-permute-start(f32[416,128]{1,0:T(8,128)} %get-tuple-element.40), channel_id=1, source_target_pairs={{0,1},{1,0},{2,3},{3,2},{4,5},{5,4},{6,7},{7,6},{8,9},{9,8},{10,11... | collective-permute-start | bytes 638984 | tf_op jit(solution)/shard_map/ppermute | solution.py:512
  4.5 2.6 %collective-permute-start.1 = (f32[416,128]{1,0:T(8,128)}, f32[416,128]{1,0:T(8,128)S(1)}, u32[]{:S(2)}, u32[]{:S(2)}) collective-permute-start(f32[416,128]{1,0:T(8,128)} %get-tuple-element.39), channel_id=1, source_target_pairs={{0,2},{1,3},{2,0},{3,1},{4,6},{5,7},{6,4},{7,5},{8,10},{9,11},{10,... | collective-permute-start | bytes 638984 | tf_op jit(solution)/shard_map/ppermute | solution.py:512
  7.1 0.1 collective-permute-start
  7.2 0.0 copy-start
  7.2 0.9 %copy-done = f32[416,128]{1,0:T(8,128)S(1)} copy-done((f32[416,128]{1,0:T(8,128)S(1)}, f32[416,128]{1,0:T(8,128)}, u32[]{:S(2)}) %copy-start) | copy-done | bytes 213016
  8.1 1.0 %shard_map.105 = (bf16[96,384]{1,0:T(8,128)(2,1)S(1)}, f32[32,96,128]{2,1,0:T(8,128)S(1)}, f32[384,1024]{1,0:T(8,128)S(1)}) custom-call(f32[416,128]{1,0:T(8,128)S(1)} %copy-done), custom_call_target="tpu_custom_call" | custom-call | tf_op jit(solution)/shard_map/pallas_call | solution.py:533
  9.2 0.0 copy-start.1
  9.2 0.8 %copy-done.1 = f32[5,2,8,8]{3,2,1,0:T(8,128)S(1)} copy-done((f32[5,2,8,8]{3,2,1,0:T(8,128)S(1)}, f32[5,2,8,8]{3,2,1,0:T(8,128)}, u32[]{:S(2)}) %copy-start.1) | copy-done | bytes 2584
  10.0 0.0 copy-start.4
  10.0 0.7 %copy-done.4 = f32[5,2,17]{2,1,0:T(2,128)S(1)} copy-done((f32[5,2,17]{2,1,0:T(2,128)S(1)}, f32[5,2,17]{2,1,0:T(2,128)}, u32[]{:S(2)}) %copy-start.4) | copy-done | bytes 704
  10.7 0.0 copy-start.5
  10.7 0.7 %copy-done.5 = f32[5,2,17]{2,1,0:T(2,128)S(1)} copy-done((f32[5,2,17]{2,1,0:T(2,128)S(1)}, f32[5,2,17]{2,1,0:T(2,128)}, u32[]{:S(2)}) %copy-start.5) | copy-done | bytes 704
  11.3 2.9 %shard_map.108 = (bf16[5,256,256]{2,1,0:T(8,128)(2,1)S(1)}, bf16[5,128,256]{2,1,0:T(8,128)(2,1)S(1)}, bf16[1504,768]{1,0:T(8,128)(2,1)S(1)}, bf16[5,128,256]{2,1...) custom-call(f32[5,2,17]{2,1,0:T(2,128)S(1)} %copy-done.4, ...), custom_call_target="tpu_custom_call" | custom-call | tf_op jit(solution)/shard_map/pallas_call | solution.py:513
  14.2 0.0 collective-permute-done.2.ref
  14.2 1.0 %shard_map.106 = (bf16[96,384]{1,0:T(8,128)(2,1)S(1)}, f32[32,96,128]{2,1,0:T(8,128)S(1)}, f32[384,1024]{1,0:T(8,128)S(1)}) custom-call(f32[416,128]{1,0:T(8,128)S(1)} %collective-permute-done.2.ref, f32[384,1024]{1,0:T(8,128)S(1)} %get-tuple-element.42.refs_0_), custom_call_target="tpu_custom_call" | custom-call | tf_op jit(solution)/shard_map/pallas_call | solution.py:533
  15.3 0.0 collective-permute-done.1.ref
  15.3 1.0 %shard_map.107 = (bf16[96,384]{1,0:T(8,128)(2,1)S(1)}, f32[32,96,128]{2,1,0:T(8,128)S(1)}, f32[384,1024]{1,0:T(8,128)S(1)}) custom-call(f32[416,128]{1,0:T(8,128)S(1)} %collective-permute-done.1.ref, f32[384,1024]{1,0:T(8,128)S(1)} %get-tuple-element.43.refs_0_), custom_call_target="tpu_custom_call" | custom-call | tf_op jit(solution)/shard_map/pallas_call | solution.py:533
  16.3 1.2 %collective-permute-done.ref = f32[416,128]{1,0:T(8,128)S(1)} collective-permute-done((f32[416,128]{1,0:T(8,128)}, f32[416,128]{1,0:T(8,128)S(1)}, u32[]{:S(2)}, u32[]{:S(2)}) %collective-permute-start) | collective-permute-done | bytes 213024 | tf_op jit(solution)/shard_map/ppermute | solution.py:512
  17.5 0.0 copy-start.2
  17.5 3.3 %shard_map.109 = (bf16[96,384]{1,0:T(8,128)(2,1)S(1)}, f32[32,96,128]{2,1,0:T(8,128)S(1)}, f32[8,384,128]{2,1,0:T(8,128)S(1)}, f32[8,192,128]{2,1,0:T(8,128)S(1)...) custom-call(f32[416,128]{1,0:T(8,128)S(1)} %collective-permute-done., ...), custom_call_target="tpu_custom_call" | custom-call | tf_op jit(solution)/shard_map/pallas_call | solution.py:542
  20.8 0.2 collective-permute-start.3
  20.9 0.8 %collective-permute-start.4 = (f32[384,128]{1,0:T(8,128)S(1)}, f32[384,128]{1,0:T(8,128)S(1)}, u32[]{:S(2)}, u32[]{:S(2)}) collective-permute-start(f32[384,128]{1,0:T(8,128)S(1)} %get-tuple-element.55), channel_id=1, source_target_pairs={{1,2},{2,1},{3,4},{4,3},{5,6},{6,5},{7,8},{8,7},{9,10},{10,9},{11,... | collective-permute-start | bytes 589832 | tf_op jit(solution)/shard_map/ppermute | solution.py:555
  21.8 0.0 copy-done.2
  21.8 8.2 %shard_map.110.refs_0_ = f32[752,1024]{1,0:T(8,128)S(1)} custom-call(f32[5,2,8,8]{3,2,1,0:T(8,128)S(1)} %copy-done.2, f32[8,384,128]{2,1,0:T(8,128)S(1)} %get-tuple-element.46.q0, f32[8,192,128]{2,1,0:T(8,128)S(1)} %get-tuple-element.47.s1, f32[8,96,128]{2,1,0:T(8,128)S(1)} %get-tuple-element.48.s2, f32[8,48,128]{2,1,0:T(8,128)S(1)} %get-tuple-element.49.s3, ...), custom_call_target="tpu_custom_call" | custom-call | tf_op jit(solution)/shard_map/pallas_call | solution.py:556
  30.0 0.0 collective-permute-done.3.refs_1_
  30.0 0.0 collective-permute-done.4.refs_2_
  30.1 0.0 copy-start.3
  30.1 5.4 %shard_map.111 = (f32[8,384,128]{2,1,0:T(8,128)}, f32[8,128]{1,0:T(8,128)S(1)}, f32[8,128]{1,0:T(8,128)S(1)}, f32[8,128]{1,0:T(8,128)S(1)}, f32[8,128]{1,0:T(8,128)S(1)}) custom-call(f32[752,1024]{1,0:T(8,128)S(1)} %shard_map.110.refs_0_, f32[384,128]{1,0:T(8,128)S(1)} %collective-permute-done.3.refs_1_, f32[384,128]{1,0:T(8,128)S(1)} %collective-permute-done.4.refs_2_, ...), custom_call_target="tpu_custom_call" | custom-call | tf_op jit(solution)/shard_map/pallas_call | solution.py:567
  35.4 3.1 %collective-permute-start.5 = (f32[8,128]{1,0:T(8,128)S(1)}, f32[8,128]{1,0:T(8,128)S(1)}, u32[]{:S(2)}, u32[]{:S(2)}) collective-permute-start(f32[8,128]{1,0:T(8,128)S(1)} %get-tuple-element.71), channel_id=1, source_target_pairs={{0,1},{1,0},{2,3},{3,2},{4,5},{5,4},{6,7},{7,6},{8,9},{9,8},{10,11... | collective-permute-start | bytes 12296 | tf_op jit(solution)/shard_map/ppermute | solution.py:579
  38.5 1.4 %collective-permute-start.6 = (f32[8,128]{1,0:T(8,128)S(1)}, f32[8,128]{1,0:T(8,128)S(1)}, u32[]{:S(2)}, u32[]{:S(2)}) collective-permute-start(f32[8,128]{1,0:T(8,128)S(1)} %get-tuple-element.72), channel_id=1, source_target_pairs={{0,2},{1,3},{2,0},{3,1},{4,6},{5,7},{6,4},{7,5},{8,10},{9,11},{10,... | collective-permute-start | bytes 12296 | tf_op jit(solution)/shard_map/ppermute | solution.py:579
  40.0 0.0 collective-permute-start.7
  40.0 0.0 copy-done.3
  40.0 0.4 shard_map.112.match_ref
  40.4 0.0 collective-permute-done.5.b1
  40.4 1.7 %collective-permute-done.6.b2 = f32[8,128]{1,0:T(8,128)S(1)} collective-permute-done((f32[8,128]{1,0:T(8,128)S(1)}, f32[8,128]{1,0:T(8,128)S(1)}, u32[]{:S(2)}, u32[]{:S(2)}) %collective-permute-start.6) | collective-permute-done | bytes 4128 | tf_op jit(solution)/shard_map/ppermute | solution.py:579
  42.1 0.9 %collective-permute-done.7.b3 = f32[8,128]{1,0:T(8,128)S(1)} collective-permute-done((f32[8,128]{1,0:T(8,128)S(1)}, f32[8,128]{1,0:T(8,128)S(1)}, u32[]{:S(2)}, u32[]{:S(2)}) %collective-permute-start.7) | collective-permute-done | bytes 4128 | tf_op jit(solution)/shard_map/ppermute | solution.py:579
  43.0 0.9 %shard_map.113 = f32[1,1024]{1,0:T(1,128)} custom-call(s32[1]{0:T(128)S(6)} %copy.11.count_ref, bf16[512,1024]{1,0:T(8,128)(2,1)S(1)} %shard_map.112.match_ref, f32[8,128]{1,0:T(8,128)S(1)} %get-tuple-element.70.b0, f32[8,128]{1,0:T(8,128)S(1)} %collective-permute-done.5.b1, f32[8,128]{1,0:T(8,128)S(1)} %collective-permute-done.6.b2, ...), custom_call_target="tpu_custom_call" | custom-call | tf_op jit(solution)/shard_map/pallas_call | solution.py:581
Async XLA Ops:
  4.0 10.2 %collective-permute-start.2 = (f32[416,128]{1,0:T(8,128)}, f32[416,128]{1,0:T(8,128)S(1)}, u32[]{:S(2)}, u32[]{:S(2)}) collective-permute-start(f32[416,128]{1,0:T(8,128)} %get-tuple-element.40), channel_id=1, source_target_pairs={{0,1},{1,0},{2,3},{3,2},{4,5},{5,4},{6,7},{7,6},{8,9},{9,8},{10,11... | collective-permute-start | bytes 638984 | tf_op jit(solution)/shard_map/ppermute | solution.py:512
  4.5 10.7 %collective-permute-start.1 = (f32[416,128]{1,0:T(8,128)}, f32[416,128]{1,0:T(8,128)S(1)}, u32[]{:S(2)}, u32[]{:S(2)}) collective-permute-start(f32[416,128]{1,0:T(8,128)} %get-tuple-element.39), channel_id=1, source_target_pairs={{0,2},{1,3},{2,0},{3,1},{4,6},{5,7},{6,4},{7,5},{8,10},{9,11},{10,... | collective-permute-start | bytes 638984 | tf_op jit(solution)/shard_map/ppermute | solution.py:512
  7.1 10.4 %collective-permute-start = (f32[416,128]{1,0:T(8,128)}, f32[416,128]{1,0:T(8,128)S(1)}, u32[]{:S(2)}, u32[]{:S(2)}) collective-permute-start(f32[416,128]{1,0:T(8,128)} %get-tuple-element.38), channel_id=1, source_target_pairs={{0,3},{1,2},{2,1},{3,0},{4,7},{5,6},{6,5},{7,4},{8,11},{9,10},{10,... | collective-permute-start | bytes 638984 | tf_op jit(solution)/shard_map/ppermute | solution.py:512
  7.2 0.9 %copy-start = (f32[416,128]{1,0:T(8,128)S(1)}, f32[416,128]{1,0:T(8,128)}, u32[]{:S(2)}) copy-start(f32[416,128]{1,0:T(8,128)} %get-tuple-element.41.ref) | copy-start | bytes 638980
  9.2 0.8 %copy-start.1 = (f32[5,2,8,8]{3,2,1,0:T(8,128)S(1)}, f32[5,2,8,8]{3,2,1,0:T(8,128)}, u32[]{:S(2)}) copy-start(f32[5,2,8,8]{3,2,1,0:T(8,128)} %mix_ref.3) | copy-start | bytes 7684
  10.0 0.7 %copy-start.4 = (f32[5,2,17]{2,1,0:T(2,128)S(1)}, f32[5,2,17]{2,1,0:T(2,128)}, u32[]{:S(2)}) copy-start(f32[5,2,17]{2,1,0:T(2,128)} %across_ref.1) | copy-start | bytes 2044
  10.7 0.7 %copy-start.5 = (f32[5,2,17]{2,1,0:T(2,128)S(1)}, f32[5,2,17]{2,1,0:T(2,128)}, u32[]{:S(2)}) copy-start(f32[5,2,17]{2,1,0:T(2,128)} %along_ref.1) | copy-start | bytes 2044
  17.5 4.3 %copy-start.2 = (f32[5,2,8,8]{3,2,1,0:T(8,128)S(1)}, f32[5,2,8,8]{3,2,1,0:T(8,128)}, u32[]{:S(2)}) copy-start(f32[5,2,8,8]{3,2,1,0:T(8,128)} %mix_ref.3) | copy-start | bytes 7684
  20.8 9.3 %collective-permute-start.3 = (f32[384,128]{1,0:T(8,128)S(1)}, f32[384,128]{1,0:T(8,128)S(1)}, u32[]{:S(2)}, u32[]{:S(2)}) collective-permute-start(f32[384,128]{1,0:T(8,128)S(1)} %get-tuple-element.54), channel_id=1, source_target_pairs={{0,1},{1,0},{2,3},{3,2},{4,5},{5,4},{6,7},{7,6},{8,9},{9,8},{10,11... | collective-permute-start | bytes 589832 | tf_op jit(solution)/shard_map/ppermute | solution.py:554
  20.9 9.1 %collective-permute-start.4 = (f32[384,128]{1,0:T(8,128)S(1)}, f32[384,128]{1,0:T(8,128)S(1)}, u32[]{:S(2)}, u32[]{:S(2)}) collective-permute-start(f32[384,128]{1,0:T(8,128)S(1)} %get-tuple-element.55), channel_id=1, source_target_pairs={{1,2},{2,1},{3,4},{4,3},{5,6},{6,5},{7,8},{8,7},{9,10},{10,9},{11,... | collective-permute-start | bytes 589832 | tf_op jit(solution)/shard_map/ppermute | solution.py:555
  30.1 9.9 %copy-start.3 = (f32[8,256]{1,0:T(8,128)S(1)}, f32[8,256]{1,0:T(8,128)}, u32[]{:S(2)}) copy-start(f32[8,256]{1,0:T(8,128)} %get-tuple-element.69.slot_ref) | copy-start | bytes 24580
  35.4 5.0 %collective-permute-start.5 = (f32[8,128]{1,0:T(8,128)S(1)}, f32[8,128]{1,0:T(8,128)S(1)}, u32[]{:S(2)}, u32[]{:S(2)}) collective-permute-start(f32[8,128]{1,0:T(8,128)S(1)} %get-tuple-element.71), channel_id=1, source_target_pairs={{0,1},{1,0},{2,3},{3,2},{4,5},{5,4},{6,7},{7,6},{8,9},{9,8},{10,11... | collective-permute-start | bytes 12296 | tf_op jit(solution)/shard_map/ppermute | solution.py:579
  38.5 3.6 %collective-permute-start.6 = (f32[8,128]{1,0:T(8,128)S(1)}, f32[8,128]{1,0:T(8,128)S(1)}, u32[]{:S(2)}, u32[]{:S(2)}) collective-permute-start(f32[8,128]{1,0:T(8,128)S(1)} %get-tuple-element.72), channel_id=1, source_target_pairs={{0,2},{1,3},{2,0},{3,1},{4,6},{5,7},{6,4},{7,5},{8,10},{9,11},{10,... | collective-permute-start | bytes 12296 | tf_op jit(solution)/shard_map/ppermute | solution.py:579
  40.0 3.0 %collective-permute-start.7 = (f32[8,128]{1,0:T(8,128)S(1)}, f32[8,128]{1,0:T(8,128)S(1)}, u32[]{:S(2)}, u32[]{:S(2)}) collective-permute-start(f32[8,128]{1,0:T(8,128)S(1)} %get-tuple-element.73), channel_id=1, source_target_pairs={{0,3},{1,2},{2,1},{3,0},{4,7},{5,6},{6,5},{7,4},{8,11},{9,10},{10,... | collective-permute-start | bytes 12296 | tf_op jit(solution)/shard_map/ppermute | solution.py:579
